TPU v7x, 32 devices: a whole 2x2x4 slice. The times are simulated.
32 devices in a mesh: fsdp: 4 (over z), tensor: 8 (over y, x, core).
Axes of the slice: x: 2, y: 2, z: 4, core: 2. Of those that a mesh axis runs over, the one named last changes fastest.
Arguments:
- tokens: bfloat16 [5120, 2048], P(('fsdp', 'tensor')), may hold values from -6 to 6
- gain_attn: bfloat16 [2048], replicated, may hold values from 0.099609375 to 1.8984375
- gain_mlp: bfloat16 [2048], replicated, may hold values from 0.099609375 to 1.8984375
- w_query: bfloat16 [2048, 2048], P('fsdp', 'tensor'), may hold values from -0.125 to 0.125
- w_key: bfloat16 [2048, 2048], P('fsdp', 'tensor'), may hold values from -0.125 to 0.125
- w_value: bfloat16 [2048, 2048], P('fsdp', 'tensor'), may hold values from -0.125 to 0.125
- w_out: bfloat16 [2048, 2048], P('tensor', 'fsdp'), may hold values from -0.5 to 0.5
- w_gate: bfloat16 [2048, 8192], P('fsdp', 'tensor'), may hold values from -0.125 to 0.125
- w_up: bfloat16 [2048, 8192], P('fsdp', 'tensor'), may hold values from -0.125 to 0.125
- w_down: bfloat16 [8192, 2048], P('tensor', 'fsdp'), may hold values from -0.09375 to 0.09375
- segment_ids: int32 [4, 1280], P('fsdp'), may hold values from 0 to 3, never falling along the last dimension, each value on 1 to 512 neighbouring positions
- out_grad: bfloat16 [5120, 2048], P(('fsdp', 'tensor')), may hold values from -6 to 6
Outputs:
- output: bfloat16 [5120, 2048], P(('fsdp', 'tensor'))
- tokens_grad: bfloat16 [5120, 2048], P(('fsdp', 'tensor'))
- gain_attn_grad: float32 [2048], replicated
- gain_mlp_grad: float32 [2048], replicated
- w_query_grad: float32 [2048, 2048], P('fsdp', 'tensor')
- w_key_grad: float32 [2048, 2048], P('fsdp', 'tensor')
- w_value_grad: float32 [2048, 2048], P('fsdp', 'tensor')
- w_out_grad: float32 [2048, 2048], P('tensor', 'fsdp')
- w_gate_grad: float32 [2048, 8192], P('fsdp', 'tensor')
- w_up_grad: float32 [2048, 8192], P('fsdp', 'tensor')
- w_down_grad: float32 [8192, 2048], P('tensor', 'fsdp')
Inputs may be any that keep to these rules, and one draw needn't show every extreme that they name: `segment_ids`: in each packed row the ids never fall; each sample has 1 to 512 tokens, and some sample in each row has exactly 512.
All inputs are finite; a program needn't handle non-finite values.
Results may differ from a plain program's by a relative error of at most 0.019.
Values may be sent and summed in bfloat16 or wider, within the bound.
A program may use at most 192 MiB of HBM per device.

v0:
```python
import math

import jax
import jax.numpy as jnp
from jax import lax
from jax.sharding import PartitionSpec as P

HEAD = 64


eps = 1e-05
rope_base = 130000.0


def dot_nt(left, right):
    return lax.dot_general(
        left, right, (((1,), (1,)), ((), ())), preferred_element_type=jnp.float32
    )


def dot_tn(left, right):
    return lax.dot_general(
        left, right, (((0,), (0,)), ((), ())), preferred_element_type=jnp.float32
    )


def rope_tables(segments):
    length = segments.shape[1]
    index = jnp.arange(length, dtype=jnp.int32)[None, :]
    change = jnp.concatenate(
        [jnp.ones((segments.shape[0], 1), dtype=bool), segments[:, 1:] != segments[:, :-1]], axis=1
    )
    start = lax.cummax(jnp.where(change, index, 0), axis=1)
    position = (index - start).astype(jnp.float32)
    half = jnp.arange(HEAD // 2, dtype=jnp.float32)
    inverse = jnp.exp(half * (-2.0 / HEAD) * math.log(rope_base))
    angle = position[:, :, None, None] * inverse[None, None, None, :]
    return (jnp.cos(angle), jnp.sin(angle))


def rotate(value, cosine, sine):
    half = value.shape[-1] // 2
    first = value[..., :half]
    second = value[..., half:]
    return jnp.concatenate(
        [first * cosine - second * sine, second * cosine + first * sine], axis=-1
    )


def norm_forward(value, gain):
    scale = lax.rsqrt(jnp.mean(value * value, axis=-1, keepdims=True) + eps)
    return (value * scale * gain, scale)


def norm_backward(value, scale, gain, grad):
    scaled_grad = grad * gain
    inner = jnp.mean(value * scaled_grad, axis=-1, keepdims=True)
    back = scale * scaled_grad - value * scale * scale * scale * inner
    gain_grad = jnp.sum(grad * value * scale, axis=0)
    return (back, gain_grad)


def row_mask(segments):
    length = segments.shape[0]
    index = jnp.arange(length, dtype=jnp.int32)
    return (segments[:, None] == segments[None, :]) & (index[None, :] <= index[:, None])


def row_scores(query, key, segments):
    scores = jnp.einsum("qhd,khd->hqk", query, key, preferred_element_type=jnp.float32) * HEAD ** (
        -0.5
    )
    return jnp.where(row_mask(segments)[None, :, :], scores, -1000000000.0)


def attend_row(inputs):
    query, key, value, segments = inputs
    scores = row_scores(query, key, segments)
    top = jnp.max(scores, axis=-1, keepdims=True)
    expo = jnp.exp(scores - top)
    total = jnp.sum(expo, axis=-1, keepdims=True)
    weights = (expo / total).astype(jnp.bfloat16)
    attended = jnp.einsum("hqk,khd->qhd", weights, value, preferred_element_type=jnp.float32)
    return (attended, (top + jnp.log(total))[..., 0])


def attend_back(inputs):
    query, key, value, segments, logsum, grad_out = inputs
    scores = row_scores(query, key, segments)
    weights = jnp.exp(scores - logsum[..., None])
    grad_value = jnp.einsum(
        "hqk,qhd->khd", weights.astype(jnp.bfloat16), grad_out, preferred_element_type=jnp.float32
    )
    grad_weights = jnp.einsum("qhd,khd->hqk", grad_out, value, preferred_element_type=jnp.float32)
    inner = jnp.sum(weights * grad_weights, axis=-1, keepdims=True)
    grad_scores = (weights * (grad_weights - inner)).astype(jnp.bfloat16)
    grad_query = jnp.einsum(
        "hqk,khd->qhd", grad_scores, key, preferred_element_type=jnp.float32
    ) * HEAD ** (-0.5)
    grad_key = jnp.einsum(
        "hqk,qhd->khd", grad_scores, query, preferred_element_type=jnp.float32
    ) * HEAD ** (-0.5)
    return (grad_query, grad_key, grad_value)


def shards(
    tokens,
    gain_attn,
    gain_mlp,
    w_query,
    w_key,
    w_value,
    w_out,
    w_gate,
    w_up,
    w_down,
    segment_ids,
    out_grad,
):
    rows_grp = segment_ids.shape[0]
    row_len = segment_ids.shape[1]
    local = (w_query, w_key, w_value, w_out, w_gate, w_up, w_down)
    gathered = (
        lax.all_gather(local[0], "fsdp", axis=0, tiled=True),
        lax.all_gather(local[1], "fsdp", axis=0, tiled=True),
        lax.all_gather(local[2], "fsdp", axis=0, tiled=True),
        lax.all_gather(local[3], "fsdp", axis=1, tiled=True),
        lax.all_gather(local[4], "fsdp", axis=0, tiled=True),
        lax.all_gather(local[5], "fsdp", axis=0, tiled=True),
        lax.all_gather(local[6], "fsdp", axis=1, tiled=True),
    )
    wq, wk, wv, wo, wg, wu, wd = gathered
    heads_dev = wq.shape[1] // HEAD
    group = rows_grp * row_len
    gain_a = gain_attn.astype(jnp.float32)
    gain_m = gain_mlp.astype(jnp.float32)
    cosine, sine = rope_tables(segment_ids)

    def heads(value):
        return value.reshape(rows_grp, row_len, heads_dev, HEAD)

    x = tokens.astype(jnp.float32)
    normed_local, scale_a = norm_forward(x, gain_a)
    normed_a = lax.all_gather(normed_local.astype(jnp.bfloat16), "tensor", axis=0, tiled=True)
    query = rotate(
        heads(jnp.dot(normed_a, wq, preferred_element_type=jnp.float32)), cosine, sine
    ).astype(jnp.bfloat16)
    key = rotate(
        heads(jnp.dot(normed_a, wk, preferred_element_type=jnp.float32)), cosine, sine
    ).astype(jnp.bfloat16)
    value = heads(jnp.dot(normed_a, wv, preferred_element_type=jnp.float32).astype(jnp.bfloat16))
    attended, logsum = lax.map(attend_row, (query, key, value, segment_ids))
    attended = attended.reshape(group, heads_dev * HEAD).astype(jnp.bfloat16)
    hidden = x + lax.psum_scatter(
        jnp.dot(attended, wo, preferred_element_type=jnp.float32),
        "tensor",
        scatter_dimension=0,
        tiled=True,
    )
    normed_hidden, scale_m = norm_forward(hidden, gain_m)
    normed_m = lax.all_gather(normed_hidden.astype(jnp.bfloat16), "tensor", axis=0, tiled=True)
    gate = jnp.dot(normed_m, wg, preferred_element_type=jnp.float32)
    up = jnp.dot(normed_m, wu, preferred_element_type=jnp.float32)
    sigma = jax.nn.sigmoid(gate)
    silu_gate = gate * sigma
    act = (silu_gate * up).astype(jnp.bfloat16)
    output = hidden + lax.psum_scatter(
        jnp.dot(act, wd, preferred_element_type=jnp.float32).astype(jnp.bfloat16),
        "tensor",
        scatter_dimension=0,
        tiled=True,
    ).astype(jnp.float32)
    wq, wk, wv, wo, wg, wu, wd = (
        lax.all_gather(local[0], "fsdp", axis=0, tiled=True),
        lax.all_gather(local[1], "fsdp", axis=0, tiled=True),
        lax.all_gather(local[2], "fsdp", axis=0, tiled=True),
        lax.all_gather(local[3], "fsdp", axis=1, tiled=True),
        lax.all_gather(local[4], "fsdp", axis=0, tiled=True),
        lax.all_gather(local[5], "fsdp", axis=0, tiled=True),
        lax.all_gather(local[6], "fsdp", axis=1, tiled=True),
    )
    grad_all = lax.all_gather(out_grad, "tensor", axis=0, tiled=True)
    grad_down = dot_tn(act, grad_all)
    grad_act = dot_nt(grad_all, wd)
    grad_gate = (grad_act * up * (sigma * (1.0 + gate * (1.0 - sigma)))).astype(jnp.bfloat16)
    grad_up = (grad_act * silu_gate).astype(jnp.bfloat16)
    grad_wgate = dot_tn(normed_m, grad_gate)
    grad_wup = dot_tn(normed_m, grad_up)
    grad_nm = lax.psum_scatter(
        dot_nt(grad_gate, wg) + dot_nt(grad_up, wu), "tensor", scatter_dimension=0, tiled=True
    )
    back_m, gain_m_part = norm_backward(hidden, scale_m, gain_m, grad_nm)
    grad_hidden = out_grad.astype(jnp.float32) + back_m
    grad_hidden_low = grad_hidden.astype(jnp.bfloat16)
    branch_all = lax.all_gather(grad_hidden_low, "tensor", axis=0, tiled=True)
    grad_wout = dot_tn(attended, branch_all)
    grad_attended = heads(dot_nt(branch_all, wo).astype(jnp.bfloat16))
    grad_query, grad_key, grad_value = lax.map(
        attend_back, (query, key, value, segment_ids, logsum, grad_attended)
    )
    grad_qpre = (
        rotate(grad_query, cosine, -sine).reshape(group, heads_dev * HEAD).astype(jnp.bfloat16)
    )
    grad_kpre = (
        rotate(grad_key, cosine, -sine).reshape(group, heads_dev * HEAD).astype(jnp.bfloat16)
    )
    grad_vpre = grad_value.reshape(group, heads_dev * HEAD).astype(jnp.bfloat16)
    grad_wq = dot_tn(normed_a, grad_qpre)
    grad_wk = dot_tn(normed_a, grad_kpre)
    grad_wv = dot_tn(normed_a, grad_vpre)
    grad_na_part = dot_nt(grad_qpre, wq) + dot_nt(grad_kpre, wk) + dot_nt(grad_vpre, wv)
    grad_na = lax.psum_scatter(
        grad_na_part.astype(jnp.bfloat16), "tensor", scatter_dimension=0, tiled=True
    ).astype(jnp.float32)
    back_a, gain_a_part = norm_backward(x, scale_a, gain_a, grad_na)
    tokens_grad = (grad_hidden + back_a).astype(jnp.bfloat16)
    gain_a_grad, gain_m_grad = lax.psum((gain_a_part, gain_m_part), ("fsdp", "tensor"))
    weight_grads = (
        lax.psum_scatter(
            grad_wq.astype(jnp.bfloat16), "fsdp", scatter_dimension=0, tiled=True
        ).astype(jnp.float32),
        lax.psum_scatter(
            grad_wk.astype(jnp.bfloat16), "fsdp", scatter_dimension=0, tiled=True
        ).astype(jnp.float32),
        lax.psum_scatter(
            grad_wv.astype(jnp.bfloat16), "fsdp", scatter_dimension=0, tiled=True
        ).astype(jnp.float32),
        lax.psum_scatter(
            grad_wout.astype(jnp.bfloat16), "fsdp", scatter_dimension=1, tiled=True
        ).astype(jnp.float32),
        lax.psum_scatter(
            grad_wgate.astype(jnp.bfloat16), "fsdp", scatter_dimension=0, tiled=True
        ).astype(jnp.float32),
        lax.psum_scatter(
            grad_wup.astype(jnp.bfloat16), "fsdp", scatter_dimension=0, tiled=True
        ).astype(jnp.float32),
        lax.psum_scatter(
            grad_down.astype(jnp.bfloat16), "fsdp", scatter_dimension=1, tiled=True
        ).astype(jnp.float32),
    )
    return (
        output.astype(jnp.bfloat16),
        tokens_grad,
        gain_a_grad,
        gain_m_grad,
        weight_grads[0],
        weight_grads[1],
        weight_grads[2],
        weight_grads[3],
        weight_grads[4],
        weight_grads[5],
        weight_grads[6],
    )


def solution(mesh):
    return jax.shard_map(
        shards,
        mesh=mesh,
        in_specs=(
            P(("fsdp", "tensor"), None),
            P(),
            P(),
            P("fsdp", "tensor"),
            P("fsdp", "tensor"),
            P("fsdp", "tensor"),
            P("tensor", "fsdp"),
            P("fsdp", "tensor"),
            P("fsdp", "tensor"),
            P("tensor", "fsdp"),
            P("fsdp", None),
            P(("fsdp", "tensor"), None),
        ),
        out_specs=(
            P(("fsdp", "tensor"), None),
            P(("fsdp", "tensor"), None),
            P(),
            P(),
            P("fsdp", "tensor"),
            P("fsdp", "tensor"),
            P("fsdp", "tensor"),
            P("tensor", "fsdp"),
            P("fsdp", "tensor"),
            P("fsdp", "tensor"),
            P("tensor", "fsdp"),
        ),
        check_vma=False,
    )
```

profile of v0, /device:TPU:8, one launch (start us, length us, event | category | flops | bytes accessed | tf_op | source)
XLA Modules:
  0.0 1229.6 jit_solution(9686080261791631921)
XLA Ops:
  10.5 2.1 fusion.18
  17.1 1.8 fusion.7
  20.3 18.5 %all-gather.18.cloned.1.call-done = bf16[2048,256]{1,0:T(8,128)(2,1)} async-done(((bf16[512,256]{1,0:T(8,128)(2,1)}), bf16[2048,256]{1,0:T(8,128)(2,1)}) %all-gather.18.cloned.1.call-update) | async-done | bytes 1048592 | tf_op jit(solution)/shard_map/all_gather | solution.py:125
  38.7 43.1 %all-gather.12.cloned.1.call-done = bf16[1280,2048]{1,0:T(8,128)(2,1)} async-done(((bf16[160,2048]{1,0:T(8,128)(2,1)}), bf16[1280,2048]{1,0:T(8,128)(2,1)}) %all-gather.12.cloned.1.call-update) | async-done | bytes 5242896 | tf_op jit(solution)/shard_map/all_gather | solution.py:144
  81.8 4.3 fusion.41
  86.1 25.2 %all-gather.16.cloned.1.call-done = bf16[2048,256]{1,0:T(8,128)(2,1)} async-done(((bf16[512,256]{1,0:T(8,128)(2,1)}), bf16[2048,256]{1,0:T(8,128)(2,1)}) %all-gather.16.cloned.1.call-update) | async-done | bytes 1048592 | tf_op jit(solution)/shard_map/all_gather | solution.py:124
  111.3 4.3 fusion.40
  116.1 11.1 fusion.39
  127.2 10.6 fusion.1
  137.8 2.4 all-gather.14.cloned.1.call-done
  140.2 4.3 convolution_convert_fusion.9
  144.5 11.5 fusion.14
  156.0 13.0 %all-gather.20.cloned.1.call-done = bf16[256,2048]{1,0:T(8,128)(2,1)} async-done(((bf16[256,512]{1,0:T(8,128)(2,1)}), bf16[256,2048]{1,0:T(8,128)(2,1)}) %all-gather.20.cloned.1.call-update) | async-done | bytes 1048592 | tf_op jit(solution)/shard_map/all_gather | solution.py:127
  169.1 6.7 fusion.42
  176.6 80.4 %reduce-scatter.12.cloned.1.call-done = f32[160,2048]{1,0:T(8,128)} async-done(((f32[1280,2048]{1,0:T(8,128)}), f32[160,2048]{1,0:T(8,128)}) %reduce-scatter.12.cloned.1.call-update) | async-done | bytes 1310736 | tf_op jit(solution)/shard_map/reduce_scatter | solution.py:154
  257.0 1.6 multiply_reduce_fusion.3
  261.7 75.0 %all-gather.26.cloned.1.call-done = bf16[2048,1024]{1,0:T(8,128)(2,1)} async-done(((bf16[512,1024]{1,0:T(8,128)(2,1)}), bf16[2048,1024]{1,0:T(8,128)(2,1)}) %all-gather.26.cloned.1.call-update) | async-done | bytes 4194320 | tf_op jit(solution)/shard_map/all_gather | solution.py:129
  336.7 44.8 %all-gather.22.cloned.1.call-done = bf16[1280,2048]{1,0:T(8,128)(2,1)} async-done(((bf16[160,2048]{1,0:T(8,128)(2,1)}), bf16[1280,2048]{1,0:T(8,128)(2,1)}) %all-gather.22.cloned.1.call-update) | async-done | bytes 5242896 | tf_op jit(solution)/shard_map/all_gather | solution.py:161
  381.5 10.2 fusion.44
  391.7 69.5 %all-gather.24.cloned.1.call-done = bf16[2048,1024]{1,0:T(8,128)(2,1)} async-done(((bf16[512,1024]{1,0:T(8,128)(2,1)}), bf16[2048,1024]{1,0:T(8,128)(2,1)}) %all-gather.24.cloned.1.call-update) | async-done | bytes 4194320 | tf_op jit(solution)/shard_map/all_gather | solution.py:128
  461.2 10.2 fusion.43
  471.5 70.5 %all-gather.28.cloned.1.call-done = bf16[1024,2048]{1,0:T(8,128)(2,1)} async-done(((bf16[1024,512]{1,0:T(8,128)(2,1)}), bf16[1024,2048]{1,0:T(8,128)(2,1)}) %all-gather.28.cloned.1.call-update) | async-done | bytes 4194320 | tf_op jit(solution)/shard_map/all_gather | solution.py:130
  541.9 44.3 %all-gather.30.cloned.1.call-done = bf16[1280,2048]{1,0:T(8,128)(2,1)} async-done(((bf16[160,2048]{1,0:T(8,128)(2,1)}), bf16[1280,2048]{1,0:T(8,128)(2,1)}) %all-gather.30.cloned.1.call-update) | async-done | bytes 5242896 | tf_op jit(solution)/shard_map/all_gather | solution.py:182
  586.2 14.7 %multiply_convert_fusion.1 = (bf16[1280,1024]{1,0:T(8,128)(2,1)S(1)}, bf16[1280,1024]{1,0:T(8,128)(2,1)S(1)}, bf16[1280,1024]{1,0:T(8,128)(2,1)}) fusion(f32[1280,1024]{1,0:T(8,128)} %fusion.43, f32[1280,1024]{1,0:T(8,128)} %fusion.44, bf16[1280,2048]{1,0:T(8,128)(2,1)} %all-gather.30.cloned.1.call-done, bf16[1024,2048]{1,0:T(8,128)(2,1)} %all-gather.28.cloned.1.call-done), kind=kOutput, calls=%fused_computation.17 | convolution fusion | flops 5388369920 | bytes 27787264 | tf_op jit(solution)/shard_map/dot_general | solution.py:16
  600.9 8.2 fusion.45
  609.1 11.0 convolution_add_fusion
  620.2 81.7 %reduce-scatter.16.cloned.1.call-done = f32[160,2048]{1,0:T(8,128)} async-done(((f32[1280,2048]{1,0:T(8,128)}), f32[160,2048]{1,0:T(8,128)}) %reduce-scatter.16.cloned.1.call-update) | async-done | bytes 1310736 | tf_op jit(solution)/shard_map/reduce_scatter | solution.py:189
  701.9 1.7 multiply_reduce_fusion.1
  703.6 2.6 fusion.38
  706.3 10.1 convolution_convert_fusion.1
  716.4 10.2 convolution_convert_fusion.2
  726.7 10.2 convolution_convert_fusion.3
  737.4 10.1 all-gather.32.cloned.1.call-done
  747.5 5.0 convolution_convert_fusion.4
  752.5 4.3 convolution_convert_fusion.8
  756.9 10.8 fusion.11
  767.7 5.1 convolution_convert_fusion.5
  772.8 16.7 %multiply_reduce_fusion = (f32[4,1280]{1,0:T(4,128)S(1)}, f32[4,1280,1280]{1,2,0:T(8,128)}) fusion(f32[4,1280,1280]{1,2,0:T(8,128)} %get-tuple-element.91, f32[4,1280]{1,0:T(4,128)S(1)} %log_add_fusion, bf16[1280,4,64]{0,2,1:T(8,128)(2,1)S(1)} %bitcast.90, bf16[1280,4,64]{0,2,1:T(8,128)(2,1)S(1)} %bitcast.98), kind=kOutput, calls=%fused_computation.3 | convolution fusion | flops 858516480 | bytes 53780480 | tf_op jit(solution)/shard_map/while/body/eval_jaxpr/qhd,khd->hqk/dot_general | solution.py:94
  789.7 22.5 %multiply_convert_fusion = bf16[4,1280,1280]{1,2,0:T(8,128)(2,1)} fusion(f32[4,1280,1280]{1,2,0:T(8,128)} %get-tuple-element.93, f32[4,1280,1280]{1,2,0:T(8,128)} %get-tuple-element.91, f32[4,1280]{1,0:T(4,128)S(1)} %get-tuple-element.92, f32[4,1280]{1,0:T(4,128)S(1)} %log_add_fusion), kind=kLoop, calls=%fused_computation.2 | loop fusion | flops 26214400 | bytes 65576960 | tf_op jit(solution)/shard_map/while/body/eval_jaxpr/convert_element_type | solution.py:96
  812.2 9.0 fusion.10
  821.2 7.2 fusion.9
  828.9 2.6 convolution_convert_fusion.6
  831.6 5.1 convolution_convert_fusion.7
  837.0 2.9 fusion.46
  839.9 5.6 fusion.47
  845.6 8.4 add_convert_fusion
  854.1 10.0 convolution_convert_fusion
  864.1 2.9 convert_element_type.194
  867.0 39.0 %reduce-scatter.30.cloned.1.call-done = bf16[512,1024]{1,0:T(8,128)(2,1)} async-done(((bf16[2048,1024]{1,0:T(8,128)(2,1)}), bf16[512,1024]{1,0:T(8,128)(2,1)}) %reduce-scatter.30.cloned.1.call-update) | async-done | bytes 1048592 | tf_op jit(solution)/shard_map/reduce_scatter | solution.py:234
  906.0 2.8 convert_element_type.192
  908.8 76.6 %reduce-scatter.28.cloned.1.call-done = bf16[512,1024]{1,0:T(8,128)(2,1)} async-done(((bf16[2048,1024]{1,0:T(8,128)(2,1)}), bf16[512,1024]{1,0:T(8,128)(2,1)}) %reduce-scatter.28.cloned.1.call-update) | async-done | bytes 1048592 | tf_op jit(solution)/shard_map/reduce_scatter | solution.py:231
  985.4 2.8 convert_element_type.190
  988.2 25.1 %reduce-scatter.26.cloned.1.call-done = bf16[256,512]{1,0:T(8,128)(2,1)} async-done(((bf16[256,2048]{1,0:T(8,128)(2,1)}), bf16[256,512]{1,0:T(8,128)(2,1)}) %reduce-scatter.26.cloned.1.call-update) | async-done | bytes 262160 | tf_op jit(solution)/shard_map/reduce_scatter | solution.py:228
  1013.3 1.8 convert_element_type.188
  1015.1 26.2 %reduce-scatter.24.cloned.1.call-done = bf16[512,256]{1,0:T(8,128)(2,1)} async-done(((bf16[2048,256]{1,0:T(8,128)(2,1)}), bf16[512,256]{1,0:T(8,128)(2,1)}) %reduce-scatter.24.cloned.1.call-update) | async-done | bytes 262160 | tf_op jit(solution)/shard_map/reduce_scatter | solution.py:225
  1041.3 1.8 convert_element_type.186
  1043.0 26.4 %reduce-scatter.22.cloned.1.call-done = bf16[512,256]{1,0:T(8,128)(2,1)} async-done(((bf16[2048,256]{1,0:T(8,128)(2,1)}), bf16[512,256]{1,0:T(8,128)(2,1)}) %reduce-scatter.22.cloned.1.call-update) | async-done | bytes 262160 | tf_op jit(solution)/shard_map/reduce_scatter | solution.py:222
  1069.5 1.8 convert_element_type.184
  1071.2 26.2 %reduce-scatter.20.cloned.1.call-done = bf16[512,256]{1,0:T(8,128)(2,1)} async-done(((bf16[2048,256]{1,0:T(8,128)(2,1)}), bf16[512,256]{1,0:T(8,128)(2,1)}) %reduce-scatter.20.cloned.1.call-update) | async-done | bytes 262160 | tf_op jit(solution)/shard_map/reduce_scatter | solution.py:219
  1097.4 1.8 convert_element_type.182
  1099.2 59.3 %reduce-scatter.18.cloned.1.call-done = bf16[160,2048]{1,0:T(8,128)(2,1)} async-done(((bf16[1280,2048]{1,0:T(8,128)(2,1)}), bf16[160,2048]{1,0:T(8,128)(2,1)}) %reduce-scatter.18.cloned.1.call-update) | async-done | bytes 655376 | tf_op jit(solution)/shard_map/reduce_scatter | solution.py:212
  1160.1 39.7 %all-reduce = (f32[2048]{0:T(1024)}, f32[2048]{0:T(1024)}) all-reduce(f32[2048]{0:T(1024)S(1)} %get-tuple-element.54, f32[2048]{0:T(1024)S(1)} %get-tuple-element.52), channel_id=1, replica_groups=mesh['fsdp'=4,'tensor'=8] {'fsdp','tensor'}, use_global_device_ids=true, to_apply=%region_14.15 | all-reduce | flops 4096 | bytes 32768 | tf_op jit(solution)/shard_map/psum | solution.py:217
  1199.8 19.3 %reduce-scatter.14.cloned.1.call-done = bf16[160,2048]{1,0:T(8,128)(2,1)} async-done(((bf16[1280,2048]{1,0:T(8,128)(2,1)}), bf16[160,2048]{1,0:T(8,128)(2,1)}) %reduce-scatter.14.cloned.1.call-update) | async-done | bytes 655376 | tf_op jit(solution)/shard_map/reduce_scatter | solution.py:167
  1219.1 3.4 fusion.23
  (127 shorter events, 16.7 us)
Async XLA Ops:
  7.2 31.5 %all-gather.18.cloned.1.call-start = ((), (), s32[]{:S(2)}) async-start(), calls=%async_computation.14 | async-start | bytes 1310720 | tf_op jit(solution)/shard_map/all_gather | solution.py:125
  7.9 73.9 %all-gather.12.cloned.1.call-start = ((), (), s32[]{:S(2)}) async-start(), calls=%async_computation.11 | async-start | bytes 5898240 | tf_op jit(solution)/shard_map/all_gather | solution.py:144
  8.6 1.3 copy-start.17
  10.0 0.6 copy-start.19
  12.7 98.6 %all-gather.16.cloned.1.call-start = ((), (), s32[]{:S(2)}) async-start(), calls=%async_computation.13 | async-start | bytes 1310720 | tf_op jit(solution)/shard_map/all_gather | solution.py:124
  13.4 126.8 %all-gather.14.cloned.1.call-start = ((), (), s32[]{:S(2)}) async-start(), calls=%async_computation.12 | async-start | bytes 1310720 | tf_op jit(solution)/shard_map/all_gather | solution.py:126
  14.0 155.1 %all-gather.20.cloned.1.call-start = ((), (), s32[]{:S(2)}) async-start(), calls=%async_computation.15 | async-start | bytes 1310720 | tf_op jit(solution)/shard_map/all_gather | solution.py:127
  14.6 242.4 %reduce-scatter.12.cloned.1.call-start = ((), (), s32[]{:S(2)}) async-start(), calls=%async_computation.16 | async-start | bytes 11796480 | tf_op jit(solution)/shard_map/reduce_scatter | solution.py:154
  20.3 95.4 %copy-start.4 = (f32[1280,32]{0,1:T(8,128)}, f32[1280,32]{0,1:T(8,128)S(1)}, u32[]{:S(2)}) copy-start(f32[1280,32]{0,1:T(8,128)S(1)} %get-tuple-element.89) | copy-start | bytes 491524
  116.0 11.2 copy-start.6
  116.0 11.1 copy-start.8
  116.0 11.1 copy-start.10
  116.1 11.1 copy-start.12
  175.7 0.8 copy-start.21
  175.7 81.3 %copy-start = (bf16[160,2048]{1,0:T(8,128)(2,1)S(1)}, bf16[160,2048]{1,0:T(8,128)(2,1)}, u32[]{:S(2)}) copy-start(bf16[160,2048]{1,0:T(8,128)(2,1)} %param.12) | copy-start | bytes 1966084
  175.8 160.9 %all-gather.26.cloned.1.call-start = ((), (), s32[]{:S(2)}) async-start(), calls=%async_computation.19 | async-start | bytes 5242880 | tf_op jit(solution)/shard_map/all_gather | solution.py:129
  176.5 205.0 %all-gather.22.cloned.1.call-start = ((), (), s32[]{:S(2)}) async-start(), calls=%async_computation.17 | async-start | bytes 5898240 | tf_op jit(solution)/shard_map/all_gather | solution.py:161
  259.6 201.6 %all-gather.24.cloned.1.call-start = ((), (), s32[]{:S(2)}) async-start(), calls=%async_computation.18 | async-start | bytes 5242880 | tf_op jit(solution)/shard_map/all_gather | solution.py:128
  260.4 281.6 %all-gather.28.cloned.1.call-start = ((), (), s32[]{:S(2)}) async-start(), calls=%async_computation.20 | async-start | bytes 5242880 | tf_op jit(solution)/shard_map/all_gather | solution.py:130
  261.0 325.2 %all-gather.30.cloned.1.call-start = ((), (), s32[]{:S(2)}) async-start(), calls=%async_computation.22 | async-start | bytes 5898240 | tf_op jit(solution)/shard_map/all_gather | solution.py:182
  261.7 440.2 %reduce-scatter.16.cloned.1.call-start = ((), (), s32[]{:S(2)}) async-start(), calls=%async_computation.23 | async-start | bytes 11796480 | tf_op jit(solution)/shard_map/reduce_scatter | solution.py:189
  586.2 14.7 %copy-start.23 = (bf16[2048,1024]{1,0:T(8,128)(2,1)S(1)}, bf16[2048,1024]{1,0:T(8,128)(2,1)}, u32[]{:S(2)}) copy-start(bf16[2048,1024]{1,0:T(8,128)(2,1)} %all-gather.24.cloned.1.call-done) | copy-start | bytes 12582916
  600.8 8.3 copy-start.25
  600.8 8.3 copy-start.24
  600.9 8.3 copy-start.22
  620.1 83.4 %copy-start.3 = (bf16[160,2048]{1,0:T(8,128)(2,1)S(1)}, bf16[160,2048]{1,0:T(8,128)(2,1)}, u32[]{:S(2)}) copy-start(bf16[160,2048]{1,0:T(8,128)(2,1)} %param.23) | copy-start | bytes 1966084
  620.2 127.3 %all-gather.32.cloned.1.call-start = ((), (), s32[]{:S(2)}) async-start(), calls=%async_computation.24 | async-start | bytes 5898240 | tf_op jit(solution)/shard_map/all_gather | solution.py:195
  706.2 157.9 %reduce-scatter.32.cloned.1.call-start = ((), (), s32[]{:S(2)}) async-start(), calls=%async_computation.32 | async-start | bytes 5242880 | tf_op jit(solution)/shard_map/reduce_scatter | solution.py:237
  716.4 189.6 %reduce-scatter.30.cloned.1.call-start = ((), (), s32[]{:S(2)}) async-start(), calls=%async_computation.31 | async-start | bytes 5242880 | tf_op jit(solution)/shard_map/reduce_scatter | solution.py:234
  726.6 258.7 %reduce-scatter.28.cloned.1.call-start = ((), (), s32[]{:S(2)}) async-start(), calls=%async_computation.30 | async-start | bytes 5242880 | tf_op jit(solution)/shard_map/reduce_scatter | solution.py:231
  736.9 276.4 %reduce-scatter.26.cloned.1.call-start = ((), (), s32[]{:S(2)}) async-start(), calls=%async_computation.29 | async-start | bytes 1310720 | tf_op jit(solution)/shard_map/reduce_scatter | solution.py:228
  752.5 288.8 %reduce-scatter.24.cloned.1.call-start = ((), (), s32[]{:S(2)}) async-start(), calls=%async_computation.28 | async-start | bytes 1310720 | tf_op jit(solution)/shard_map/reduce_scatter | solution.py:225
  789.4 280.0 %reduce-scatter.22.cloned.1.call-start = ((), (), s32[]{:S(2)}) async-start(), calls=%async_computation.27 | async-start | bytes 1310720 | tf_op jit(solution)/shard_map/reduce_scatter | solution.py:222
  789.7 22.5 %copy-start.11 = (bf16[1280,4,32]{0,2,1:T(8,128)(2,1)S(1)}, bf16[1280,4,32]{0,2,1:T(8,128)(2,1)}, u32[]{:S(2)}) copy-start(bf16[1280,4,32]{0,2,1:T(8,128)(2,1)} %copy-done.10) | copy-start | bytes 983044
  789.7 22.5 %copy-start.13 = (bf16[1280,4,32]{0,2,1:T(8,128)(2,1)S(1)}, bf16[1280,4,32]{0,2,1:T(8,128)(2,1)}, u32[]{:S(2)}) copy-start(bf16[1280,4,32]{0,2,1:T(8,128)(2,1)} %copy-done.12) | copy-start | bytes 983044
  812.2 9.0 copy-start.7
  812.2 9.0 copy-start.9
  812.2 16.7 %slice-start = ((s8[5242880]{0:T(1024)(128)(4,1)}), s8[1048576]{0:T(1024)(128)(4,1)S(1)}, s32[]{:S(2)}) async-start(s8[5242880]{0:T(1024)(128)(4,1)} %bitcast.104), calls=%async_computation.33 | async-start | bytes 2097152
  821.2 7.3 copy-start.5
  821.2 7.3 copy-start.16
  821.2 7.7 slice-start.1
  831.6 265.8 %reduce-scatter.20.cloned.1.call-start = ((), (), s32[]{:S(2)}) async-start(), calls=%async_computation.26 | async-start | bytes 1310720 | tf_op jit(solution)/shard_map/reduce_scatter | solution.py:219
  836.8 321.8 %reduce-scatter.18.cloned.1.call-start = ((), (), s32[]{:S(2)}) async-start(), calls=%async_computation.25 | async-start | bytes 5898240 | tf_op jit(solution)/shard_map/reduce_scatter | solution.py:212
  837.0 2.9 copy-start.14
  839.9 5.6 copy-start.15
  854.0 365.1 %reduce-scatter.14.cloned.1.call-start = ((), (), s32[]{:S(2)}) async-start(), calls=%async_computation.21 | async-start | bytes 5898240 | tf_op jit(solution)/shard_map/reduce_scatter | solution.py:167
  867.0 291.6 %copy-start.1 = (bf16[160,2048]{1,0:T(8,128)(2,1)S(1)}, bf16[160,2048]{1,0:T(8,128)(2,1)}, u32[]{:S(2)}) copy-start(bf16[160,2048]{1,0:T(8,128)(2,1)} %param.12) | copy-start | bytes 1966084
  867.0 291.6 %copy-start.18 = (f32[2048]{0:T(1024)S(1)}, f32[2048]{0:T(1024)}, u32[]{:S(2)}) copy-start(f32[2048]{0:T(1024)} %copy-done.17) | copy-start | bytes 24580
  867.0 291.6 %copy-start.20 = (f32[160]{0:T(256)S(1)}, f32[160]{0:T(256)}, u32[]{:S(2)}) copy-start(f32[160]{0:T(256)} %copy-done.19) | copy-start | bytes 1924
  908.8 310.4 %copy-start.2 = (f32[160,2048]{1,0:T(8,128)S(1)}, f32[160,2048]{1,0:T(8,128)}, u32[]{:S(2)}) copy-start(f32[160,2048]{1,0:T(8,128)} %reduce-scatter.16.cloned.1.call-done) | copy-start | bytes 3932164
Sparse Core Ops, SparseCore 0:
  9.6 29.0 all-gather.17
  41.2 40.5 all-gather.11
  83.4 27.8 all-gather.15
  112.7 27.4 all-gather.13
  141.6 27.4 all-gather.19
  175.9 81.0 reduce-scatter.11
  258.6 78.0 all-gather.25
  339.2 42.2 all-gather.21
  383.1 78.1 all-gather.23
  462.6 79.2 all-gather.27
  543.8 42.3 all-gather.29
  620.3 81.5 reduce-scatter.15
  706.3 41.0 all-gather.31
  749.6 76.7 reduce-scatter.31
  828.7 77.2 reduce-scatter.29
  908.1 77.2 reduce-scatter.27
  987.6 25.5 reduce-scatter.25
  1015.4 25.7 reduce-scatter.23
  1043.6 25.7 reduce-scatter.21
  1071.6 25.7 reduce-scatter.19
  1101.2 57.2 reduce-scatter.17
  1161.9 57.1 reduce-scatter.13
where the time goes:
time: 1240 us; the launch traced here: 1230 us
  waiting for transfers between devices  882 us (71%)
  matrix products  220 us (18%)
  other arithmetic  70.8 us (6%)
  blocking collectives  39.7 us (3%)
  between operations  15 us (1%)
    reduce_scatter x1, waiting for transfers between devices, shards(): lax.psum_scatter(dot_nt(grad_gate, wg) + dot_nt(grad_up, wu), 'tensor', s...  81.7 us
    reduce_scatter x1, waiting for transfers between devices, shards(): lax.psum_scatter(jnp.dot(attended, wo, preferred_element_type=jnp.float32...  80.4 us
    reduce_scatter x1, waiting for transfers between devices, shards(): lax.psum_scatter(grad_wgate.astype(jnp.bfloat16), 'fsdp', scatter_dimensi...  76.6 us
    all_gather x1, waiting for transfers between devices, shards(): lax.all_gather(local[5], 'fsdp', axis=0, tiled=True)  75 us
    all_gather x1, waiting for transfers between devices, shards(): lax.all_gather(local[6], 'fsdp', axis=1, tiled=True)  70.5 us
    all_gather x1, waiting for transfers between devices, shards(): lax.all_gather(local[4], 'fsdp', axis=0, tiled=True)  69.5 us
    reduce_scatter x1, waiting for transfers between devices, shards(): lax.psum_scatter(grad_na_part.astype(jnp.bfloat16), 'tensor', scatter_dim...  59.3 us
    dot_general x7, matrix products, dot_nt(): lax.dot_general(left, right, (((1,), (1,)), ((), ())), preferred_element_...  55.2 us
  transfers between devices with their start and end apart: 22, of which 21 were waited for; matrix products, arithmetic and copies ran while one was open for 20% of the time, Pallas kernels for 0%

commit v1 on v0

v1 whole, which is shorter than its diff:
```python
import functools
import math

import jax
import jax.numpy as jnp
from jax import lax
from jax.experimental import pallas as pl
from jax.experimental.pallas import tpu as pltpu
from jax.sharding import PartitionSpec as P

HEAD = 64
SAMPLE = 512
EPS = 1e-05
ROPE_BASE = 130000.0
MESH = pl.DeviceIdType.MESH
BF16 = jnp.bfloat16
F32 = jnp.float32
ANY = pl.BlockSpec(memory_space=pl.ANY)
VMEM = pl.BlockSpec(memory_space=pltpu.VMEM)


def flip(index, bit):
    return index + bit - 2 * bit * ((index // bit) % 2)


def dot_nt(left, right):
    return lax.dot_general(left, right, (((1,), (1,)), ((), ())), preferred_element_type=F32)


def dot_tn(left, right):
    return lax.dot_general(left, right, (((0,), (0,)), ((), ())), preferred_element_type=F32)


class Group:
    def __init__(self, z_size, t_size):
        self.z_size = z_size
        self.t_size = t_size
        self.size = 2 * t_size
        inner = []
        bit = 2
        while bit < t_size:
            inner.append(bit)
            bit *= 2
        self.core = 1
        self.pair = t_size
        self.orders = (tuple(inner) + (self.pair,), tuple(inner[::-1]) + (self.pair,))
        self.inner = (tuple(inner), tuple(inner[::-1]))
        self.bits = (self.core,) + tuple(inner) + (self.pair,)
        masks = [0]
        for b in self.orders[0]:
            masks = masks + [m + b for m in masks]
        self.masks = tuple(masks)

    def place(self):
        return lax.axis_index("fsdp"), lax.axis_index("tensor")

    def rank(self, mask=0):
        z, t = self.place()
        r = (z % 2) * self.t_size + t
        for b in self.bits:
            if mask & b:
                r = flip(r, b)
        return r

    def partner(self, bit):
        z, t = self.place()
        if bit == self.pair:
            return (flip(z, 1), t)
        return (z, flip(t, bit))

    def greet(self, bits=None):
        barrier = pltpu.get_barrier_semaphore()
        bits = self.bits if bits is None else bits
        for b in bits:
            pl.semaphore_signal(barrier, inc=1, device_id=self.partner(b), device_id_type=MESH)
        pl.semaphore_wait(barrier, len(bits))


def last_bit(mask, order):
    found = None
    for b in order:
        if mask & b:
            found = b
    return found


def gather_steps(grp, x_ref, o_ref, send, recv, local):
    rows = x_ref.shape[0]
    half = rows // 2

    def at(ref, mask, h):
        return ref.at[pl.ds(pl.multiple_of(grp.rank(mask) * rows + h * half, half), half)]

    own = pltpu.make_async_copy(x_ref, o_ref.at[pl.ds(pl.multiple_of(grp.rank() * rows, rows), rows)], local)
    own.start()
    full = [(grp.pair,) + grp.inner[h] + (grp.core,) for h in range(2)]
    sent = []

    def copy(h, mask, bit):
        src = x_ref.at[pl.ds(h * half, half)] if mask == 0 else at(o_ref, mask, h)
        k = mask | bit
        return pltpu.make_async_remote_copy(
            src_ref=src,
            dst_ref=at(o_ref, mask, h),
            send_sem=send.at[h, k],
            recv_sem=recv.at[h, k],
            device_id=grp.partner(bit),
            device_id_type=MESH,
        )

    def arrived(h, mask):
        bit = last_bit(mask, full[h])
        pltpu.make_async_remote_copy(
            src_ref=at(o_ref, mask, h),
            dst_ref=at(o_ref, mask, h),
            send_sem=send.at[h, mask],
            recv_sem=recv.at[h, mask],
            device_id=grp.partner(bit),
            device_id_type=MESH,
        ).wait_recv()

    def forward(h, mask):
        order = full[h]
        start = 0 if mask == 0 else order.index(last_bit(mask, order)) + 1
        for bit in order[start:]:
            c = copy(h, mask, bit)
            c.start()
            sent.append(c)

    for h in range(2):
        forward(h, 0)
    plain = sorted(
        (m for m in grp.masks if m), key=lambda m: (m & grp.pair, bin(m).count("1"))
    )
    for i, _ in enumerate(plain):
        for h in range(2):
            m = plain[i] if h == 0 else mirror(grp, plain[i])
            arrived(h, m)
            forward(h, m)
    for m in grp.masks:
        for h in range(2):
            arrived(h, m | grp.core)
    own.wait()
    for c in sent:
        c.wait_send()


def mirror(grp, mask):
    out = mask & (grp.pair | grp.core)
    a, b = grp.inner
    for p, q in zip(a, b):
        if mask & p:
            out |= q
    return out


def gather_kernel(grp, x_ref, o_ref, send, recv, local):
    grp.greet()
    gather_steps(grp, x_ref, o_ref, send, recv, local)


def gather(grp, x, cid, name):
    rows, width = x.shape
    return pl.pallas_call(
        functools.partial(gather_kernel, grp),
        out_shape=jax.ShapeDtypeStruct((rows * grp.size, width), x.dtype),
        in_specs=[ANY],
        out_specs=ANY,
        scratch_shapes=[
            pltpu.SemaphoreType.DMA((2, grp.size)),
            pltpu.SemaphoreType.DMA((2, grp.size)),
            pltpu.SemaphoreType.DMA,
        ],
        compiler_params=pltpu.CompilerParams(collective_id=cid, has_side_effects=True),
        name=name,
    )(x)


TILE = 16


def add_rows(dst, src, rows):
    @pl.loop(0, rows // TILE)
    def _(i):
        part = pl.ds(pl.multiple_of(i * TILE, TILE), TILE)
        dst[part] = (dst[part].astype(F32) + src[part].astype(F32)).astype(dst.dtype)


def scatter_scratch(grp, rows, width):
    n = len(grp.masks)
    return [
        pltpu.VMEM((n, rows, width), BF16),
        pltpu.VMEM((n, rows, width), BF16),
        pltpu.VMEM((2, n, rows // 2, width), BF16),
        pltpu.SemaphoreType.DMA((n,)),
        pltpu.SemaphoreType.DMA((n,)),
        pltpu.SemaphoreType.DMA((n,)),
        pltpu.SemaphoreType.DMA((2, n)),
        pltpu.SemaphoreType.DMA((2, n)),
    ]


def scatter_steps(grp, p_ref, acc, crecv, rbuf, local, csend, crecv_sem, send, recv):
    n, rows, _ = acc.shape
    half = rows // 2
    index = {m: i for i, m in enumerate(grp.masks)}
    order_masks = sorted(grp.masks, key=lambda m: (0 if m & grp.pair else 1, -bin(m).count("1")))

    def block(mask):
        return p_ref.at[pl.ds(pl.multiple_of(grp.rank(mask) * rows, rows), rows)]

    started = []
    loads = {}
    for m in order_masks:
        i = index[m]
        c = pltpu.make_async_remote_copy(
            src_ref=block(m | grp.core),
            dst_ref=crecv.at[i],
            send_sem=csend.at[i],
            recv_sem=crecv_sem.at[i],
            device_id=grp.partner(grp.core),
            device_id_type=MESH,
        )
        c.start()
        started.append(c)
        d = pltpu.make_async_copy(block(m), acc.at[i], local.at[i])
        d.start()
        loads[m] = (c, d)
    for m in order_masks:
        c, d = loads[m]
        d.wait()
        c.wait_recv()
        add_rows(acc.at[index[m]], crecv.at[index[m]], rows)

        def nothing():
            return None

    slots = []
    for h in range(2):
        s = {}
        order = grp.orders[h]
        for i in range(len(order)):
            later = order[i + 1 :]
            for m in grp.masks:
                if all((not m & b) or b in later for b in order):
                    s[(i, m)] = len(s)
        slots.append(s)

    def part(h, mask):
        return acc.at[index[mask], pl.ds(h * half, half)]

    def ship(h, i, mask):
        bit = grp.orders[h][i]
        k = slots[h][(i, mask - bit)]
        c = pltpu.make_async_remote_copy(
            src_ref=part(h, mask),
            dst_ref=rbuf.at[h, k],
            send_sem=send.at[h, k],
            recv_sem=recv.at[h, k],
            device_id=grp.partner(bit),
            device_id_type=MESH,
        )
        c.start()
        started.append(c)

    def take(h, i, mask):
        bit = grp.orders[h][i]
        k = slots[h][(i, mask)]
        pltpu.make_async_remote_copy(
            src_ref=part(h, mask),
            dst_ref=rbuf.at[h, k],
            send_sem=send.at[h, k],
            recv_sem=recv.at[h, k],
            device_id=grp.partner(bit),
            device_id_type=MESH,
        ).wait_recv()
        add_rows(part(h, mask), rbuf.at[h, k], half)

    last = len(grp.orders[0]) - 1
    for p in (grp.pair, 0):
        for i in range(last + 1):
            for h in range(2):
                order = grp.orders[h]
                later = order[i:]
                alive = [
                    m
                    for m in order_masks
                    if (m & grp.pair) == p and all((not m & b) or b in later for b in order)
                ]
                for m in alive:
                    if i > 0:
                        take(h, i - 1, m)
                    if m & order[i]:
                        ship(h, i, m)
    for h in range(2):
        take(h, last, 0)
    for c in started:
        c.wait_send()


def scatter_kernel(grp, rows, p_ref, o_ref, *scratch):
    grp.greet()
    scatter_steps(grp, p_ref, *scratch)
    o_ref[...] = scratch[0][0].astype(o_ref.dtype)


def scatter(grp, part, cid, name):
    rows, width = part.shape[0] // grp.size, part.shape[1]
    return pl.pallas_call(
        functools.partial(scatter_kernel, grp, rows),
        out_shape=jax.ShapeDtypeStruct((rows, width), F32),
        in_specs=[ANY],
        out_specs=VMEM,
        scratch_shapes=scatter_scratch(grp, rows, width),
        compiler_params=pltpu.CompilerParams(
            collective_id=cid, has_side_effects=True, vmem_limit_bytes=48 << 20
        ),
        name=name,
    )(part)


def sum_kernel(hops, x_ref, o_ref, buf, send, recv):
    z, t = lax.axis_index("fsdp"), lax.axis_index("tensor")

    def where(hop):
        axis, bit = hop
        return (flip(z, bit), t) if axis == "fsdp" else (z, flip(t, bit))

    barrier = pltpu.get_barrier_semaphore()
    for hop in hops:
        pl.semaphore_signal(barrier, inc=1, device_id=where(hop), device_id_type=MESH)
    pl.semaphore_wait(barrier, len(hops))
    buf[0] = x_ref[...]
    for i, hop in enumerate(hops):
        c = pltpu.make_async_remote_copy(
            src_ref=buf.at[2 * i],
            dst_ref=buf.at[2 * i + 1],
            send_sem=send.at[i],
            recv_sem=recv.at[i],
            device_id=where(hop),
            device_id_type=MESH,
        )
        c.start()
        c.wait()
        buf[2 * i + 2] = buf[2 * i] + buf[2 * i + 1]
    o_ref[...] = buf[2 * len(hops)]


def sum_all(z_size, t_size, x, cid):
    hops = []
    for axis, size in (("tensor", t_size), ("fsdp", z_size)):
        bit = 1
        while bit < size:
            hops.append((axis, bit))
            bit *= 2
    n = len(hops)
    return pl.pallas_call(
        functools.partial(sum_kernel, hops),
        out_shape=jax.ShapeDtypeStruct(x.shape, x.dtype),
        in_specs=[VMEM],
        out_specs=VMEM,
        scratch_shapes=[
            pltpu.VMEM((2 * n + 1,) + x.shape, x.dtype),
            pltpu.SemaphoreType.DMA((n,)),
            pltpu.SemaphoreType.DMA((n,)),
        ],
        compiler_params=pltpu.CompilerParams(collective_id=cid, has_side_effects=True),
        name="sum_all",
    )(x)


def swap_halves(value):
    half = HEAD // 2
    width = value.shape[1]
    pieces = []
    for at in range(0, width, HEAD):
        pieces.append(value[:, at + half : at + HEAD])
        pieces.append(value[:, at : at + half])
    if width % 128:
        return jnp.concatenate(pieces, axis=1)
    lane = lax.broadcasted_iota(jnp.int32, value.shape, 1)
    return jnp.where(
        lane % HEAD < half, pltpu.roll(value, width - half, 1), pltpu.roll(value, half, 1)
    )


QB = 256


def bands(length):
    for at in range(0, length, QB):
        first = max(0, at - SAMPLE)
        yield at, min(QB, length - at), first, at + min(QB, length - at) - first


def kept(start_row, at, size, first, width):
    key = first + lax.broadcasted_iota(jnp.int32, (width, size), 0)
    query = at + lax.broadcasted_iota(jnp.int32, (width, size), 1)
    return (key >= start_row) & (key <= query)


def attend_kernel(heads, qkv_ref, cos_ref, sin_ref, start_ref, q_ref, k_ref, v_ref, o_ref, lse_ref):
    wide = heads * HEAD
    length = qkv_ref.shape[0]

    @pl.loop(0, length // QB)
    def _(i):
        rows = pl.ds(pl.multiple_of(i * QB, QB), QB)
        cosine, sine = cos_ref[rows], sin_ref[rows]
        query, key = qkv_ref[rows, :wide], qkv_ref[rows, wide : 2 * wide]
        query = (query * cosine + swap_halves(query) * sine).astype(BF16)
        q_ref[rows] = query
        k_ref[rows] = (key * cosine + swap_halves(key) * sine).astype(BF16)
        v_ref[rows] = qkv_ref[rows, 2 * wide :].astype(BF16)

    for h in range(heads):
        lanes = slice(h * HEAD, (h + 1) * HEAD)
        for at, size, first, width in bands(length):
            query = q_ref[at : at + size, lanes] * BF16(HEAD**-0.5)
            key = k_ref[first : first + width, lanes]
            scores = dot_nt(key, query)
            mask = kept(start_ref[0, :, at : at + size], at, size, first, width)
            scores = jnp.where(mask, scores, -1e9)
            top = jnp.max(scores, axis=0, keepdims=True)
            expo = jnp.exp(scores - top)
            total = jnp.sum(expo, axis=0, keepdims=True)
            weights = (expo * (1.0 / total)).astype(BF16)
            o_ref[at : at + size, lanes] = dot_tn(
                weights, v_ref[first : first + width, lanes]
            ).astype(BF16)
            lse_ref[0, h : h + 1, at : at + size] = top + jnp.log(total)


def attend(qkv, cosine, sine, start, heads):
    rows, _, length = start.shape
    wide = heads * HEAD

    def tall(width):
        return pl.BlockSpec((length, width), lambda r: (r, 0))

    out = jax.ShapeDtypeStruct((rows * length, wide), BF16)
    return pl.pallas_call(
        functools.partial(attend_kernel, heads),
        grid=(rows,),
        out_shape=[out, out, out, out, jax.ShapeDtypeStruct((rows, heads, length), F32)],
        in_specs=[tall(3 * wide), tall(wide), tall(wide), pl.BlockSpec((1, 1, length), lambda r: (r, 0, 0))],
        out_specs=[tall(wide)] * 4 + [pl.BlockSpec((1, heads, length), lambda r: (r, 0, 0))],
        compiler_params=pltpu.CompilerParams(vmem_limit_bytes=48 << 20),
        name="attend",
    )(qkv, cosine, sine, start)


def attend_back_kernel(
    heads, q_ref, k_ref, v_ref, do_ref, lse_ref, cos_ref, sin_ref, start_ref, out_ref, dq, dk, dv
):
    wide = heads * HEAD
    length = q_ref.shape[0]
    dk[...] = jnp.zeros_like(dk)
    dv[...] = jnp.zeros_like(dv)
    for h in range(heads):
        lanes = slice(h * HEAD, (h + 1) * HEAD)
        for at, size, first, width in bands(length):
            query = q_ref[at : at + size, lanes]
            key = k_ref[first : first + width, lanes]
            value = v_ref[first : first + width, lanes]
            grad = do_ref[at : at + size, lanes]
            scores = dot_nt(key, query * BF16(HEAD**-0.5))
            mask = kept(start_ref[0, :, at : at + size], at, size, first, width)
            weights = jnp.where(
                mask, jnp.exp(jnp.where(mask, scores, -1e9) - lse_ref[0, h : h + 1, at : at + size]), 0.0
            )
            dv[first : first + width, lanes] += jnp.dot(
                weights.astype(BF16), grad, preferred_element_type=F32
            )
            grad_weights = dot_nt(value, grad)
            inner = jnp.sum(weights * grad_weights, axis=0, keepdims=True)
            grad_scores = (weights * (grad_weights - inner)).astype(BF16)
            dq[at : at + size, lanes] = dot_tn(grad_scores, key)
            dk[first : first + width, lanes] += jnp.dot(
                grad_scores, query, preferred_element_type=F32
            )

    @pl.loop(0, length // QB)
    def _(i):
        rows = pl.ds(pl.multiple_of(i * QB, QB), QB)
        cosine, sine = cos_ref[rows], sin_ref[rows]
        query, key = dq[rows] * HEAD**-0.5, dk[rows] * HEAD**-0.5
        out_ref[rows, :wide] = (query * cosine - swap_halves(query) * sine).astype(BF16)
        out_ref[rows, wide : 2 * wide] = (key * cosine - swap_halves(key) * sine).astype(BF16)
        out_ref[rows, 2 * wide :] = dv[rows].astype(BF16)


def attend_back(query, key, value, grad, lse, cosine, sine, start, heads):
    rows, _, length = start.shape
    wide = heads * HEAD

    def tall(width):
        return pl.BlockSpec((length, width), lambda r: (r, 0))

    return pl.pallas_call(
        functools.partial(attend_back_kernel, heads),
        grid=(rows,),
        out_shape=jax.ShapeDtypeStruct((rows * length, 3 * wide), BF16),
        in_specs=[tall(wide)] * 4
        + [pl.BlockSpec((1, heads, length), lambda r: (r, 0, 0)), tall(wide), tall(wide)]
        + [pl.BlockSpec((1, 1, length), lambda r: (r, 0, 0))],
        out_specs=tall(3 * wide),
        scratch_shapes=[pltpu.VMEM((length, wide), F32)] * 3,
        compiler_params=pltpu.CompilerParams(vmem_limit_bytes=48 << 20),
        name="attend_back",
    )(query, key, value, grad, lse, cosine, sine, start)


def norm_forward(value, gain):
    scale = lax.rsqrt(jnp.mean(value * value, axis=-1, keepdims=True) + EPS)
    return (value * scale * gain, scale)


def norm_backward(value, scale, gain, grad):
    scaled_grad = grad * gain
    inner = jnp.mean(value * scaled_grad, axis=-1, keepdims=True)
    back = scale * scaled_grad - value * scale * scale * scale * inner
    return (back, jnp.sum(grad * value * scale, axis=0))


def shards(
    z_size,
    t_size,
    tokens,
    gain_attn,
    gain_mlp,
    w_query,
    w_key,
    w_value,
    w_out,
    w_gate,
    w_up,
    w_down,
    segment_ids,
    out_grad,
):
    grp = Group(z_size, t_size)
    z = lax.axis_index("fsdp")
    low = z % 2

    def hop(value, mask):
        return lax.ppermute(value, "fsdp", [(i, i ^ mask) for i in range(z_size)])

    def half_of(value, which, axis):
        size = value.shape[axis] // 2
        return lax.dynamic_slice_in_dim(value, which * size, size, axis)

    def collect(sharded, half_axis, axis):
        mine = [half_of(w, low, half_axis) for w in sharded]
        other = [half_of(w, 1 - low, half_axis) for w in sharded]
        mine = mine[0] if len(mine) == 1 else jnp.concatenate(mine, axis=half_axis)
        other = other[0] if len(other) == 1 else jnp.concatenate(other, axis=half_axis)
        size = mine.shape[axis]
        shape = list(mine.shape)
        shape[axis] = size * z_size
        whole = jnp.zeros(shape, mine.dtype)
        for m in range(z_size):
            got = mine if m == 0 else hop(other if m % 2 else mine, m)
            whole = lax.dynamic_update_slice_in_dim(whole, got, (z ^ m) * size, axis)
        return whole

    def deliver(grad, half_axis, axis, parts):
        size = grad.shape[axis] // z_size
        sums = [None, None]
        for m in range(z_size):
            block = lax.dynamic_slice_in_dim(grad, (z ^ m) * size, size, axis)
            got = (block if m == 0 else hop(block, m)).astype(F32)
            sums[m % 2] = got if sums[m % 2] is None else sums[m % 2] + got
        outs = []
        piece = sums[0].shape[half_axis] // parts
        for i in range(parts):
            a, b = (lax.slice_in_dim(s, i * piece, (i + 1) * piece, axis=half_axis) for s in sums)
            outs.append(
                jnp.where(
                    low == 0,
                    jnp.concatenate([a, b], axis=half_axis),
                    jnp.concatenate([b, a], axis=half_axis),
                )
            )
        return outs

    wqkv = collect((w_query, w_key, w_value), 1, 0)
    wo = collect((w_out,), 0, 1)
    wgu = collect((w_gate, w_up), 1, 0)
    wd = collect((w_down,), 0, 1)
    wide = wqkv.shape[1] // 3
    heads = wide // HEAD
    units = wd.shape[0]

    other_ids = hop(segment_ids, 1)
    segments = jnp.where(
        low == 0,
        jnp.concatenate([segment_ids, other_ids], axis=0),
        jnp.concatenate([other_ids, segment_ids], axis=0),
    )
    rows, length = segments.shape
    start = jnp.sum(segments[:, :, None] > segments[:, None, :], axis=2, dtype=jnp.int32)
    position = (jnp.arange(length, dtype=jnp.int32)[None, :] - start).astype(F32)
    lane = jnp.arange(wide, dtype=jnp.int32)
    half = (lane % (HEAD // 2)).astype(F32)
    inverse = jnp.exp(half * (-2.0 / HEAD) * math.log(ROPE_BASE))
    angle = position.reshape(rows * length, 1) * inverse[None, :]
    cosine = jnp.cos(angle)
    sine = jnp.where(lane[None, :] % HEAD < HEAD // 2, -1.0, 1.0) * jnp.sin(angle)
    start = start.reshape(rows, 1, length)

    gain_a = gain_attn.astype(F32)
    gain_m = gain_mlp.astype(F32)
    x = tokens.astype(F32)
    normed_local, scale_a = norm_forward(x, gain_a)
    normed_a = gather(grp, normed_local.astype(BF16), 0, "gather_normed_a")
    grad_all = gather(grp, out_grad, 1, "gather_out_grad")
    qkv = jnp.dot(normed_a, wqkv, preferred_element_type=F32)
    query, key, value, attended, lse = attend(qkv, cosine, sine, start, heads)
    branch = jnp.dot(attended, wo, preferred_element_type=F32).astype(BF16)
    hidden = x + scatter(grp, branch, 2, "scatter_attn")
    normed_hidden, scale_m = norm_forward(hidden, gain_m)
    normed_m = gather(grp, normed_hidden.astype(BF16), 3, "gather_normed_m")
    gate_up = jnp.dot(normed_m, wgu, preferred_element_type=F32)
    gate, up = gate_up[:, :units], gate_up[:, units:]
    sigma = jax.nn.sigmoid(gate)
    silu_gate = gate * sigma
    act = (silu_gate * up).astype(BF16)
    grad_down = dot_tn(act, grad_all).astype(BF16)
    grad_act = dot_nt(grad_all, wd)
    grad_gate = (grad_act * up * (sigma * (1.0 + gate * (1.0 - sigma)))).astype(BF16)
    grad_up = (grad_act * silu_gate).astype(BF16)
    grad_gu = jnp.concatenate([grad_gate, grad_up], axis=1)
    grad_wgu = dot_tn(normed_m, grad_gu).astype(BF16)
    grad_nm = scatter(grp, dot_nt(grad_gu, wgu).astype(BF16), 4, "scatter_nm")
    back_m, gain_m_part = norm_backward(hidden, scale_m, gain_m, grad_nm)
    grad_hidden = out_grad.astype(F32) + back_m
    branch_all = gather(grp, grad_hidden.astype(BF16), 5, "gather_branch")
    out_part = jnp.dot(act, wd, preferred_element_type=F32).astype(BF16)
    output = hidden + scatter(grp, out_part, 6, "scatter_out")
    grad_wout = dot_tn(attended, branch_all).astype(BF16)
    grad_attended = dot_nt(branch_all, wo).astype(BF16)
    grad_qkv = attend_back(query, key, value, grad_attended, lse, cosine, sine, start, heads)
    grad_wqkv = dot_tn(normed_a, grad_qkv).astype(BF16)
    grad_na = scatter(grp, dot_nt(grad_qkv, wqkv).astype(BF16), 7, "scatter_na")
    back_a, gain_a_part = norm_backward(x, scale_a, gain_a, grad_na)
    tokens_grad = (grad_hidden + back_a).astype(BF16)
    gains = sum_all(z_size, t_size, jnp.stack([gain_a_part, gain_m_part]), 8)
    (down_out,) = deliver(grad_down, 0, 1, 1)
    gate_out, up_out = deliver(grad_wgu, 1, 0, 2)
    (out_out,) = deliver(grad_wout, 0, 1, 1)
    query_out, key_out, value_out = deliver(grad_wqkv, 1, 0, 3)
    return (
        output.astype(BF16),
        tokens_grad,
        gains[0],
        gains[1],
        query_out,
        key_out,
        value_out,
        out_out,
        gate_out,
        up_out,
        down_out,
    )


def solution(mesh):
    return jax.shard_map(
        functools.partial(shards, mesh.shape["fsdp"], mesh.shape["tensor"]),
        mesh=mesh,
        in_specs=(
            P(("fsdp", "tensor"), None),
            P(),
            P(),
            P("fsdp", "tensor"),
            P("fsdp", "tensor"),
            P("fsdp", "tensor"),
            P("tensor", "fsdp"),
            P("fsdp", "tensor"),
            P("fsdp", "tensor"),
            P("tensor", "fsdp"),
            P("fsdp", None),
            P(("fsdp", "tensor"), None),
        ),
        out_specs=(
            P(("fsdp", "tensor"), None),
            P(("fsdp", "tensor"), None),
            P(),
            P(),
            P("fsdp", "tensor"),
            P("fsdp", "tensor"),
            P("fsdp", "tensor"),
            P("tensor", "fsdp"),
            P("fsdp", "tensor"),
            P("fsdp", "tensor"),
            P("tensor", "fsdp"),
        ),
        check_vma=False,
    )
```

time: 1240 us -> 878 us (0.71)
  waiting for transfers between devices: 882 us -> 123 us
  Pallas kernels: 0 us -> 490 us
  matrix products: 220 us -> 129 us
  starting transfers between devices: 1.68 us -> 50.1 us
  local copies, waits for them, and re-layouts: 0.97 us -> 42.9 us
  blocking collectives: 39.7 us -> 0 us
  other arithmetic: 70.8 us -> 33.9 us
  between operations: 15 us -> 1.83 us
    pallas_call x0 -> x11, Pallas kernels: none -> 490 us  [the longest x4 240 us: scatter(): pl.pallas_call(functools.partial(scatter_kernel, grp, rows), out_shape=ja...]
    reduce_scatter x11 -> x0, waiting for transfers between devices: 460 us -> none  [the longest x1 81.7 us: shards(): lax.psum_scatter(dot_nt(grad_gate, wg) + dot_nt(grad_up, wu), 'tensor', s...]
    all_gather x11 -> x0, waiting for transfers between devices: 416 us -> none  [the longest x1 75 us: shards(): lax.all_gather(local[5], 'fsdp', axis=0, tiled=True)]
    ppermute x0 -> x25, waiting for transfers between devices: none -> 123 us  [hop(): return lax.ppermute(value, 'fsdp', [(i, i ^ mask) for i in range(z_size)])]
    dot_general x13 -> x4, matrix products: 116 us -> 41.9 us  [the longest x1 17.7 us: shards(): gate_up = jnp.dot(normed_m, wgu, preferred_element_type=F32)]
    ppermute x0 -> x25, starting transfers between devices: none -> 50.1 us  [hop(): return lax.ppermute(value, 'fsdp', [(i, i ^ mask) for i in range(z_size)])]
    convert_element_type x15 -> x7, other arithmetic: 47.9 us -> 7.28 us  [the longest x1 3.88 us: shards(): tokens_grad = (grad_hidden + back_a).astype(BF16)]
    psum x1 -> x0, blocking collectives: 39.7 us -> none  [shards(): lax.psum((gain_a_part, gain_m_part), ('fsdp', 'tensor'))]
  transfers between devices with their start and end apart: 22 -> 25, of which waited for: 21 -> 6; matrix products, arithmetic and copies ran while one was open for 20% -> 8% of each run, Pallas kernels for 0% -> 42%
where the time goes in v1:
time: 878 us; the launch traced here: 870 us
  Pallas kernels  490 us (56%)
  matrix products  129 us (15%)
  waiting for transfers between devices  123 us (14%)
  starting transfers between devices  50.1 us (6%)
  local copies, waits for them, and re-layouts  42.9 us (5%)
  other arithmetic  33.9 us (4%)
    pallas_call x4, Pallas kernels, scatter(): pl.pallas_call(functools.partial(scatter_kernel, grp, rows), out_shape=ja...  240 us
    pallas_call x4, Pallas kernels, gather(): pl.pallas_call(functools.partial(gather_kernel, grp), out_shape=jax.Shape...  205 us
    ppermute x25, waiting for transfers between devices, hop(): return lax.ppermute(value, 'fsdp', [(i, i ^ mask) for i in range(z_size)])  123 us
    ppermute x25, starting transfers between devices, hop(): return lax.ppermute(value, 'fsdp', [(i, i ^ mask) for i in range(z_size)])  50.1 us
    dot_general x4, matrix products, dot_nt(): lax.dot_general(left, right, (((1,), (1,)), ((), ())), preferred_element_...  43.5 us
    dot_general x4, matrix products, dot_tn(): lax.dot_general(left, right, (((0,), (0,)), ((), ())), preferred_element_...  43.3 us
    pallas_call x1, Pallas kernels, attend_back(): pl.pallas_call(functools.partial(attend_back_kernel, heads), grid=(rows,)...  19 us
    dot_general x1, matrix products, shards(): gate_up = jnp.dot(normed_m, wgu, preferred_element_type=F32)  17.7 us
  transfers between devices with their start and end apart: 25, of which 6 were waited for; matrix products, arithmetic and copies ran while one was open for 8% of the time, Pallas kernels for 42%

profile of v1, /device:TPU:8, one launch (start us, length us, event | category | flops | bytes accessed | tf_op | source)
XLA Modules:
  0.0 870.1 jit_solution(8201266288957474687)
XLA Ops:
  0.8 1.8 constant_dynamic-update-slice_fusion.11
  2.5 1.6 collective-permute-start.6
  4.1 2.5 collective-permute-start.4
  17.2 2.6 broadcast_in_dim.20
  19.8 1.6 pad_maximum_fusion.3
  23.6 51.0 %gather_normed_a.1 = bf16[2560,2048]{1,0:T(8,128)(2,1)} custom-call(bf16[160,2048]{1,0:T(8,128)(2,1)} %fusion.6.x_ref), custom_call_target="tpu_custom_call" | custom-call | tf_op jit(solution)/shard_map/gather_normed_a/pallas_call | solution.py:164
  74.6 52.0 %gather_out_grad.1 = bf16[2560,2048]{1,0:T(8,128)(2,1)} custom-call(bf16[160,2048]{1,0:T(8,128)(2,1)} %x_ref.1), custom_call_target="tpu_custom_call" | custom-call | tf_op jit(solution)/shard_map/gather_out_grad/pallas_call | solution.py:164
  126.7 2.8 collective-permute-start.5
  129.5 1.7 convert_reduce_fusion
  131.3 4.6 fusion.12
  136.3 2.0 collective-permute-start.12
  138.3 2.5 collective-permute-start.10
  141.0 1.8 constant_dynamic-update-slice_fusion.14
  142.8 22.9 %collective-permute-done.1 = bf16[512,384]{1,0:T(8,128)(2,1)S(1)} collective-permute-done((bf16[512,384]{1,0:T(8,128)(2,1)}, bf16[512,384]{1,0:T(8,128)(2,1)S(1)}, u32[]{:S(2)}, u32[]{:S(2)}) %collective-permute-start.1) | collective-permute-done | bytes 393248 | tf_op jit(solution)/shard_map/ppermute | solution.py:547
  165.7 3.8 collective-permute-start.7
  171.1 10.3 %fusion.28.qkv_ref = f32[2560,384]{1,0:T(8,128)} fusion(bf16[2560,2048]{1,0:T(8,128)(2,1)} %gather_normed_a.1, bf16[2048,384]{1,0:T(8,128)(2,1)} %constant_dynamic-update-slice_fusion.12), kind=kOutput, calls=%fused_computation.127 | convolution fusion | flops 4026531840 | bytes 15990784 | tf_op jit(solution)/shard_map/dot_general | solution.py:618
  181.3 10.6 %attend.1 = (bf16[2560,128]{1,0:T(8,128)(2,1)S(1)}, bf16[2560,128]{1,0:T(8,128)(2,1)S(1)}, bf16[2560,128]{1,0:T(8,128)(2,1)S(1)}, bf16[2560,128]{1,0:T(8,128)(2,1)S(1)}, f32[2,2,1280]{2,1,0:T(2,128)S(1)}) custom-call(f32[2560,384]{1,0:T(8,128)} %fusion.28.qkv_ref, f32[2560,128]{1,0:T(8,128)S(1)} %get-tuple-element.99.cos_ref, ...), custom_call_target="tpu_custom_call" | custom-call | tf_op jit(solution)/shard_map/attend/pallas_call | solution.py:442
  192.0 5.5 convolution_convert_fusion.3.p_ref
  197.4 60.8 %scatter_attn.1 = f32[160,2048]{1,0:T(8,128)S(1)} custom-call(bf16[2560,2048]{1,0:T(8,128)(2,1)} %convolution_convert_fusion.3.p_ref), custom_call_target="tpu_custom_call" | custom-call | tf_op jit(solution)/shard_map/scatter_attn/pallas_call | solution.py:309
  259.2 13.3 %collective-permute-start.11 = (bf16[512,512]{1,0:T(8,128)(2,1)S(1)}, bf16[512,512]{1,0:T(8,128)(2,1)S(1)}, u32[]{:S(2)}, u32[]{:S(2)}) collective-permute-start(bf16[512,512]{1,0:T(8,128)(2,1)S(1)} %copy-done.28), channel_id=1, source_target_pairs={{0,16},{8,24},{16,0},{24,8},{1,17},{9,25},{17,1},{25,9},{2,18},{10... | collective-permute-start | bytes 1572872 | tf_op jit(solution)/shard_map/ppermute | solution.py:547
  273.6 51.5 %gather_normed_m.1 = bf16[2560,2048]{1,0:T(8,128)(2,1)} custom-call(bf16[160,2048]{1,0:T(8,128)(2,1)} %multiply_convert_fusion.1.x_ref), custom_call_target="tpu_custom_call" | custom-call | tf_op jit(solution)/shard_map/gather_normed_m/pallas_call | solution.py:164
  325.1 1.9 constant_dynamic-update-slice_fusion.2
  327.8 1.9 constant_dynamic-update-slice_fusion
  329.7 2.3 constant_dynamic-update-slice_fusion.6
  332.0 2.3 constant_dynamic-update-slice_fusion.5
  334.3 2.3 constant_dynamic-update-slice_fusion.4
  336.5 17.7 %fusion.29 = f32[2560,1024]{0,1:T(8,128)} fusion(bf16[2560,2048]{1,0:T(8,128)(2,1)} %gather_normed_m.1, bf16[2048,1024]{1,0:T(8,128)(2,1)} %constant_dynamic-update-slice_fusion.4), kind=kOutput, calls=%fused_computation.128 | convolution fusion | flops 10737418240 | bytes 25165824 | tf_op jit(solution)/shard_map/dot_general | solution.py:624
  354.3 14.1 %fusion.1 = (bf16[2560,512]{0,1:T(8,128)(2,1)S(1)}, bf16[2560,512]{0,1:T(8,128)(2,1)}, bf16[2560,512]{0,1:T(8,128)(2,1)S(1)}) fusion(f32[2560,1024]{0,1:T(8,128)} %fusion.29, bf16[512,2048]{1,0:T(8,128)(2,1)S(1)} %copy-done.21, bf16[2560,2048]{1,0:T(8,128)(2,1)} %gather_out_grad.1), kind=kOutput, calls=%fused_computation.9 | convolution fusion | flops 5388369920 | bytes 30932992 | tf_op jit(solution)/shard_map/dot_general | solution.py:27
  368.4 16.3 %convolution_convert_fusion.4 = bf16[2048,1024]{0,1:T(8,128)(2,1)} fusion(bf16[2560,2048]{1,0:T(8,128)(2,1)} %gather_normed_m.1, bf16[2560,512]{0,1:T(8,128)(2,1)} %get-tuple-element.54, bf16[2560,512]{0,1:T(8,128)(2,1)S(1)} %get-tuple-element.53), kind=kOutput, calls=%fused_computation.14 | convolution fusion | flops 10750001152 | bytes 19922944 | tf_op jit(solution)/shard_map/dot_general | solution.py:31
  384.7 16.4 %convolution_convert_fusion.1.p_ref = bf16[2560,2048]{1,0:T(8,128)(2,1)} fusion(bf16[2048,1024]{1,0:T(8,128)(2,1)} %constant_dynamic-update-slice_fusion.4, bf16[2560,512]{0,1:T(8,128)(2,1)} %get-tuple-element.54, bf16[2560,512]{0,1:T(8,128)(2,1)S(1)} %get-tuple-element.53), kind=kOutput, calls=%fused_computation.2 | convolution fusion | flops 10753146880 | bytes 19922944 | tf_op jit(solution)/shard_map/dot_general | solution.py:27
  401.1 11.1 %convolution_convert_fusion.6 = bf16[512,2048]{1,0:T(8,128)(2,1)} fusion(bf16[2560,512]{0,1:T(8,128)(2,1)S(1)} %get-tuple-element.55, bf16[2560,2048]{1,0:T(8,128)(2,1)} %gather_out_grad.1), kind=kOutput, calls=%fused_computation.16 | convolution fusion | flops 5369757696 | bytes 15204352 | tf_op jit(solution)/shard_map/dot_general | solution.py:31
  412.2 8.4 convolution_convert_fusion.2.p_ref
  420.6 58.9 %scatter_nm.1 = f32[160,2048]{1,0:T(8,128)S(1)} custom-call(bf16[2560,2048]{1,0:T(8,128)(2,1)} %convolution_convert_fusion.1.p_ref), custom_call_target="tpu_custom_call" | custom-call | tf_op jit(solution)/shard_map/scatter_nm/pallas_call | solution.py:309
  481.9 50.6 %gather_branch.1 = bf16[2560,2048]{1,0:T(8,128)(2,1)} custom-call(bf16[160,2048]{1,0:T(8,128)(2,1)} %fusion.22.x_ref), custom_call_target="tpu_custom_call" | custom-call | tf_op jit(solution)/shard_map/gather_branch/pallas_call | solution.py:164
  532.6 5.7 convolution_convert_fusion.8
  539.6 2.9 convolution_convert_fusion.5.do_ref
  542.5 19.0 %attend_back.1 = bf16[2560,384]{1,0:T(8,128)(2,1)} custom-call(bf16[2560,128]{1,0:T(8,128)(2,1)S(1)} %copy-done.4, bf16[2560,128]{1,0:T(8,128)(2,1)S(1)} %copy-done.6, bf16[2560,128]{1,0:T(8,128)(2,1)S(1)} %copy-done.8, bf16[2560,128]{1,0:T(8,128)(2,1)S(1)} %convolution_convert_fusion.5.do_ref, f32[2,2,1280]{2,1,0:T(2,128)S(1)} %get-tuple-element.20.lse_ref, ...), custom_call_target="tpu_custom_call" | custom-call | tf_op jit(solution)/shard_map/attend_back/pallas_call | solution.py:500
  561.5 10.2 %convolution_convert_fusion.7 = bf16[2048,384]{0,1:T(8,128)(2,1)} fusion(bf16[2560,2048]{1,0:T(8,128)(2,1)} %gather_normed_a.1, bf16[2560,384]{1,0:T(8,128)(2,1)} %attend_back.1), kind=kOutput, calls=%fused_computation.17 | convolution fusion | flops 4027318272 | bytes 14024704 | tf_op jit(solution)/shard_map/dot_general | solution.py:31
  571.7 10.1 %convolution_convert_fusion.p_ref = bf16[2560,2048]{1,0:T(8,128)(2,1)} fusion(bf16[2560,384]{1,0:T(8,128)(2,1)S(1)} %copy-done.22, bf16[2048,384]{1,0:T(8,128)(2,1)} %constant_dynamic-update-slice_fusion.12), kind=kOutput, calls=%fused_computation.1 | convolution fusion | flops 4031774720 | bytes 14024704 | tf_op jit(solution)/shard_map/dot_general | solution.py:27
  583.0 3.3 collective-permute-start.24
  586.3 1.9 constant_dynamic-slice_fusion.5
  588.2 60.2 %scatter_out.1 = f32[160,2048]{1,0:T(8,128)S(1)} custom-call(bf16[2560,2048]{1,0:T(8,128)(2,1)} %convolution_convert_fusion.2.p_ref), custom_call_target="tpu_custom_call" | custom-call | tf_op jit(solution)/shard_map/scatter_out/pallas_call | solution.py:309
  649.3 3.4 collective-permute-start.18
  653.7 60.4 %scatter_na.1 = f32[160,2048]{1,0:T(8,128)S(1)} custom-call(bf16[2560,2048]{1,0:T(8,128)(2,1)} %convolution_convert_fusion.p_ref), custom_call_target="tpu_custom_call" | custom-call | tf_op jit(solution)/shard_map/scatter_na/pallas_call | solution.py:309
  715.2 14.9 %sum_all.1 = f32[2,2048]{1,0:T(2,128)} custom-call(f32[2,2048]{1,0:T(2,128)} %pad_maximum_fusion.7.x_ref), custom_call_target="tpu_custom_call" | custom-call | tf_op jit(solution)/shard_map/sum_all/pallas_call | solution.py:357
  730.1 1.4 fusion.27
  731.5 3.9 fusion.11
  735.6 1.6 collective-permute-start.13
  738.7 1.5 collective-permute-start.15
  742.0 10.0 %collective-permute-done.13 = bf16[512,384]{0,1:T(8,128)(2,1)S(1)} collective-permute-done((bf16[512,384]{0,1:T(8,128)(2,1)S(1)}, bf16[512,384]{0,1:T(8,128)(2,1)S(1)}, u32[]{:S(2)}, u32[]{:S(2)}) %collective-permute-start.13) | collective-permute-done | bytes 393248 | tf_op jit(solution)/shard_map/ppermute | solution.py:547
  752.0 3.9 collective-permute-start.14
  756.0 13.6 %collective-permute-done.15 = bf16[512,384]{0,1:T(8,128)(2,1)S(1)} collective-permute-done((bf16[512,384]{0,1:T(8,128)(2,1)S(1)}, bf16[512,384]{0,1:T(8,128)(2,1)S(1)}, u32[]{:S(2)}, u32[]{:S(2)}) %collective-permute-start.15) | collective-permute-done | bytes 393248 | tf_op jit(solution)/shard_map/ppermute | solution.py:547
  769.7 4.3 collective-permute-done.14
  779.7 3.4 collective-permute-start.20
  783.0 1.3 convert_add_fusion.4
  784.4 1.3 convert_add_fusion.3
  785.8 1.6 maximum_select_fusion.2
  787.3 50.9 %collective-permute-done.19 = bf16[512,1024]{0,1:T(8,128)(2,1)S(1)} collective-permute-done((bf16[512,1024]{0,1:T(8,128)(2,1)S(1)}, bf16[512,1024]{0,1:T(8,128)(2,1)S(1)}, u32[]{:S(2)}, u32[]{:S(2)}) %collective-permute-start.19) | collective-permute-done | bytes 1048608 | tf_op jit(solution)/shard_map/ppermute | solution.py:547
  838.3 1.5 convert_add_fusion.2
  840.0 21.0 %collective-permute-done.21 = bf16[512,1024]{0,1:T(8,128)(2,1)} collective-permute-done((bf16[512,1024]{0,1:T(8,128)(2,1)}, bf16[512,1024]{0,1:T(8,128)(2,1)}, u32[]{:S(2)}, u32[]{:S(2)}) %collective-permute-start.21) | collective-permute-done | bytes 1048608 | tf_op jit(solution)/shard_map/ppermute | solution.py:547
  861.0 1.5 convert_add_fusion.1
  864.0 1.8 copy.32
  865.8 2.0 maximum_select_fusion
  867.8 1.8 copy.31
  (157 shorter events, 36.6 us)
Async XLA Ops:
  0.6 9.8 %copy-start.33 = (s32[1,1280]{1,0:T(1,128)S(1)}, s32[1,1280]{1,0:T(1,128)}, u32[]{:S(2)}) copy-start(s32[1,1280]{1,0:T(1,128)} %param.22) | copy-start | bytes 15364
  0.7 10.9 %copy-start.12 = (bf16[160,2048]{1,0:T(8,128)(2,1)S(1)}, bf16[160,2048]{1,0:T(8,128)(2,1)}, u32[]{:S(2)}) copy-start(bf16[160,2048]{1,0:T(8,128)(2,1)} %param.12) | copy-start | bytes 1966084
  0.7 11.1 %copy-start.34 = (bf16[2048]{0:T(1024)(128)(2,1)S(1)}, bf16[2048]{0:T(1024)(128)(2,1)}, u32[]{:S(2)}) copy-start(bf16[2048]{0:T(1024)(128)(2,1)} %param.13) | copy-start | bytes 12292
  2.5 135.8 %collective-permute-start.6 = (bf16[128,512]{1,0:T(8,128)(2,1)}, bf16[128,512]{1,0:T(8,128)(2,1)S(1)}, u32[]{:S(2)}, u32[]{:S(2)}) collective-permute-start(bf16[128,512]{1,0:T(8,128)(2,1)} %get-tuple-element.89), channel_id=1, source_target_pairs={{0,24},{8,16},{16,8},{24,0},{1,25},{9,17},{17,9},{25,1},{2,26},{10... | collective-permute-start | bytes 393224 | tf_op jit(solution)/shard_map/ppermute | solution.py:547
  4.1 131.9 %collective-permute-start.4 = (bf16[128,512]{1,0:T(8,128)(2,1)}, bf16[128,512]{1,0:T(8,128)(2,1)S(1)}, u32[]{:S(2)}, u32[]{:S(2)}) collective-permute-start(bf16[128,512]{1,0:T(8,128)(2,1)} %get-tuple-element.89), channel_id=1, source_target_pairs={{0,8},{8,0},{16,24},{24,16},{1,9},{9,1},{17,25},{25,17},{2,10},{10... | collective-permute-start | bytes 393224 | tf_op jit(solution)/shard_map/ppermute | solution.py:547
  9.5 3.6 copy-start.26
  9.5 160.8 %collective-permute-start.2 = (bf16[512,384]{1,0:T(8,128)(2,1)}, bf16[512,384]{1,0:T(8,128)(2,1)S(1)}, u32[]{:S(2)}, u32[]{:S(2)}) collective-permute-start(bf16[512,384]{1,0:T(8,128)(2,1)} %pad_maximum_fusion.6), channel_id=1, source_target_pairs={{0,24},{8,16},{16,8},{24,0},{1,25},{9,17},{17,9},{25,1},{2,26},{10... | collective-permute-start | bytes 1179656 | tf_op jit(solution)/shard_map/ppermute | solution.py:547
  9.5 131.3 %collective-permute-start = (bf16[512,384]{1,0:T(8,128)(2,1)}, bf16[512,384]{1,0:T(8,128)(2,1)}, u32[]{:S(2)}, u32[]{:S(2)}) collective-permute-start(bf16[512,384]{1,0:T(8,128)(2,1)} %pad_maximum_fusion.6), channel_id=1, source_target_pairs={{0,8},{8,0},{16,24},{24,16},{1,9},{9,1},{17,25},{25,17},{2,10},{10... | collective-permute-start | bytes 1179656 | tf_op jit(solution)/shard_map/ppermute | solution.py:547
  10.4 116.3 %collective-permute-start.3 = (s32[1,1280]{1,0:T(1,128)S(1)}, s32[1,1280]{1,0:T(1,128)S(1)}, u32[]{:S(2)}, u32[]{:S(2)}) collective-permute-start(s32[1,1280]{1,0:T(1,128)S(1)} %copy-done.33), channel_id=1, source_target_pairs={{0,8},{8,0},{16,24},{24,16},{1,9},{9,1},{17,25},{25,17},{2,10},{10... | collective-permute-start | bytes 15368 | tf_op jit(solution)/shard_map/ppermute | solution.py:547
  11.8 2.5 copy-start.31
  11.8 2.5 copy-start.29
  12.9 1.4 copy-start.24
  12.9 1.9 copy-start.25
  14.8 1.3 copy-start.20
  21.4 2.2 copy-start.35
  126.7 9.5 %collective-permute-start.5 = (bf16[128,512]{1,0:T(8,128)(2,1)}, bf16[128,512]{1,0:T(8,128)(2,1)S(1)}, u32[]{:S(2)}, u32[]{:S(2)}) collective-permute-start(bf16[128,512]{1,0:T(8,128)(2,1)} %get-tuple-element.52), channel_id=1, source_target_pairs={{0,16},{8,24},{16,0},{24,8},{1,17},{9,25},{17,1},{25,9},{2,18},{10... | collective-permute-start | bytes 393224 | tf_op jit(solution)/shard_map/ppermute | solution.py:547
  135.9 45.4 %copy-start = (f32[2560,128]{1,0:T(8,128)}, f32[2560,128]{1,0:T(8,128)S(1)}, u32[]{:S(2)}) copy-start(f32[2560,128]{1,0:T(8,128)S(1)} %get-tuple-element.99.cos_ref) | copy-start | bytes 3932164
  136.0 29.7 %collective-permute-start.1 = (bf16[512,384]{1,0:T(8,128)(2,1)}, bf16[512,384]{1,0:T(8,128)(2,1)S(1)}, u32[]{:S(2)}, u32[]{:S(2)}) collective-permute-start(bf16[512,384]{1,0:T(8,128)(2,1)} %get-tuple-element.87), channel_id=1, source_target_pairs={{0,16},{8,24},{16,0},{24,8},{1,17},{9,25},{17,1},{25,9},{2,18},{10... | collective-permute-start | bytes 1179656 | tf_op jit(solution)/shard_map/ppermute | solution.py:547
  136.3 191.6 %collective-permute-start.12 = (bf16[512,512]{1,0:T(8,128)(2,1)}, bf16[512,512]{1,0:T(8,128)(2,1)}, u32[]{:S(2)}, u32[]{:S(2)}) collective-permute-start(bf16[512,512]{1,0:T(8,128)(2,1)} %get-tuple-element.71), channel_id=1, source_target_pairs={{0,24},{8,16},{16,8},{24,0},{1,25},{9,17},{17,9},{25,1},{2,26},{10... | collective-permute-start | bytes 1572872 | tf_op jit(solution)/shard_map/ppermute | solution.py:547
  138.3 120.2 %collective-permute-start.10 = (bf16[512,512]{1,0:T(8,128)(2,1)}, bf16[512,512]{1,0:T(8,128)(2,1)}, u32[]{:S(2)}, u32[]{:S(2)}) collective-permute-start(bf16[512,512]{1,0:T(8,128)(2,1)} %get-tuple-element.71), channel_id=1, source_target_pairs={{0,8},{8,0},{16,24},{24,16},{1,9},{9,1},{17,25},{25,17},{2,10},{10... | collective-permute-start | bytes 1572872 | tf_op jit(solution)/shard_map/ppermute | solution.py:547
  140.8 51.1 %copy-start.18 = (bf16[128,2048]{1,0:T(8,128)(2,1)}, bf16[128,2048]{1,0:T(8,128)(2,1)S(1)}, u32[]{:S(2)}) copy-start(bf16[128,2048]{1,0:T(8,128)(2,1)S(1)} %constant_dynamic-update-slice_fusion.8) | copy-start | bytes 1572868
  140.9 193.4 %collective-permute-start.9 = (bf16[512,1024]{1,0:T(8,128)(2,1)}, bf16[512,1024]{1,0:T(8,128)(2,1)}, u32[]{:S(2)}, u32[]{:S(2)}) collective-permute-start(bf16[512,1024]{1,0:T(8,128)(2,1)} %pad_maximum_fusion.4), channel_id=1, source_target_pairs={{0,24},{8,16},{16,8},{24,0},{1,25},{9,17},{17,9},{25,1},{2,26},{10... | collective-permute-start | bytes 3145736 | tf_op jit(solution)/shard_map/ppermute | solution.py:547
  165.7 164.0 %collective-permute-start.7 = (bf16[512,1024]{1,0:T(8,128)(2,1)}, bf16[512,1024]{1,0:T(8,128)(2,1)}, u32[]{:S(2)}, u32[]{:S(2)}) collective-permute-start(bf16[512,1024]{1,0:T(8,128)(2,1)} %pad_maximum_fusion.4), channel_id=1, source_target_pairs={{0,8},{8,0},{16,24},{24,16},{1,9},{9,1},{17,25},{25,17},{2,10},{10... | collective-permute-start | bytes 3145736 | tf_op jit(solution)/shard_map/ppermute | solution.py:547
  170.3 161.7 %collective-permute-start.8 = (bf16[512,1024]{1,0:T(8,128)(2,1)}, bf16[512,1024]{1,0:T(8,128)(2,1)}, u32[]{:S(2)}, u32[]{:S(2)}) collective-permute-start(bf16[512,1024]{1,0:T(8,128)(2,1)} %get-tuple-element.72), channel_id=1, source_target_pairs={{0,16},{8,24},{16,0},{24,8},{1,17},{9,25},{17,1},{25,9},{2,18},{10... | collective-permute-start | bytes 3145736 | tf_op jit(solution)/shard_map/ppermute | solution.py:547
  191.9 5.5 copy-start.3
  191.9 5.5 copy-start.5
  191.9 5.5 copy-start.7
  258.2 1.0 copy-start.28
  258.5 14.1 %copy-start.10 = (f32[160,2048]{1,0:T(8,128)}, f32[160,2048]{1,0:T(8,128)S(1)}, u32[]{:S(2)}) copy-start(f32[160,2048]{1,0:T(8,128)S(1)} %get-tuple-element.50) | copy-start | bytes 3932164
  259.2 67.7 %collective-permute-start.11 = (bf16[512,512]{1,0:T(8,128)(2,1)S(1)}, bf16[512,512]{1,0:T(8,128)(2,1)S(1)}, u32[]{:S(2)}, u32[]{:S(2)}) collective-permute-start(bf16[512,512]{1,0:T(8,128)(2,1)S(1)} %copy-done.28), channel_id=1, source_target_pairs={{0,16},{8,24},{16,0},{24,8},{1,17},{9,25},{17,1},{25,9},{2,18},{10... | collective-permute-start | bytes 1572872 | tf_op jit(solution)/shard_map/ppermute | solution.py:547
  336.5 17.7 %copy-start.21 = (bf16[512,2048]{1,0:T(8,128)(2,1)S(1)}, bf16[512,2048]{1,0:T(8,128)(2,1)}, u32[]{:S(2)}) copy-start(bf16[512,2048]{1,0:T(8,128)(2,1)} %constant_dynamic-update-slice_fusion) | copy-start | bytes 6291460
  420.6 58.9 %copy-start.11 = (f32[160,2048]{1,0:T(8,128)S(1)}, f32[160,2048]{1,0:T(8,128)}, u32[]{:S(2)}) copy-start(f32[160,2048]{1,0:T(8,128)} %copy-done.10) | copy-start | bytes 3932164
  479.5 1.1 copy-start.14
  532.6 7.0 copy-start.9
  532.6 7.0 copy-start.19
  539.6 108.9 %copy-start.17 = (bf16[128,2048]{1,0:T(8,128)(2,1)}, bf16[128,2048]{1,0:T(8,128)(2,1)S(1)}, u32[]{:S(2)}) copy-start(bf16[128,2048]{1,0:T(8,128)(2,1)S(1)} %convolution_convert_fusion.8) | copy-start | bytes 1572868
  539.6 2.9 copy-start.1
  539.6 2.9 copy-start.4
  539.6 2.9 copy-start.6
  539.6 3.0 copy-start.8
  561.5 10.2 %copy-start.22 = (bf16[2560,384]{1,0:T(8,128)(2,1)S(1)}, bf16[2560,384]{1,0:T(8,128)(2,1)}, u32[]{:S(2)}) copy-start(bf16[2560,384]{1,0:T(8,128)(2,1)} %attend_back.1) | copy-start | bytes 5898244
  571.7 10.1 %copy-start.16 = (bf16[512,2048]{1,0:T(8,128)(2,1)S(1)}, bf16[512,2048]{1,0:T(8,128)(2,1)}, u32[]{:S(2)}) copy-start(bf16[512,2048]{1,0:T(8,128)(2,1)} %convolution_convert_fusion.6) | copy-start | bytes 6291460
  571.7 14.6 %copy-start.15 = (bf16[2048,1024]{0,1:T(8,128)(2,1)S(1)}, bf16[2048,1024]{0,1:T(8,128)(2,1)}, u32[]{:S(2)}) copy-start(bf16[2048,1024]{0,1:T(8,128)(2,1)} %convolution_convert_fusion.4) | copy-start | bytes 12582916
  583.0 196.6 %collective-permute-start.22 = (bf16[512,512]{1,0:T(8,128)(2,1)}, bf16[512,512]{1,0:T(8,128)(2,1)}, u32[]{:S(2)}, u32[]{:S(2)}) collective-permute-start(bf16[512,512]{1,0:T(8,128)(2,1)} %get-tuple-element.59), channel_id=1, source_target_pairs={{0,16},{8,24},{16,0},{24,8},{1,17},{9,25},{17,1},{25,9},{2,18},{10... | collective-permute-start | bytes 1572872 | tf_op jit(solution)/shard_map/ppermute | solution.py:547
  583.0 201.4 %collective-permute-start.24 = (bf16[512,512]{1,0:T(8,128)(2,1)}, bf16[512,512]{1,0:T(8,128)(2,1)}, u32[]{:S(2)}, u32[]{:S(2)}) collective-permute-start(bf16[512,512]{1,0:T(8,128)(2,1)} %get-tuple-element.60), channel_id=1, source_target_pairs={{0,24},{8,16},{16,8},{24,0},{1,25},{9,17},{17,9},{25,1},{2,26},{10... | collective-permute-start | bytes 1572872 | tf_op jit(solution)/shard_map/ppermute | solution.py:547
  648.5 65.7 %copy-start.2 = (f32[160,2048]{1,0:T(8,128)}, f32[160,2048]{1,0:T(8,128)S(1)}, u32[]{:S(2)}) copy-start(f32[160,2048]{1,0:T(8,128)S(1)} %scatter_out.1) | copy-start | bytes 3932164
  649.3 86.3 %collective-permute-start.16 = (bf16[128,512]{1,0:T(8,128)(2,1)}, bf16[128,512]{1,0:T(8,128)(2,1)S(1)}, u32[]{:S(2)}, u32[]{:S(2)}) collective-permute-start(bf16[128,512]{1,0:T(8,128)(2,1)} %get-tuple-element.84), channel_id=1, source_target_pairs={{0,16},{8,24},{16,0},{24,8},{1,17},{9,25},{17,1},{25,9},{2,18},{10... | collective-permute-start | bytes 393224 | tf_op jit(solution)/shard_map/ppermute | solution.py:547
  649.3 88.8 %collective-permute-start.18 = (bf16[128,512]{1,0:T(8,128)(2,1)}, bf16[128,512]{1,0:T(8,128)(2,1)}, u32[]{:S(2)}, u32[]{:S(2)}) collective-permute-start(bf16[128,512]{1,0:T(8,128)(2,1)} %get-tuple-element.85), channel_id=1, source_target_pairs={{0,24},{8,16},{16,8},{24,0},{1,25},{9,17},{17,9},{25,1},{2,26},{10... | collective-permute-start | bytes 393224 | tf_op jit(solution)/shard_map/ppermute | solution.py:547
  652.7 61.4 %copy-start.13 = (bf16[160,2048]{1,0:T(8,128)(2,1)S(1)}, bf16[160,2048]{1,0:T(8,128)(2,1)}, u32[]{:S(2)}) copy-start(bf16[160,2048]{1,0:T(8,128)(2,1)} %param.12) | copy-start | bytes 1966084
  652.7 61.4 %copy-start.30 = (f32[2048]{0:T(1024)S(1)}, f32[2048]{0:T(1024)}, u32[]{:S(2)}) copy-start(f32[2048]{0:T(1024)} %copy-done.29) | copy-start | bytes 24580
  652.7 61.4 %copy-start.32 = (f32[160]{0:T(256)S(1)}, f32[160]{0:T(256)}, u32[]{:S(2)}) copy-start(f32[160]{0:T(256)} %copy-done.31) | copy-start | bytes 1924
  652.7 85.9 %collective-permute-start.17 = (bf16[128,512]{1,0:T(8,128)(2,1)}, bf16[128,512]{1,0:T(8,128)(2,1)}, u32[]{:S(2)}, u32[]{:S(2)}) collective-permute-start(bf16[128,512]{1,0:T(8,128)(2,1)} %get-tuple-element.86), channel_id=1, source_target_pairs={{0,8},{8,0},{16,24},{24,16},{1,9},{9,1},{17,25},{25,17},{2,10},{10... | collective-permute-start | bytes 393224 | tf_op jit(solution)/shard_map/ppermute | solution.py:547
  731.5 3.9 copy-start.23
  735.6 16.4 %collective-permute-start.13 = (bf16[512,384]{0,1:T(8,128)(2,1)S(1)}, bf16[512,384]{0,1:T(8,128)(2,1)S(1)}, u32[]{:S(2)}, u32[]{:S(2)}) collective-permute-start(bf16[512,384]{0,1:T(8,128)(2,1)S(1)} %get-tuple-element.66), channel_id=1, source_target_pairs={{0,16},{8,24},{16,0},{24,8},{1,17},{9,25},{17,1},{25,9},{2,18},{10... | collective-permute-start | bytes 1179656 | tf_op jit(solution)/shard_map/ppermute | solution.py:547
  738.1 46.3 %collective-permute-start.23 = (bf16[512,512]{1,0:T(8,128)(2,1)}, bf16[512,512]{1,0:T(8,128)(2,1)}, u32[]{:S(2)}, u32[]{:S(2)}) collective-permute-start(bf16[512,512]{1,0:T(8,128)(2,1)} %get-tuple-element.61), channel_id=1, source_target_pairs={{0,8},{8,0},{16,24},{24,16},{1,9},{9,1},{17,25},{25,17},{2,10},{10... | collective-permute-start | bytes 1572872 | tf_op jit(solution)/shard_map/ppermute | solution.py:547
  738.7 31.0 %collective-permute-start.15 = (bf16[512,384]{0,1:T(8,128)(2,1)S(1)}, bf16[512,384]{0,1:T(8,128)(2,1)S(1)}, u32[]{:S(2)}, u32[]{:S(2)}) collective-permute-start(bf16[512,384]{0,1:T(8,128)(2,1)S(1)} %get-tuple-element.67), channel_id=1, source_target_pairs={{0,24},{8,16},{16,8},{24,0},{1,25},{9,17},{17,9},{25,1},{2,26},{10... | collective-permute-start | bytes 1179656 | tf_op jit(solution)/shard_map/ppermute | solution.py:547
  741.1 28.5 %copy-start.27 = (bf16[512,1024]{0,1:T(8,128)(2,1)S(1)}, bf16[512,1024]{0,1:T(8,128)(2,1)}, u32[]{:S(2)}) copy-start(bf16[512,1024]{0,1:T(8,128)(2,1)} %get-tuple-element.56) | copy-start | bytes 3145732
  752.0 22.0 %collective-permute-start.14 = (bf16[512,384]{0,1:T(8,128)(2,1)S(1)}, bf16[512,384]{0,1:T(8,128)(2,1)S(1)}, u32[]{:S(2)}, u32[]{:S(2)}) collective-permute-start(bf16[512,384]{0,1:T(8,128)(2,1)S(1)} %get-tuple-element.68), channel_id=1, source_target_pairs={{0,8},{8,0},{16,24},{24,16},{1,9},{9,1},{17,25},{25,17},{2,10},{10... | collective-permute-start | bytes 1179656 | tf_op jit(solution)/shard_map/ppermute | solution.py:547
  769.6 68.7 %collective-permute-start.19 = (bf16[512,1024]{0,1:T(8,128)(2,1)S(1)}, bf16[512,1024]{0,1:T(8,128)(2,1)S(1)}, u32[]{:S(2)}, u32[]{:S(2)}) collective-permute-start(bf16[512,1024]{0,1:T(8,128)(2,1)S(1)} %copy-done.27), channel_id=1, source_target_pairs={{0,16},{8,24},{16,0},{24,8},{1,17},{9,25},{17,1},{25,9},{2,18},{10... | collective-permute-start | bytes 3145736 | tf_op jit(solution)/shard_map/ppermute | solution.py:547
  774.0 87.0 %collective-permute-start.21 = (bf16[512,1024]{0,1:T(8,128)(2,1)}, bf16[512,1024]{0,1:T(8,128)(2,1)}, u32[]{:S(2)}, u32[]{:S(2)}) collective-permute-start(bf16[512,1024]{0,1:T(8,128)(2,1)} %get-tuple-element.57), channel_id=1, source_target_pairs={{0,24},{8,16},{16,8},{24,0},{1,25},{9,17},{17,9},{25,1},{2,26},{10... | collective-permute-start | bytes 3145736 | tf_op jit(solution)/shard_map/ppermute | solution.py:547
  779.7 81.3 %collective-permute-start.20 = (bf16[512,1024]{0,1:T(8,128)(2,1)}, bf16[512,1024]{0,1:T(8,128)(2,1)S(1)}, u32[]{:S(2)}, u32[]{:S(2)}) collective-permute-start(bf16[512,1024]{0,1:T(8,128)(2,1)} %get-tuple-element.58), channel_id=1, source_target_pairs={{0,8},{8,0},{16,24},{24,16},{1,9},{9,1},{17,25},{25,17},{2,10},{10... | collective-permute-start | bytes 3145736 | tf_op jit(solution)/shard_map/ppermute | solution.py:547

commit v2 on v1

v2 whole, which is shorter than its diff:
```python
import functools
import math

import jax
import jax.numpy as jnp
from jax import lax
from jax.experimental import pallas as pl
from jax.experimental.pallas import tpu as pltpu
from jax.sharding import PartitionSpec as P

HEAD = 64
SAMPLE = 512
EPS = 1e-05
ROPE_BASE = 130000.0
MESH = pl.DeviceIdType.MESH
BF16 = jnp.bfloat16
F32 = jnp.float32
ANY = pl.BlockSpec(memory_space=pl.ANY)
VMEM = pl.BlockSpec(memory_space=pltpu.VMEM)


def flip(index, bit):
    return index + bit - 2 * bit * ((index // bit) % 2)


def dot_nt(left, right):
    return lax.dot_general(left, right, (((1,), (1,)), ((), ())), preferred_element_type=F32)


def dot_tn(left, right):
    return lax.dot_general(left, right, (((0,), (0,)), ((), ())), preferred_element_type=F32)


class Group:
    def __init__(self, z_size, t_size):
        self.z_size = z_size
        self.t_size = t_size
        self.size = 2 * t_size
        inner = []
        bit = 2
        while bit < t_size:
            inner.append(bit)
            bit *= 2
        self.core = 1
        self.pair = t_size
        self.orders = (tuple(inner) + (self.pair,), tuple(inner[::-1]) + (self.pair,))
        self.inner = (tuple(inner), tuple(inner[::-1]))
        self.bits = (self.core,) + tuple(inner) + (self.pair,)
        masks = [0]
        for b in self.orders[0]:
            masks = masks + [m + b for m in masks]
        self.masks = tuple(masks)
        self.far = tuple(range(2, z_size))

    def place(self):
        return lax.axis_index("fsdp"), lax.axis_index("tensor")

    def rank(self, mask=0):
        z, t = self.place()
        r = (z % 2) * self.t_size + t
        for b in self.bits:
            if mask & b:
                r = flip(r, b)
        return r

    def partner(self, bit):
        z, t = self.place()
        if bit == self.pair:
            return (flip(z, 1), t)
        return (z, flip(t, bit))

    def across(self, mask):
        z, t = self.place()
        bit = 1
        while bit < self.z_size:
            if mask & bit:
                z = flip(z, bit)
            bit *= 2
        return (z, t)

    def greet(self):
        barrier = pltpu.get_barrier_semaphore()
        peers = [self.partner(b) for b in self.bits if b != self.pair]
        peers += [self.across(m) for m in range(1, self.z_size)]
        for peer in peers:
            pl.semaphore_signal(barrier, inc=1, device_id=peer, device_id_type=MESH)
        pl.semaphore_wait(barrier, len(peers))


def last_bit(mask, order):
    found = None
    for b in order:
        if mask & b:
            found = b
    return found


class Gather:
    def __init__(self, grp, x_ref, o_ref, send, recv, local):
        self.grp, self.x, self.o = grp, x_ref, o_ref
        self.send, self.recv = send, recv
        self.rows = x_ref.shape[0]
        self.half = self.rows // 2
        self.order = [(grp.pair,) + grp.inner[h] + (grp.core,) for h in range(2)]
        self.sent = []
        own = pl.ds(pl.multiple_of(grp.rank() * self.rows, self.rows), self.rows)
        self.own = pltpu.make_async_copy(x_ref, o_ref.at[own], local)

    def at(self, mask, h):
        first = self.grp.rank(mask) * self.rows + h * self.half
        return self.o.at[pl.ds(pl.multiple_of(first, self.half), self.half)]

    def copy(self, src, mask, h, key, bit):
        return pltpu.make_async_remote_copy(
            src_ref=src,
            dst_ref=self.at(mask, h),
            send_sem=self.send.at[h, key],
            recv_sem=self.recv.at[h, key],
            device_id=self.grp.partner(bit),
            device_id_type=MESH,
        )

    def forward(self, h, mask, bits=None):
        order = self.order[h]
        start = 0 if mask == 0 else order.index(last_bit(mask, order)) + 1
        for bit in order[start:] if bits is None else bits:
            src = self.x.at[pl.ds(h * self.half, self.half)] if mask == 0 else self.at(mask, h)
            c = self.copy(src, mask, h, mask | bit, bit)
            c.start()
            self.sent.append(c)

    def arrived(self, h, mask):
        bit = last_bit(mask, self.order[h])
        self.copy(self.at(mask, h), mask, h, mask, bit).wait_recv()

    def begin(self):
        self.own.start()
        for h in range(2):
            self.forward(h, 0, (self.grp.pair,))
        for h in range(2):
            self.forward(h, 0, self.order[h][1:])
        grp = self.grp
        plain = sorted(
            (m for m in grp.masks if m), key=lambda m: (m & grp.pair, bin(m).count("1"))
        )
        if len(plain) > 3:
            plain.remove(grp.pair)
            plain.insert(2, grp.pair)

        def step(h, m):
            self.arrived(h, m)
            self.forward(h, m)

        return [
            functools.partial(step, h, m if h == 0 else mirror(grp, m))
            for m in plain
            for h in range(2)
        ]

    def finish(self):
        for m in self.grp.masks:
            for h in range(2):
                self.arrived(h, m | self.grp.core)
        self.own.wait()
        for c in self.sent:
            c.wait_send()


def mirror(grp, mask):
    out = mask & (grp.pair | grp.core)
    a, b = grp.inner
    for p, q in zip(a, b):
        if mask & p:
            out |= q
    return out


TILE = 16


def add_rows(dst, src, rows):
    @pl.loop(0, rows // TILE)
    def _(i):
        part = pl.ds(pl.multiple_of(i * TILE, TILE), TILE)
        dst[part] = (dst[part].astype(F32) + src[part].astype(F32)).astype(dst.dtype)


def scatter_scratch(grp, rows, width):
    n = len(grp.masks)
    return [
        pltpu.VMEM((n, rows, width), BF16),
        pltpu.VMEM((2, n - 1, rows // 2, width), BF16),
        pltpu.SemaphoreType.DMA((n,)),
        pltpu.SemaphoreType.DMA((n,)),
        pltpu.SemaphoreType.DMA((2, n)),
        pltpu.SemaphoreType.DMA((2, n)),
    ]


N_SCATTER = 6


class Scatter:
    def __init__(self, grp, p, rows, got, rbuf, csend, crecv, send, recv):
        self.grp, self.p, self.rows, self.half = grp, p, rows, rows // 2
        self.got, self.rbuf = got, rbuf
        self.csend, self.crecv, self.send, self.recv = csend, crecv, send, recv
        self.index = {m: i for i, m in enumerate(grp.masks)}
        self.started = []
        self.slots = []
        for h in range(2):
            s = {}
            order = grp.orders[h]
            for i in range(len(order)):
                later = order[i + 1 :]
                for m in grp.masks:
                    if all((not m & b) or b in later for b in order):
                        s[(i, m)] = len(s)
            self.slots.append(s)

    def masks(self, pair):
        chosen = [m for m in self.grp.masks if bool(m & self.grp.pair) == pair]
        return sorted(chosen, key=lambda m: -bin(m).count("1"))

    def block(self, mask, h=None):
        first = self.grp.rank(mask) * self.rows
        if h is None:
            return self.p.at[pl.ds(pl.multiple_of(first, self.rows), self.rows)]
        return self.p.at[pl.ds(pl.multiple_of(first + h * self.half, self.half), self.half)]

    def core_copy(self, mask):
        i = self.index[mask]
        return pltpu.make_async_remote_copy(
            src_ref=self.block(mask | self.grp.core),
            dst_ref=self.got.at[i],
            send_sem=self.csend.at[i],
            recv_sem=self.crecv.at[i],
            device_id=self.grp.partner(self.grp.core),
            device_id_type=MESH,
        )

    def begin(self, masks):
        for m in masks:
            c = self.core_copy(m)
            c.start()
            self.started.append(c)

    def core_step(self, mask):
        self.core_copy(mask).wait_recv()
        add_rows(self.block(mask), self.got.at[self.index[mask]], self.rows)
        for h in range(2):
            if mask & self.grp.orders[h][0]:
                self.ship(h, 0, mask)

    def link_copy(self, h, i, mask, k):
        return pltpu.make_async_remote_copy(
            src_ref=self.block(mask, h),
            dst_ref=self.rbuf.at[h, k],
            send_sem=self.send.at[h, k],
            recv_sem=self.recv.at[h, k],
            device_id=self.grp.partner(self.grp.orders[h][i]),
            device_id_type=MESH,
        )

    def ship(self, h, i, mask):
        c = self.link_copy(h, i, mask, self.slots[h][(i, mask - self.grp.orders[h][i])])
        c.start()
        self.started.append(c)

    def take(self, h, i, mask):
        k = self.slots[h][(i, mask)]
        self.link_copy(h, i, mask, k).wait_recv()
        add_rows(self.block(mask, h), self.rbuf.at[h, k], self.half)

    def core_steps(self, pair):
        return [functools.partial(self.core_step, m) for m in self.masks(pair)]

    def link_steps(self, pair):
        steps = []
        for i in range(1, len(self.grp.orders[0])):
            for m in self.masks(pair):
                for h in range(2):
                    order = self.grp.orders[h]
                    mine = m if h == 0 else mirror(self.grp, m)
                    if any(mine & b for b in order[:i]):
                        continue

                    def step(h=h, i=i, mine=mine, order=order):
                        self.take(h, i - 1, mine)
                        if mine & order[i]:
                            self.ship(h, i, mine)

                    steps.append(step)
        return steps

    def finish(self):
        for h in range(2):
            self.take(h, len(self.grp.orders[h]) - 1, 0)

    def drain(self):
        for c in self.started:
            c.wait_send()


def plain_scatter(grp, p, rows, refs):
    scat = Scatter(grp, p, rows, *refs)
    scat.begin(scat.masks(True) + scat.masks(False))
    run(scat.core_steps(True) + scat.core_steps(False))
    run(scat.link_steps(True) + scat.link_steps(False))
    scat.finish()
    scat.drain()
    return scat.block(0)


def run(*lists):
    for i in range(max(len(x) for x in lists)):
        for steps in lists:
            if i < len(steps):
                steps[i]()


class Spread:
    def __init__(self, grp, send, recv):
        self.grp, self.send, self.recv = grp, send, recv
        self.used = 0
        self.copies = []

    def to(self, mask, src, dst):
        if mask == 0:
            c = pltpu.make_async_copy(src, dst, self.send.at[self.used])
        else:
            c = pltpu.make_async_remote_copy(
                src_ref=src,
                dst_ref=dst,
                send_sem=self.send.at[self.used],
                recv_sem=self.recv.at[self.used],
                device_id=self.grp.across(mask),
                device_id_type=MESH,
            )
        self.used += 1
        c.start()
        self.copies.append(c)

    def wait(self):
        for c in self.copies:
            c.wait()


def spread_sems(grp, parts):
    return [pltpu.SemaphoreType.DMA((grp.z_size * parts,))] * 2


def spread_weight(grp, spread, shard, whole, half_axis, at, masks=None):
    z, _ = grp.place()
    axis = 1 - half_axis
    mine, other = shard
    for m in grp.far + (0, 1) if masks is None else masks:
        src = other if m % 2 else mine
        size, width = src.shape[axis], src.shape[half_axis]
        place = pl.ds(pl.multiple_of(z * size, size), size)
        if axis == 0:
            dst = whole.at[place, at : at + width]
        else:
            dst = whole.at[at : at + width, place]
        spread.to(m, src, dst)


def halves_of(grp, ref, axis):
    z, _ = grp.place()
    size = ref.shape[axis] // 2
    out = []
    for which in (z % 2, 1 - z % 2):
        part = pl.ds(pl.multiple_of(which * size, size), size)
        out.append(ref.at[:, part] if axis == 1 else ref.at[part])
    return out


def spread_grad(grp, spread, grad, got, axis, masks=None):
    for m in grp.far + (1,) if masks is None else masks:
        place = grp.across(m)[0]
        size = grad.shape[axis] // grp.z_size
        part = pl.ds(pl.multiple_of(place * size, size), size)
        spread.to(m, grad.at[part] if axis == 0 else grad.at[:, part], got.at[m - 1])


def staged_gather(gather, after_pair):
    steps = gather.begin()
    cut = 6 if len(steps) > 6 else len(steps)
    run(steps[:cut])
    after_pair()
    run(steps[cut:])
    gather.finish()


def tiles(rows, body):
    @pl.loop(0, rows // TILE)
    def _(i):
        body(pl.ds(pl.multiple_of(i * TILE, TILE), TILE))


def norm_scale(value):
    return lax.rsqrt(jnp.mean(value * value, axis=-1, keepdims=True) + EPS)


def gather_scratch(grp):
    return [
        pltpu.SemaphoreType.DMA((2, grp.size)),
        pltpu.SemaphoreType.DMA((2, grp.size)),
        pltpu.SemaphoreType.DMA,
    ]


def params(cid):
    return pltpu.CompilerParams(
        collective_id=cid, has_side_effects=True, vmem_limit_bytes=60 << 20
    )


def sds(shape, dtype):
    return jax.ShapeDtypeStruct(shape, dtype)


def weight_views(grp, refs, axis, presliced):
    if presliced:
        return [(refs[2 * i], refs[2 * i + 1]) for i in range(len(refs) // 2)]
    return [tuple(halves_of(grp, r, axis)) for r in refs]


def shard_args(low, shards_, axis):
    aligned = shards_[0].shape[axis] // 2 % (128 if axis == 1 else 16) == 0
    if aligned:
        return False, list(shards_)
    out = []
    for w in shards_:
        size = w.shape[axis] // 2
        out += [
            lax.dynamic_slice_in_dim(w, low * size, size, axis),
            lax.dynamic_slice_in_dim(w, (1 - low) * size, size, axis),
        ]
    return True, out


def first_kernel(grp, flags, n_qkv, x_ref, gain_ref, *rest):
    pre_qkv, pre_o = flags
    qkv_refs, rest = rest[:n_qkv], rest[n_qkv:]
    n_o = 2 if pre_o else 1
    o_refs, rest = rest[:n_o], rest[n_o:]
    all_ref, wqkv_ref, wo_ref, local, send, recv, sem, zs, zr = rest
    grp.greet()
    spread = Spread(grp, zs, zr)

    def weights(masks):
        at = 0
        for pair in weight_views(grp, qkv_refs, 1, pre_qkv):
            spread_weight(grp, spread, pair, wqkv_ref, 1, at, masks)
            at += pair[0].shape[1]
        for pair in weight_views(grp, o_refs, 0, pre_o):
            spread_weight(grp, spread, pair, wo_ref, 0, 0, masks)

    def norm(rows):
        x = x_ref[rows].astype(F32)
        local[rows] = (x * norm_scale(x) * gain_ref[...]).astype(BF16)

    tiles(x_ref.shape[0], norm)
    gather = Gather(grp, local, all_ref, send, recv, sem)
    steps = gather.begin()
    weights(grp.far + (0,))
    run(steps[:6])
    weights((1,))
    run(steps[6:] or [lambda: None])
    gather.finish()
    spread.wait()


def first(grp, low, x, gain, w_query, w_key, w_value, w_out, cid):
    pre_qkv, qkv = shard_args(low, (w_query, w_key, w_value), 1)
    pre_o, out = shard_args(low, (w_out,), 0)
    rows, width = x.shape
    if pre_qkv:
        qkv = [jnp.concatenate(qkv[i::2], axis=1) for i in range(2)]
    deep = w_query.shape[0] * grp.z_size
    thin = 3 * w_query.shape[1] // 2
    return pl.pallas_call(
        functools.partial(first_kernel, grp, (pre_qkv, pre_o), len(qkv)),
        out_shape=[
            sds((rows * grp.size, width), BF16),
            sds((deep, thin), BF16),
            sds((w_out.shape[0] // 2, w_out.shape[1] * grp.z_size), BF16),
        ],
        in_specs=[VMEM, VMEM] + [ANY] * (len(qkv) + len(out)),
        out_specs=[ANY] * 3,
        scratch_shapes=[pltpu.VMEM((rows, width), BF16)]
        + gather_scratch(grp)
        + spread_sems(grp, 4),
        compiler_params=params(cid),
        name="first",
    )(x, gain, *qkv, *out)


def attend_rows(length, heads, q_ref, k_ref, v_ref, start_ref, o_ref, lse_ref, row):
    base = row * length

    def band(h, at, first, width, size):
        lanes = slice(h * HEAD, (h + 1) * HEAD)
        mine = pl.ds(pl.multiple_of(base + at, QB), size)
        keys = pl.ds(pl.multiple_of(base + first, QB), width)
        cols = pl.ds(pl.multiple_of(at, QB), size)
        query = q_ref[mine, lanes] * BF16(HEAD**-0.5)
        scores = dot_nt(k_ref[keys, lanes], query)
        mask = kept(start_ref[row, :, cols], at, size, first, width)
        scores = jnp.where(mask, scores, -1e9)
        top = jnp.max(scores, axis=0, keepdims=True)
        expo = jnp.exp(scores - top)
        total = jnp.sum(expo, axis=0, keepdims=True)
        weights = (expo * (1.0 / total)).astype(BF16)
        o_ref[mine, lanes] = dot_tn(weights, v_ref[keys, lanes]).astype(BF16)
        lse_ref[row, h : h + 1, cols] = top + jnp.log(total)

    return banded(length, heads, band)


def banded(length, heads, band):
    parts = []
    for h in range(heads):
        whole = [b for b in bands(length) if b[3] == SAMPLE + QB]
        for at, size, first, width in bands(length):
            if width != SAMPLE + QB:
                parts.append(functools.partial(band, h, at, first, width, size))

        def loop(h=h, whole=whole):
            @pl.loop(0, len(whole))
            def _(i):
                at = whole[0][0] + i * QB
                band(h, at, at - SAMPLE, SAMPLE + QB, QB)

        if whole:
            parts.append(loop)
    return parts


def middle_kernel(
    grp,
    heads,
    na_ref,
    wqkv_ref,
    wo_ref,
    cos_ref,
    sin_ref,
    start_ref,
    dy_ref,
    x_ref,
    gain_ref,
    gate_ref,
    up_ref,
    down_ref,
    q_ref,
    k_ref,
    v_ref,
    o_ref,
    lse_ref,
    h_ref,
    nm_ref,
    dyall_ref,
    wg_ref,
    wu_ref,
    wd_ref,
    p,
    rowbuf,
    rowsem,
    local,
    *rest,
):
    scat_refs, rest = rest[:N_SCATTER], rest[N_SCATTER:]
    dsend, drecv, dsem, send, recv, sem, zs, zr = rest
    rows_all, _, length = start_ref.shape
    wide = heads * HEAD
    z, _ = grp.place()
    n = rows_all // 2
    rows = [(1 - z % 2) * n + j for j in range(n)] + [(z % 2) * n + j for j in range(n)]

    blocks = length // QB

    def load(i, j):
        part = pl.ds(pl.multiple_of(rows[i] * length + j * QB, QB), QB)
        return pltpu.make_async_copy(na_ref.at[part], rowbuf.at[j % 2], rowsem.at[j % 2])

    load(0, 0).start()
    grp.greet()
    spread = Spread(grp, zs, zr)
    views = [
        (halves_of(grp, gate_ref, 1), wg_ref, 1),
        (halves_of(grp, up_ref, 1), wu_ref, 1),
        (halves_of(grp, down_ref, 0), wd_ref, 0),
    ]
    outer = Gather(grp, dy_ref, dyall_ref, dsend, drecv, dsem)
    outer_steps = outer.begin()
    for masks in (grp.far, (0, 1)):
        for pair, whole, axis in views:
            spread_weight(grp, spread, pair, whole, axis, 0, masks)
    scat = Scatter(grp, p, x_ref.shape[0], *scat_refs)

    def project(i):
        base = rows[i] * length
        if i:
            load(i, 0).start()

        @pl.loop(0, blocks)
        def _(j):
            @pl.when(j + 1 < blocks)
            def _():
                load(i, j + 1).start()

            load(i, j).wait()
            there = pl.ds(pl.multiple_of(base + j * QB, QB), QB)
            qkv = jnp.dot(rowbuf[j % 2], wqkv_ref[...], preferred_element_type=F32)
            cosine, sine = cos_ref[there], sin_ref[there]
            query, key = qkv[:, :wide], qkv[:, wide : 2 * wide]
            q_ref[there] = (query * cosine + swap_halves(query) * sine).astype(BF16)
            k_ref[there] = (key * cosine + swap_halves(key) * sine).astype(BF16)
            v_ref[there] = qkv[:, 2 * wide :].astype(BF16)

    def branch(i):
        base = rows[i] * length

        @pl.loop(0, length // QB)
        def _(j):
            there = pl.ds(pl.multiple_of(base + j * QB, QB), QB)
            p[there] = jnp.dot(o_ref[there], wo_ref[...], preferred_element_type=F32).astype(BF16)

    def parts(i):
        return (
            [functools.partial(project, i)]
            + attend_rows(length, heads, q_ref, k_ref, v_ref, start_ref, o_ref, lse_ref, rows[i])
            + [functools.partial(branch, i)]
        )

    for i in range(n):
        run(parts(i))
    scat.begin(scat.masks(True))
    run(outer_steps[:4])
    pair_steps = scat.core_steps(True)
    for i in range(n, 2 * n):
        todo = parts(i)
        run(todo, pair_steps)
        pair_steps = pair_steps[len(todo) :]
    scat.begin(scat.masks(False))
    run(pair_steps or [lambda: None])
    run(scat.core_steps(False), outer_steps[4:8])
    run(scat.link_steps(True), outer_steps[8:])
    run(scat.link_steps(False))
    scat.finish()
    summed = scat.block(0)

    def norm(part):
        h = x_ref[part].astype(F32) + summed[part].astype(F32)
        h_ref[part] = h
        local[part] = (h * norm_scale(h) * gain_ref[...]).astype(BF16)

    tiles(x_ref.shape[0], norm)
    gather = Gather(grp, local, nm_ref, send, recv, sem)
    run(gather.begin())
    scat.drain()
    outer.finish()
    gather.finish()
    spread.wait()


def middle(grp, heads, normed, wqkv, wo, cosine, sine, start, dy, x, gain, w_gate, w_up, w_down, cid):
    rows, width = x.shape
    total = rows * grp.size
    wide = heads * HEAD
    rows_all, _, length = start.shape
    thin = sds((total, wide), BF16)
    return pl.pallas_call(
        functools.partial(middle_kernel, grp, heads),
        out_shape=[thin] * 4
        + [
            sds((rows_all, heads, length), F32),
            sds((rows, width), F32),
            sds((total, width), BF16),
            sds((total, width), BF16),
            sds((w_gate.shape[0] * grp.z_size, w_gate.shape[1] // 2), BF16),
            sds((w_up.shape[0] * grp.z_size, w_up.shape[1] // 2), BF16),
            sds((w_down.shape[0] // 2, w_down.shape[1] * grp.z_size), BF16),
        ],
        in_specs=[ANY, VMEM, VMEM, VMEM, VMEM, VMEM, ANY, VMEM, VMEM, ANY, ANY, ANY],
        out_specs=[VMEM] * 6 + [ANY] * 5,
        scratch_shapes=[
            pltpu.VMEM((total, width), BF16),
            pltpu.VMEM((2, QB, width), BF16),
            pltpu.SemaphoreType.DMA((2,)),
            pltpu.VMEM((rows, width), BF16),
        ]
        + scatter_scratch(grp, rows, width)
        + gather_scratch(grp)
        + gather_scratch(grp)
        + spread_sems(grp, 3),
        compiler_params=params(cid),
        name="middle",
    )(normed, wqkv, wo, cosine, sine, start, dy, x, gain, w_gate, w_up, w_down)


def norm_back_tile(value, gain, grad):
    scale = norm_scale(value)
    scaled = grad * gain
    inner = jnp.mean(value * scaled, axis=-1, keepdims=True)
    back = scale * scaled - value * (scale * scale * scale * inner)
    return back, jnp.sum(grad * value * scale, axis=0, keepdims=True)


def got_shape(grp, grad, axis):
    shape = list(grad.shape)
    shape[axis] //= grp.z_size
    return sds((grp.z_size - 1, *shape), BF16)


def fourth_kernel(
    grp, p_ref, h_ref, dy_ref, gain_ref, gdown_ref, ggate_ref, dh_ref, gm_ref, all_ref, down_ref, gate_ref, *rest
):
    p, psem, rest = rest[0], rest[1], rest[2:]
    scat, rest = rest[:N_SCATTER], rest[N_SCATTER:]
    local, send, recv, sem, zs, zr = rest
    pltpu.make_async_copy(p_ref, p, psem).start()
    grp.greet()
    spread = Spread(grp, zs, zr)
    spread_grad(grp, spread, gdown_ref, down_ref, 1)
    spread_grad(grp, spread, ggate_ref, gate_ref, 0, grp.far)
    pltpu.make_async_copy(p_ref, p, psem).wait()
    acc = plain_scatter(grp, p, h_ref.shape[0], scat)
    gm_ref[...] = jnp.zeros_like(gm_ref)

    def back(rows):
        dn, gain_part = norm_back_tile(h_ref[rows], gain_ref[...], acc[rows].astype(F32))
        gm_ref[...] += gain_part
        dh = dy_ref[rows].astype(F32) + dn
        dh_ref[rows] = dh
        local[rows] = dh.astype(BF16)

    tiles(h_ref.shape[0], back)
    staged_gather(
        Gather(grp, local, all_ref, send, recv, sem),
        lambda: spread_grad(grp, spread, ggate_ref, gate_ref, 0, (1,)),
    )
    spread.wait()


def fourth(grp, part, hidden, out_grad, gain, grad_down, grad_gate, cid):
    rows, width = hidden.shape
    return pl.pallas_call(
        functools.partial(fourth_kernel, grp),
        out_shape=[
            sds((rows, width), F32),
            sds((1, width), F32),
            sds((rows * grp.size, width), BF16),
            got_shape(grp, grad_down, 1),
            got_shape(grp, grad_gate, 0),
        ],
        in_specs=[ANY, VMEM, VMEM, VMEM, ANY, ANY],
        out_specs=[VMEM, VMEM, ANY, ANY, ANY],
        scratch_shapes=[pltpu.VMEM((rows * grp.size, width), BF16), pltpu.SemaphoreType.DMA]
        + scatter_scratch(grp, rows, width)
        + [pltpu.VMEM((rows, width), BF16)]
        + gather_scratch(grp)
        + spread_sems(grp, 2),
        compiler_params=params(cid),
        name="fourth",
    )(part, hidden, out_grad, gain, grad_down, grad_gate)


def fifth_kernel(grp, p_ref, h_ref, gup_ref, out_ref, up_ref, *rest):
    p, psem, rest = rest[0], rest[1], rest[2:]
    scat, rest = rest[:N_SCATTER], rest[N_SCATTER:]
    zs, zr = rest
    pltpu.make_async_copy(p_ref, p, psem).start()
    grp.greet()
    spread = Spread(grp, zs, zr)
    spread_grad(grp, spread, gup_ref, up_ref, 0)
    pltpu.make_async_copy(p_ref, p, psem).wait()
    acc = plain_scatter(grp, p, h_ref.shape[0], scat)

    def finish(rows):
        out_ref[rows] = (h_ref[rows] + acc[rows].astype(F32)).astype(BF16)

    tiles(h_ref.shape[0], finish)
    spread.wait()


def fifth(grp, part, hidden, grad_up, cid):
    rows, width = hidden.shape
    return pl.pallas_call(
        functools.partial(fifth_kernel, grp),
        out_shape=[sds((rows, width), BF16), got_shape(grp, grad_up, 0)],
        in_specs=[ANY, VMEM, ANY],
        out_specs=[VMEM, ANY],
        scratch_shapes=[pltpu.VMEM((rows * grp.size, width), BF16), pltpu.SemaphoreType.DMA]
        + scatter_scratch(grp, rows, width)
        + spread_sems(grp, 1),
        compiler_params=params(cid),
        name="fifth",
    )(part, hidden, grad_up)


def sixth_kernel(
    grp, p_ref, x_ref, dh_ref, gain_ref, gm_ref, gout_ref, gqkv_ref, tok_ref, gains_ref, o_ref, qkv_ref, *rest
):
    p, psem, rest = rest[0], rest[1], rest[2:]
    scat, rest = rest[:N_SCATTER], rest[N_SCATTER:]
    buf, gs, gr, zs, zr = rest
    pltpu.make_async_copy(p_ref, p, psem).start()
    grp.greet()
    spread = Spread(grp, zs, zr)
    spread_grad(grp, spread, gout_ref, o_ref, 1)
    spread_grad(grp, spread, gqkv_ref, qkv_ref, 0)
    pltpu.make_async_copy(p_ref, p, psem).wait()
    acc = plain_scatter(grp, p, x_ref.shape[0], scat)
    buf[0, 0:1] = jnp.zeros_like(gm_ref)
    buf[0, 1:2] = gm_ref[...]

    def back(rows):
        dn, gain_part = norm_back_tile(
            x_ref[rows].astype(F32), gain_ref[...], acc[rows].astype(F32)
        )
        buf[0, 0:1] += gain_part
        tok_ref[rows] = (dh_ref[rows] + dn).astype(BF16)

    tiles(x_ref.shape[0], back)
    hops = [grp.partner(b) for b in grp.bits if b != grp.pair]
    bit = 1
    while bit < grp.z_size:
        hops.append(grp.across(bit))
        bit *= 2
    for i, hop in enumerate(hops):
        c = pltpu.make_async_remote_copy(
            src_ref=buf.at[2 * i],
            dst_ref=buf.at[2 * i + 1],
            send_sem=gs.at[i],
            recv_sem=gr.at[i],
            device_id=hop,
            device_id_type=MESH,
        )
        c.start()
        c.wait()
        buf[2 * i + 2] = buf[2 * i] + buf[2 * i + 1]
    gains_ref[...] = buf[2 * len(hops)]
    spread.wait()


def sixth(grp, part, x, dh, gain, gain_m, grad_out, grad_qkv, cid):
    rows, width = x.shape
    n = len(grp.bits) - 1 + (grp.z_size - 1).bit_length()
    return pl.pallas_call(
        functools.partial(sixth_kernel, grp),
        out_shape=[
            sds((rows, width), BF16),
            sds((2, width), F32),
            got_shape(grp, grad_out, 1),
            got_shape(grp, grad_qkv, 0),
        ],
        in_specs=[ANY, VMEM, VMEM, VMEM, VMEM, ANY, ANY],
        out_specs=[VMEM, VMEM, ANY, ANY],
        scratch_shapes=[pltpu.VMEM((rows * grp.size, width), BF16), pltpu.SemaphoreType.DMA]
        + scatter_scratch(grp, rows, width)
        + [
            pltpu.VMEM((2 * n + 1, 2, width), F32),
            pltpu.SemaphoreType.DMA((n,)),
            pltpu.SemaphoreType.DMA((n,)),
        ]
        + spread_sems(grp, 2),
        compiler_params=params(cid),
        name="sixth",
    )(part, x, dh, gain, gain_m, grad_out, grad_qkv)


def swap_halves(value):
    half = HEAD // 2
    width = value.shape[1]
    pieces = []
    for at in range(0, width, HEAD):
        pieces.append(value[:, at + half : at + HEAD])
        pieces.append(value[:, at : at + half])
    if width % 128:
        return jnp.concatenate(pieces, axis=1)
    lane = lax.broadcasted_iota(jnp.int32, value.shape, 1)
    return jnp.where(
        lane % HEAD < half, pltpu.roll(value, width - half, 1), pltpu.roll(value, half, 1)
    )


QB = 256


def bands(length):
    for at in range(0, length, QB):
        first = max(0, at - SAMPLE)
        yield at, min(QB, length - at), first, at + min(QB, length - at) - first


def kept(start_row, at, size, first, width):
    key = first + lax.broadcasted_iota(jnp.int32, (width, size), 0)
    query = at + lax.broadcasted_iota(jnp.int32, (width, size), 1)
    return (key >= start_row) & (key <= query)


def attend_back_kernel(
    heads, q_ref, k_ref, v_ref, do_ref, lse_ref, cos_ref, sin_ref, start_ref, out_ref, dq, dk, dv
):
    wide = heads * HEAD
    length = q_ref.shape[0]
    dk[...] = jnp.zeros_like(dk)
    dv[...] = jnp.zeros_like(dv)
    for h in range(heads):
        lanes = slice(h * HEAD, (h + 1) * HEAD)
        for at, size, first, width in bands(length):
            query = q_ref[at : at + size, lanes]
            key = k_ref[first : first + width, lanes]
            value = v_ref[first : first + width, lanes]
            grad = do_ref[at : at + size, lanes]
            scores = dot_nt(key, query * BF16(HEAD**-0.5))
            mask = kept(start_ref[0, :, at : at + size], at, size, first, width)
            weights = jnp.where(
                mask, jnp.exp(jnp.where(mask, scores, -1e9) - lse_ref[0, h : h + 1, at : at + size]), 0.0
            )
            dv[first : first + width, lanes] += jnp.dot(
                weights.astype(BF16), grad, preferred_element_type=F32
            )
            grad_weights = dot_nt(value, grad)
            inner = jnp.sum(weights * grad_weights, axis=0, keepdims=True)
            grad_scores = (weights * (grad_weights - inner)).astype(BF16)
            dq[at : at + size, lanes] = dot_tn(grad_scores, key)
            dk[first : first + width, lanes] += jnp.dot(
                grad_scores, query, preferred_element_type=F32
            )

    @pl.loop(0, length // QB)
    def _(i):
        rows = pl.ds(pl.multiple_of(i * QB, QB), QB)
        cosine, sine = cos_ref[rows], sin_ref[rows]
        query, key = dq[rows] * HEAD**-0.5, dk[rows] * HEAD**-0.5
        out_ref[rows, :wide] = (query * cosine - swap_halves(query) * sine).astype(BF16)
        out_ref[rows, wide : 2 * wide] = (key * cosine - swap_halves(key) * sine).astype(BF16)
        out_ref[rows, 2 * wide :] = dv[rows].astype(BF16)


def attend_back(query, key, value, grad, lse, cosine, sine, start, heads):
    rows, _, length = start.shape
    wide = heads * HEAD

    def tall(width):
        return pl.BlockSpec((length, width), lambda r: (r, 0))

    return pl.pallas_call(
        functools.partial(attend_back_kernel, heads),
        grid=(rows,),
        out_shape=jax.ShapeDtypeStruct((rows * length, 3 * wide), BF16),
        in_specs=[tall(wide)] * 4
        + [pl.BlockSpec((1, heads, length), lambda r: (r, 0, 0)), tall(wide), tall(wide)]
        + [pl.BlockSpec((1, 1, length), lambda r: (r, 0, 0))],
        out_specs=tall(3 * wide),
        scratch_shapes=[pltpu.VMEM((length, wide), F32)] * 3,
        compiler_params=pltpu.CompilerParams(vmem_limit_bytes=48 << 20),
        name="attend_back",
    )(query, key, value, grad, lse, cosine, sine, start)


def shards(
    z_size,
    t_size,
    tokens,
    gain_attn,
    gain_mlp,
    w_query,
    w_key,
    w_value,
    w_out,
    w_gate,
    w_up,
    w_down,
    segment_ids,
    out_grad,
):
    grp = Group(z_size, t_size)
    z = lax.axis_index("fsdp")
    low = z % 2

    def hop(value, mask):
        return lax.ppermute(value, "fsdp", [(i, i ^ mask) for i in range(z_size)])

    def deliver(grad, got, half_axis, axis, parts=1):
        size = grad.shape[axis] // z_size
        sums = [lax.dynamic_slice_in_dim(grad, z * size, size, axis).astype(F32), None]
        for m in range(1, z_size):
            term = got[m - 1].astype(F32)
            sums[m % 2] = term if sums[m % 2] is None else sums[m % 2] + term
        outs = []
        piece = sums[0].shape[half_axis] // parts
        for i in range(parts):
            a, b = (lax.slice_in_dim(s, i * piece, (i + 1) * piece, axis=half_axis) for s in sums)
            outs.append(
                jnp.where(
                    low == 0,
                    jnp.concatenate([a, b], axis=half_axis),
                    jnp.concatenate([b, a], axis=half_axis),
                )
            )
        return outs

    wide = w_query.shape[1] // 2
    heads = wide // HEAD

    other_ids = hop(segment_ids, 1)
    segments = jnp.where(
        low == 0,
        jnp.concatenate([segment_ids, other_ids], axis=0),
        jnp.concatenate([other_ids, segment_ids], axis=0),
    )
    rows, length = segments.shape
    start = jnp.sum(segments[:, :, None] > segments[:, None, :], axis=2, dtype=jnp.int32)
    position = (jnp.arange(length, dtype=jnp.int32)[None, :] - start).astype(F32)
    lane = jnp.arange(wide, dtype=jnp.int32)
    half = (lane % (HEAD // 2)).astype(F32)
    inverse = jnp.exp(half * (-2.0 / HEAD) * math.log(ROPE_BASE))
    angle = position.reshape(rows * length, 1) * inverse[None, :]
    cosine = jnp.cos(angle)
    sine = jnp.where(lane[None, :] % HEAD < HEAD // 2, -1.0, 1.0) * jnp.sin(angle)
    start = start.reshape(rows, 1, length)

    gain_a = gain_attn.astype(F32)[None, :]
    gain_m = gain_mlp.astype(F32)[None, :]
    normed_a, wqkv, wo = first(grp, low, tokens, gain_a, w_query, w_key, w_value, w_out, 0)
    query, key, value, attended, lse, hidden, normed_m, grad_all, wg, wu, wd = middle(
        grp,
        heads,
        normed_a,
        wqkv,
        wo,
        cosine,
        sine,
        start,
        out_grad,
        tokens,
        gain_m,
        w_gate,
        w_up,
        w_down,
        1,
    )
    gate = jnp.dot(normed_m, wg, preferred_element_type=F32)
    up = jnp.dot(normed_m, wu, preferred_element_type=F32)
    sigma = jax.nn.sigmoid(gate)
    silu_gate = gate * sigma
    act = (silu_gate * up).astype(BF16)
    grad_down = dot_tn(act, grad_all).astype(BF16)
    grad_act = dot_nt(grad_all, wd)
    grad_gate = (grad_act * up * (sigma * (1.0 + gate * (1.0 - sigma)))).astype(BF16)
    grad_up = (grad_act * silu_gate).astype(BF16)
    grad_wg = dot_tn(normed_m, grad_gate).astype(BF16)
    grad_wu = dot_tn(normed_m, grad_up).astype(BF16)
    grad_nm = (dot_nt(grad_gate, wg) + dot_nt(grad_up, wu)).astype(BF16)
    grad_hidden, gain_m_part, branch_all, got_down, got_gate = fourth(
        grp, grad_nm, hidden, out_grad, gain_m, grad_down, grad_wg, 3
    )
    out_part = jnp.dot(act, wd, preferred_element_type=F32).astype(BF16)
    output, got_up = fifth(grp, out_part, hidden, grad_wu, 4)
    grad_wout = dot_tn(attended, branch_all).astype(BF16)
    grad_attended = dot_nt(branch_all, wo).astype(BF16)
    grad_qkv = attend_back(query, key, value, grad_attended, lse, cosine, sine, start, heads)
    grad_wqkv = dot_tn(normed_a, grad_qkv).astype(BF16)
    grad_na = dot_nt(grad_qkv, wqkv).astype(BF16)
    tokens_grad, gains, got_out, got_qkv = sixth(
        grp, grad_na, tokens, grad_hidden, gain_a, gain_m_part, grad_wout, grad_wqkv, 5
    )
    (down_out,) = deliver(grad_down, got_down, 0, 1)
    (gate_out,) = deliver(grad_wg, got_gate, 1, 0)
    (up_out,) = deliver(grad_wu, got_up, 1, 0)
    (out_out,) = deliver(grad_wout, got_out, 0, 1)
    query_out, key_out, value_out = deliver(grad_wqkv, got_qkv, 1, 0, 3)
    return (
        output,
        tokens_grad,
        gains[0],
        gains[1],
        query_out,
        key_out,
        value_out,
        out_out,
        gate_out,
        up_out,
        down_out,
    )


def solution(mesh):
    return jax.shard_map(
        functools.partial(shards, mesh.shape["fsdp"], mesh.shape["tensor"]),
        mesh=mesh,
        in_specs=(
            P(("fsdp", "tensor"), None),
            P(),
            P(),
            P("fsdp", "tensor"),
            P("fsdp", "tensor"),
            P("fsdp", "tensor"),
            P("tensor", "fsdp"),
            P("fsdp", "tensor"),
            P("fsdp", "tensor"),
            P("tensor", "fsdp"),
            P("fsdp", None),
            P(("fsdp", "tensor"), None),
        ),
        out_specs=(
            P(("fsdp", "tensor"), None),
            P(("fsdp", "tensor"), None),
            P(),
            P(),
            P("fsdp", "tensor"),
            P("fsdp", "tensor"),
            P("fsdp", "tensor"),
            P("tensor", "fsdp"),
            P("fsdp", "tensor"),
            P("fsdp", "tensor"),
            P("tensor", "fsdp"),
        ),
        check_vma=False,
    )
```

time: 878 us -> 689 us (0.78)
  waiting for transfers between devices: 123 us -> 0.01 us
  starting transfers between devices: 50.1 us -> 0.07 us
  local copies, waits for them, and re-layouts: 42.9 us -> 4.21 us
  Pallas kernels: 490 us -> 523 us
  matrix products: 129 us -> 112 us
    ppermute x25 -> x1, waiting for transfers between devices: 123 us -> 0.01 us  [hop(): return lax.ppermute(value, 'fsdp', [(i, i ^ mask) for i in range(z_size)])]
    ppermute x25 -> x1, starting transfers between devices: 50.1 us -> 0.07 us  [hop(): return lax.ppermute(value, 'fsdp', [(i, i ^ mask) for i in range(z_size)])]
    pallas_call x10 -> x5, Pallas kernels: 471 us -> 504 us  [the longest x1 187 us: middle(): pl.pallas_call(functools.partial(middle_kernel, grp, heads), out_shape=[t...]
    dynamic_update_slice x14 -> x0, local copies, waits for them, and re-layouts: 17.7 us -> none  [collect(): whole = lax.dynamic_update_slice_in_dim(whole, got, (z ^ m) * size, axis)]
    dot_general x4 -> x5, matrix products: 43.3 us -> 33 us  [dot_tn(): lax.dot_general(left, right, (((0,), (0,)), ((), ())), preferred_element_...]
    dot_general x3 -> x2, matrix products: 33.5 us -> 24 us  [the longest x1 13.5 us: shards(): gate = jnp.dot(normed_m, wg, preferred_element_type=F32)]
    dot_general x4 -> x5, matrix products: 43.5 us -> 46 us  [dot_nt(): lax.dot_general(left, right, (((1,), (1,)), ((), ())), preferred_element_...]
  transfers between devices with their start and end apart: 25 -> 1, of which waited for: 6 -> 0; matrix products, arithmetic and copies ran while one was open for 8% -> 0% of each run, Pallas kernels for 42% -> 8%
where the time goes in v2:
time: 689 us; the launch traced here: 677 us
  Pallas kernels  523 us (76%)
  matrix products  112 us (16%)
  other arithmetic  36.3 us (5%)
    pallas_call x1, Pallas kernels, middle(): pl.pallas_call(functools.partial(middle_kernel, grp, heads), out_shape=[t...  187 us
    pallas_call x1, Pallas kernels, fourth(): pl.pallas_call(functools.partial(fourth_kernel, grp), out_shape=[sds((row...  124 us
    pallas_call x1, Pallas kernels, sixth(): pl.pallas_call(functools.partial(sixth_kernel, grp), out_shape=[sds((rows...  74.9 us
    pallas_call x1, Pallas kernels, fifth(): pl.pallas_call(functools.partial(fifth_kernel, grp), out_shape=[sds((rows...  62.8 us
    pallas_call x1, Pallas kernels, first(): pl.pallas_call(functools.partial(first_kernel, grp, (pre_qkv, pre_o), len...  55.7 us
    dot_general x5, matrix products, dot_nt(): lax.dot_general(left, right, (((1,), (1,)), ((), ())), preferred_element_...  46 us
    dot_general x5, matrix products, dot_tn(): lax.dot_general(left, right, (((0,), (0,)), ((), ())), preferred_element_...  33 us
    pallas_call x1, Pallas kernels, attend_back(): pl.pallas_call(functools.partial(attend_back_kernel, heads), grid=(rows,)...  19 us
  transfers between devices with their start and end apart: 1, of which 0 were waited for; matrix products, arithmetic and copies ran while one was open for 0% of the time, Pallas kernels for 8%

profile of v2, /device:TPU:8, one launch (start us, length us, event | category | flops | bytes accessed | tf_op | source)
XLA Modules:
  0.0 676.5 jit_solution(10109638959621959139)
XLA Ops:
  0.6 0.1 collective-permute-start
  0.8 1.3 broadcast_in_dim.29
  2.0 1.3 broadcast_in_dim.30
  3.3 55.7 %first.1 = (bf16[2560,2048]{1,0:T(8,128)(2,1)}, bf16[2048,384]{1,0:T(8,128)(2,1)}, bf16[128,2048]{1,0:T(8,128)(2,1)}) custom-call(bf16[160,2048]{1,0:T(8,128)(2,1)} %x_ref.5, f32[1,2048]{1,0:T(1,128)} %bitcast.59, bf16[512,256]{1,0:T(8,128)(2,1)} %rest_0_.1, bf16[512,256]{1,0:T(8,128)(2,1)} %rest_1_.1, bf16[512,256]{1,0:T(8,128)(2,1)} %rest_2_.1, ...), custom_call_target="tpu_custom_call" | custom-call | tf_op jit(solution)/shard_map/first/pallas_call | solution.py:483
  59.0 0.0 collective-permute-done
  59.0 0.8 add_select_fusion
  59.8 1.7 convert_reduce_fusion
  61.6 0.6 reshape.154.start_ref
  62.2 6.3 fusion.1
  68.5 186.9 %middle.1 = (bf16[2560,128]{1,0:T(8,128)(2,1)}, bf16[2560,128]{1,0:T(8,128)(2,1)}, bf16[2560,128]{1,0:T(8,128)(2,1)}, bf16[2560,128]{1,0:T(8,128)(2,1)}, f32[2,2...) custom-call(bf16[2560,2048]{1,0:T(8,128)(2,1)} %get-tuple-element.36, ...), custom_call_target="tpu_custom_call" | custom-call | tf_op jit(solution)/shard_map/middle/pallas_call | solution.py:674
  255.4 0.0 slice-start.6
  255.4 0.0 slice-start.7
  255.4 10.5 %fusion.8 = f32[2560,512]{1,0:T(8,128)} fusion(bf16[2560,2048]{1,0:T(8,128)(2,1)} %get-tuple-element.39, bf16[2048,512]{1,0:T(8,128)(2,1)} %get-tuple-element.41), kind=kOutput, calls=%fused_computation.46 | convolution fusion | flops 5368709120 | bytes 17825792 | tf_op jit(solution)/shard_map/dot_general | solution.py:1048
  265.9 0.0 copy-done.22
  266.0 7.9 %fusion.9 = f32[2560,512]{1,0:T(8,128)} fusion(bf16[2560,2048]{1,0:T(8,128)(2,1)S(1)} %copy-done.22, bf16[512,2048]{1,0:T(8,128)(2,1)S(1)} %copy-done.25), kind=kOutput, calls=%fused_computation.47 | convolution fusion | flops 5368709120 | bytes 17825792 | tf_op jit(solution)/shard_map/dot_general | solution.py:27
  273.8 13.5 %multiply_convert_fusion = (bf16[2560,512]{1,0:T(8,128)(2,1)}, bf16[2560,512]{1,0:T(8,128)(2,1)}, bf16[2560,512]{1,0:T(8,128)(2,1)}) fusion(f32[2560,512]{1,0:T(8,128)} %fusion.9, f32[2560,512]{1,0:T(8,128)} %fusion.8, bf16[2560,2048]{1,0:T(8,128)(2,1)S(1)} %bitcast.66, bf16[2048,512]{1,0:T(8,128)(2,1)} %get-tuple-element.40), kind=kOutput, calls=%fused_computation.4 | convolution fusion | flops 5388369920 | bytes 30932992 | tf_op jit(solution)/shard_map/dot_general | solution.py:1047
  287.3 8.7 %convolution_convert_fusion.4.gdown_ref = bf16[512,2048]{1,0:T(8,128)(2,1)} fusion(bf16[2560,512]{1,0:T(8,128)(2,1)} %get-tuple-element.63, bf16[2560,2048]{1,0:T(8,128)(2,1)S(1)} %copy-done.22), kind=kOutput, calls=%fused_computation.11 | convolution fusion | flops 5369757696 | bytes 15204352 | tf_op jit(solution)/shard_map/dot_general | solution.py:31
  296.0 0.0 copy-done.27
  296.0 8.5 %convolution_convert_fusion.1.p_ref = bf16[2560,2048]{1,0:T(8,128)(2,1)} fusion(bf16[2560,512]{1,0:T(8,128)(2,1)S(1)} %copy-done.27, bf16[512,2048]{1,0:T(8,128)(2,1)S(1)} %copy-done.26), kind=kOutput, calls=%fused_computation.3 | convolution fusion | flops 5373952000 | bytes 15204352 | tf_op jit(solution)/shard_map/dot_general | solution.py:1062
  304.5 6.8 %convolution_convert_fusion.3.ggate_ref = bf16[2048,512]{1,0:T(8,128)(2,1)} fusion(bf16[2560,2048]{1,0:T(8,128)(2,1)S(1)} %bitcast.66, bf16[2560,512]{1,0:T(8,128)(2,1)S(1)} %copy-done.28), kind=kOutput, calls=%fused_computation.10 | convolution fusion | flops 5369757696 | bytes 15204352 | tf_op jit(solution)/shard_map/dot_general | solution.py:31
  311.4 10.2 %fusion.10 = f32[2560,2048]{1,0:T(8,128)} fusion(bf16[2560,512]{1,0:T(8,128)(2,1)S(1)} %copy-done.28, bf16[2048,512]{1,0:T(8,128)(2,1)S(1)} %copy-done.24), kind=kOutput, calls=%fused_computation.48 | convolution fusion | flops 5368709120 | bytes 25690112 | tf_op jit(solution)/shard_map/dot_general | solution.py:27
  321.6 6.8 %convolution_convert_fusion.5.gup_ref = bf16[2048,512]{1,0:T(8,128)(2,1)} fusion(bf16[2560,2048]{1,0:T(8,128)(2,1)S(1)} %bitcast.66, bf16[2560,512]{1,0:T(8,128)(2,1)S(1)} %copy-done.29), kind=kOutput, calls=%fused_computation.12 | convolution fusion | flops 5369757696 | bytes 15204352 | tf_op jit(solution)/shard_map/dot_general | solution.py:31
  328.4 62.8 %fifth.1 = (bf16[160,2048]{1,0:T(8,128)(2,1)}, bf16[3,512,512]{2,1,0:T(8,128)(2,1)}) custom-call(bf16[2560,2048]{1,0:T(8,128)(2,1)} %convolution_convert_fusion.1.p_ref, f32[160,2048]{1,0:T(8,128)} %get-tuple-element.43.h_ref, bf16[2048,512]{1,0:T(8,128)(2,1)} %convolution_convert_fusion.5.gup_ref), custom_call_target="tpu_custom_call" | custom-call | tf_op jit(solution)/shard_map/fifth/pallas_call | solution.py:790
  391.2 2.5 add_bitcast_fusion.1
  393.7 2.3 convert_add_fusion.1
  396.0 12.4 %add_convert_fusion.p_ref = bf16[2560,2048]{1,0:T(8,128)(2,1)} fusion(f32[2560,2048]{1,0:T(8,128)} %fusion.10, bf16[2560,512]{1,0:T(8,128)(2,1)S(1)} %copy-done.29, bf16[2048,512]{1,0:T(8,128)(2,1)S(1)} %copy-done.23), kind=kOutput, calls=%fused_computation | convolution fusion | flops 5379194880 | bytes 36175872 | tf_op jit(solution)/shard_map/dot_general | solution.py:27
  408.4 123.6 %fourth.1 = (f32[160,2048]{1,0:T(8,128)}, f32[1,2048]{1,0:T(1,128)}, bf16[2560,2048]{1,0:T(8,128)(2,1)}, bf16[3,512,512]{2,1,0:T(8,128)(2,1)}, bf16[3,512,512]{2,1,0:T(8,128)(2,1)}) custom-call(bf16[2560,2048]{1,0:T(8,128)(2,1)} %add_convert_fusion.p_ref, f32[160,2048]{1,0:T(8,128)} %get-tuple-element.43.h_ref, bf16[160,2048]{1,0:T(8,128)(2,1)} %dy_ref.3, ...), custom_call_target="tpu_custom_call" | custom-call | tf_op jit(solution)/shard_map/fourth/pallas_call | solution.py:749
  532.0 2.5 convert_add_fusion.2
  534.5 2.5 add_bitcast_fusion.2
  537.0 0.0 copy-done.16
  537.0 2.2 convert_add_fusion
  539.2 1.1 add_bitcast_fusion
  540.4 0.0 copy-start.5
  540.4 0.0 copy-start.6
  540.4 0.0 slice-start.4
  540.4 0.0 slice-start.5
  540.4 7.0 %convolution_convert_fusion.2.do_ref = bf16[2560,128]{1,0:T(8,128)(2,1)S(1)} fusion(bf16[2560,2048]{1,0:T(8,128)(2,1)} %get-tuple-element.49, bf16[128,2048]{1,0:T(8,128)(2,1)S(1)} %copy-done.20), kind=kOutput, calls=%fused_computation.9 | convolution fusion | flops 1342504960 | bytes 11665408 | tf_op jit(solution)/shard_map/dot_general | solution.py:27
  547.6 19.0 %attend_back.1 = bf16[2560,384]{1,0:T(8,128)(2,1)} custom-call(bf16[2560,128]{1,0:T(8,128)(2,1)S(1)} %copy-done.2, bf16[2560,128]{1,0:T(8,128)(2,1)S(1)} %copy-done.3, bf16[2560,128]{1,0:T(8,128)(2,1)S(1)} %copy-done.4, bf16[2560,128]{1,0:T(8,128)(2,1)S(1)} %convolution_convert_fusion.2.do_ref, f32[2,2,1280]{2,1,0:T(2,128)S(1)} %copy-done.6, ...), custom_call_target="tpu_custom_call" | custom-call | tf_op jit(solution)/shard_map/attend_back/pallas_call | solution.py:951
  566.5 0.0 copy-start.13
  566.5 0.0 slice-start
  566.6 0.0 slice-start.1
  566.6 8.4 %convolution_convert_fusion.6.gqkv_ref = bf16[2048,384]{1,0:T(8,128)(2,1)} fusion(bf16[2560,2048]{1,0:T(8,128)(2,1)S(1)} %bitcast.58, bf16[2560,384]{1,0:T(8,128)(2,1)} %attend_back.1), kind=kOutput, calls=%fused_computation.13 | convolution fusion | flops 4027318272 | bytes 14024704 | tf_op jit(solution)/shard_map/dot_general | solution.py:31
  575.0 8.5 %convolution_convert_fusion.p_ref = bf16[2560,2048]{1,0:T(8,128)(2,1)} fusion(bf16[2560,384]{1,0:T(8,128)(2,1)S(1)} %copy-done.13, bf16[2048,384]{1,0:T(8,128)(2,1)S(1)} %copy-done.15), kind=kOutput, calls=%fused_computation.2 | convolution fusion | flops 4031774720 | bytes 14024704 | tf_op jit(solution)/shard_map/dot_general | solution.py:27
  583.6 2.3 convolution_convert_fusion.7.gout_ref
  585.9 74.9 %sixth.1 = (bf16[160,2048]{1,0:T(8,128)(2,1)}, f32[2,2048]{1,0:T(2,128)}, bf16[3,128,512]{2,1,0:T(8,128)(2,1)}, bf16[3,512,384]{2,1,0:T(8,128)(2,1)}) custom-call(bf16[2560,2048]{1,0:T(8,128)(2,1)} %convolution_convert_fusion.p_ref, bf16[160,2048]{1,0:T(8,128)(2,1)} %x_ref.5, f32[160,2048]{1,0:T(8,128)} %get-tuple-element.51.dh_ref, f32[1,2048]{1,0:T(1,128)} %bitcast.60, ...), custom_call_target="tpu_custom_call" | custom-call | tf_op jit(solution)/shard_map/sixth/pallas_call | solution.py:851
  660.8 1.1 convert_add_fusion.4
  661.9 1.0 add_bitcast_fusion.4
  662.9 1.2 convert_add_fusion.3
  664.2 0.1 add_bitcast_fusion.3
  664.2 0.1 fusion.5
  664.3 0.6 fusion.7
  664.9 0.1 fusion.6
  665.0 0.4 copy-done.7
  665.4 0.3 copy-done.10
  665.7 1.7 maximum_select_fusion.1
  667.4 1.7 maximum_select_fusion
  669.1 0.3 copy-done.12
  669.5 1.6 maximum_select_fusion.2
  671.1 0.8 maximum_select_fusion.6
  671.9 0.8 maximum_select_fusion.5
  672.7 0.8 maximum_select_fusion.4
  673.6 0.8 maximum_select_fusion.3
  674.4 0.8 copy.34
  675.2 0.8 copy.35
  (69 shorter events, 0.2 us)
Async XLA Ops:
  0.6 58.4 %collective-permute-start = (s32[1,1280]{1,0:T(1,128)}, s32[1,1280]{1,0:T(1,128)S(1)}, u32[]{:S(2)}, u32[]{:S(2)}) collective-permute-start(s32[1,1280]{1,0:T(1,128)} %param.22), channel_id=1, source_target_pairs={{0,8},{8,0},{16,24},{24,16},{1,9},{9,1},{17,25},{25,17},{2,10},{10... | collective-permute-start | bytes 15368 | tf_op jit(solution)/shard_map/ppermute | solution.py:986
  255.4 10.6 %copy-start.22 = (bf16[2560,2048]{1,0:T(8,128)(2,1)S(1)}, bf16[2560,2048]{1,0:T(8,128)(2,1)}, u32[]{:S(2)}) copy-start(bf16[2560,2048]{1,0:T(8,128)(2,1)} %get-tuple-element.44) | copy-start | bytes 31457284
  255.4 10.6 %copy-start.25 = (bf16[512,2048]{1,0:T(8,128)(2,1)S(1)}, bf16[512,2048]{1,0:T(8,128)(2,1)}, u32[]{:S(2)}) copy-start(bf16[512,2048]{1,0:T(8,128)(2,1)} %get-tuple-element.42) | copy-start | bytes 6291460
  255.4 18.4 %slice-start.6 = ((s8[10485760]{0:T(1024)(128)(4,1)}), s8[4194304]{0:T(1024)(128)(4,1)S(1)}, s32[]{:S(2)}) async-start(s8[10485760]{0:T(1024)(128)(4,1)} %bitcast.65), calls=%async_computation.6 | async-start | bytes 8388608
  255.4 18.4 %slice-start.7 = ((s8[10485760]{0:T(1024)(128)(4,1)}), s8[4194304]{0:T(1024)(128)(4,1)S(1)}, s32[]{:S(2)}) async-start(s8[10485760]{0:T(1024)(128)(4,1)} %bitcast.65), calls=%async_computation.7 | async-start | bytes 8388608
  265.9 7.9 %slice-start.8 = ((s8[10485760]{0:T(1024)(128)(4,1)}), s8[2097152]{0:T(1024)(128)(4,1)S(1)}, s32[]{:S(2)}) async-start(s8[10485760]{0:T(1024)(128)(4,1)} %bitcast.65), calls=%async_computation.8 | async-start | bytes 4194304
  287.3 8.7 %copy-start.26 = (bf16[512,2048]{1,0:T(8,128)(2,1)S(1)}, bf16[512,2048]{1,0:T(8,128)(2,1)}, u32[]{:S(2)}) copy-start(bf16[512,2048]{1,0:T(8,128)(2,1)} %get-tuple-element.42) | copy-start | bytes 6291460
  287.3 8.7 %copy-start.27 = (bf16[2560,512]{1,0:T(8,128)(2,1)S(1)}, bf16[2560,512]{1,0:T(8,128)(2,1)}, u32[]{:S(2)}) copy-start(bf16[2560,512]{1,0:T(8,128)(2,1)} %get-tuple-element.63) | copy-start | bytes 7864324
  296.0 8.5 %copy-start.28 = (bf16[2560,512]{1,0:T(8,128)(2,1)S(1)}, bf16[2560,512]{1,0:T(8,128)(2,1)}, u32[]{:S(2)}) copy-start(bf16[2560,512]{1,0:T(8,128)(2,1)} %get-tuple-element.61) | copy-start | bytes 7864324
  304.5 6.8 %copy-start.24 = (bf16[2048,512]{1,0:T(8,128)(2,1)S(1)}, bf16[2048,512]{1,0:T(8,128)(2,1)}, u32[]{:S(2)}) copy-start(bf16[2048,512]{1,0:T(8,128)(2,1)} %get-tuple-element.40) | copy-start | bytes 6291460
  311.4 10.2 %copy-start.29 = (bf16[2560,512]{1,0:T(8,128)(2,1)S(1)}, bf16[2560,512]{1,0:T(8,128)(2,1)}, u32[]{:S(2)}) copy-start(bf16[2560,512]{1,0:T(8,128)(2,1)} %get-tuple-element.62) | copy-start | bytes 7864324
  391.2 4.8 copy-start.23
  532.0 5.0 copy-start.16
  534.5 32.0 %slice-start.3 = ((s8[10485760]{0:T(1024)(128)(4,1)}), s8[4194304]{0:T(1024)(128)(4,1)S(1)}, s32[]{:S(2)}) async-start(s8[10485760]{0:T(1024)(128)(4,1)} %bitcast.57), calls=%async_computation.3 | async-start | bytes 8388608
  537.0 3.4 copy-start.20
  540.4 7.1 %copy-start = (f32[2560,128]{1,0:T(8,128)S(1)}, f32[2560,128]{1,0:T(8,128)}, u32[]{:S(2)}) copy-start(f32[2560,128]{1,0:T(8,128)} %get-tuple-element.72.sin_ref) | copy-start | bytes 3932164
  540.4 7.1 %copy-start.1 = (f32[2560,128]{1,0:T(8,128)S(1)}, f32[2560,128]{1,0:T(8,128)}, u32[]{:S(2)}) copy-start(f32[2560,128]{1,0:T(8,128)} %get-tuple-element.73.cos_ref) | copy-start | bytes 3932164
  540.4 7.1 %copy-start.2 = (bf16[2560,128]{1,0:T(8,128)(2,1)S(1)}, bf16[2560,128]{1,0:T(8,128)(2,1)}, u32[]{:S(2)}) copy-start(bf16[2560,128]{1,0:T(8,128)(2,1)} %get-tuple-element.46.q_ref) | copy-start | bytes 1966084
  540.4 7.1 %copy-start.3 = (bf16[2560,128]{1,0:T(8,128)(2,1)S(1)}, bf16[2560,128]{1,0:T(8,128)(2,1)}, u32[]{:S(2)}) copy-start(bf16[2560,128]{1,0:T(8,128)(2,1)} %get-tuple-element.47.k_ref) | copy-start | bytes 1966084
  540.4 7.1 %copy-start.4 = (bf16[2560,128]{1,0:T(8,128)(2,1)S(1)}, bf16[2560,128]{1,0:T(8,128)(2,1)}, u32[]{:S(2)}) copy-start(bf16[2560,128]{1,0:T(8,128)(2,1)} %get-tuple-element.48.v_ref) | copy-start | bytes 1966084
  540.4 7.1 %copy-start.5 = (s32[2,1,1280]{2,1,0:T(1,128)S(1)}, s32[2,1,1280]{2,1,0:T(1,128)}, u32[]{:S(2)}) copy-start(s32[2,1,1280]{2,1,0:T(1,128)} %reshape.154.start_ref) | copy-start | bytes 30724
  540.4 7.1 %copy-start.6 = (f32[2,2,1280]{2,1,0:T(2,128)S(1)}, f32[2,2,1280]{2,1,0:T(2,128)}, u32[]{:S(2)}) copy-start(f32[2,2,1280]{2,1,0:T(2,128)} %get-tuple-element.50.lse_ref) | copy-start | bytes 61444
  540.4 26.1 %slice-start.4 = ((s8[10485760]{0:T(1024)(128)(4,1)}), s8[4194304]{0:T(1024)(128)(4,1)S(1)}, s32[]{:S(2)}) async-start(s8[10485760]{0:T(1024)(128)(4,1)} %bitcast.57), calls=%async_computation.4 | async-start | bytes 8388608
  540.4 26.1 %slice-start.5 = ((s8[10485760]{0:T(1024)(128)(4,1)}), s8[2097152]{0:T(1024)(128)(4,1)S(1)}, s32[]{:S(2)}) async-start(s8[10485760]{0:T(1024)(128)(4,1)} %bitcast.57), calls=%async_computation.5 | async-start | bytes 4194304
  566.5 8.5 %copy-start.13 = (bf16[2560,384]{1,0:T(8,128)(2,1)S(1)}, bf16[2560,384]{1,0:T(8,128)(2,1)}, u32[]{:S(2)}) copy-start(bf16[2560,384]{1,0:T(8,128)(2,1)} %attend_back.1) | copy-start | bytes 5898244
  566.5 8.4 %copy-start.15 = (bf16[2048,384]{1,0:T(8,128)(2,1)S(1)}, bf16[2048,384]{1,0:T(8,128)(2,1)}, u32[]{:S(2)}) copy-start(bf16[2048,384]{1,0:T(8,128)(2,1)} %get-tuple-element.37.wqkv_ref) | copy-start | bytes 4718596
  566.5 17.0 %slice-start = ((s8[10485760]{0:T(1024)(128)(4,1)}), s8[4194304]{0:T(1024)(128)(4,1)S(1)}, s32[]{:S(2)}) async-start(s8[10485760]{0:T(1024)(128)(4,1)} %bitcast.55), calls=%async_computation | async-start | bytes 8388608
  566.6 17.0 %slice-start.1 = ((s8[10485760]{0:T(1024)(128)(4,1)}), s8[4194304]{0:T(1024)(128)(4,1)S(1)}, s32[]{:S(2)}) async-start(s8[10485760]{0:T(1024)(128)(4,1)} %bitcast.55), calls=%async_computation.1 | async-start | bytes 8388608
  575.0 8.6 %slice-start.2 = ((s8[10485760]{0:T(1024)(128)(4,1)}), s8[2097152]{0:T(1024)(128)(4,1)S(1)}, s32[]{:S(2)}) async-start(s8[10485760]{0:T(1024)(128)(4,1)} %bitcast.55), calls=%async_computation.2 | async-start | bytes 4194304
  575.0 8.6 %copy-start.14 = (bf16[2560,128]{1,0:T(8,128)(2,1)S(1)}, bf16[2560,128]{1,0:T(8,128)(2,1)}, u32[]{:S(2)}) copy-start(bf16[2560,128]{1,0:T(8,128)(2,1)} %get-tuple-element.53) | copy-start | bytes 1966084
  660.8 3.3 copy-start.17
  661.9 2.4 copy-start.21
  664.1 1.2 copy-start.7
  664.1 1.5 copy-start.10
  664.9 2.5 copy-start.8
  664.9 2.5 copy-start.11
  667.4 1.7 copy-start.9
  667.4 2.1 copy-start.12
  671.1 3.3 copy-start.18
  671.1 4.2 copy-start.19

commit v3 on v2

--- a/solution.py
+++ b/solution.py
@@ -11,6 +11,7 @@
 HEAD = 64
 SAMPLE = 512
 EPS = 1e-05
+LANES = 128
 ROPE_BASE = 130000.0
 MESH = pl.DeviceIdType.MESH
 BF16 = jnp.bfloat16
@@ -63,6 +64,17 @@
                 r = flip(r, b)
         return r
 
+    def chip_at(self, j):
+        chip = self.rank() // 2
+        mask = len(self.masks) - 1 - j
+        out = 0
+        bit = 1
+        while bit < len(self.masks):
+            a, b = (chip // bit) % 2, (mask // bit) % 2
+            out = out + (a + b - 2 * a * b) * bit
+            bit *= 2
+        return out
+
     def partner(self, bit):
         z, t = self.place()
         if bit == self.pair:
@@ -124,10 +136,12 @@
         order = self.order[h]
         start = 0 if mask == 0 else order.index(last_bit(mask, order)) + 1
         for bit in order[start:] if bits is None else bits:
-            src = self.x.at[pl.ds(h * self.half, self.half)] if mask == 0 else self.at(mask, h)
-            c = self.copy(src, mask, h, mask | bit, bit)
-            c.start()
-            self.sent.append(c)
+            self.own_copy(h, mask, bit).start()
+            self.sent.append((h, mask, bit))
+
+    def own_copy(self, h, mask, bit):
+        src = self.x.at[pl.ds(h * self.half, self.half)] if mask == 0 else self.at(mask, h)
+        return self.copy(src, mask, h, mask | bit, bit)
 
     def arrived(self, h, mask):
         bit = last_bit(mask, self.order[h])
@@ -137,8 +151,9 @@
         self.own.start()
         for h in range(2):
             self.forward(h, 0, (self.grp.pair,))
-        for h in range(2):
-            self.forward(h, 0, self.order[h][1:])
+        for k in range(1, len(self.order[0])):
+            for h in range(2):
+                self.forward(h, 0, (self.order[h][k],))
         grp = self.grp
         plain = sorted(
             (m for m in grp.masks if m), key=lambda m: (m & grp.pair, bin(m).count("1"))
@@ -162,8 +177,8 @@
             for h in range(2):
                 self.arrived(h, m | self.grp.core)
         self.own.wait()
-        for c in self.sent:
-            c.wait_send()
+        for sent in self.sent:
+            self.own_copy(*sent).wait_send()
 
 
 def mirror(grp, mask):
@@ -201,11 +216,12 @@
 
 
 class Scatter:
-    def __init__(self, grp, p, rows, got, rbuf, csend, crecv, send, recv):
+    def __init__(self, grp, p, rows, got, rbuf, csend, crecv, send, recv, own=None):
         self.grp, self.p, self.rows, self.half = grp, p, rows, rows // 2
+        self.own = own
         self.got, self.rbuf = got, rbuf
         self.csend, self.crecv, self.send, self.recv = csend, crecv, send, recv
-        self.index = {m: i for i, m in enumerate(grp.masks)}
+        self.index = {m: len(grp.masks) - 1 - m // 2 for m in grp.masks}
         self.started = []
         self.slots = []
         for h in range(2):
@@ -220,9 +236,24 @@
 
     def masks(self, pair):
         chosen = [m for m in self.grp.masks if bool(m & self.grp.pair) == pair]
-        return sorted(chosen, key=lambda m: -bin(m).count("1"))
+        return sorted(chosen, reverse=True)
+
+    def begin_tile(self, j):
+        _, t = self.grp.place()
+        first = (self.grp.chip_at(j) * 2 + 1 - t % 2) * self.rows
+        pltpu.make_async_remote_copy(
+            src_ref=self.p.at[pl.ds(pl.multiple_of(first, self.rows), self.rows)],
+            dst_ref=self.got.at[j],
+            send_sem=self.csend.at[j],
+            recv_sem=self.crecv.at[j],
+            device_id=self.grp.partner(self.grp.core),
+            device_id_type=MESH,
+        ).start()
 
     def block(self, mask, h=None):
+        if self.own is not None and not mask & self.grp.core:
+            mine = self.own.at[self.index[mask]]
+            return mine if h is None else mine.at[pl.ds(h * self.half, self.half)]
         first = self.grp.rank(mask) * self.rows
         if h is None:
             return self.p.at[pl.ds(pl.multiple_of(first, self.rows), self.rows)]
@@ -241,9 +272,12 @@
 
     def begin(self, masks):
         for m in masks:
-            c = self.core_copy(m)
-            c.start()
-            self.started.append(c)
+            self.core_copy(m).start()
+
+    def load(self, mask, sem):
+        first = pl.multiple_of(self.grp.rank(mask) * self.rows, self.rows)
+        i = self.index[mask]
+        return pltpu.make_async_copy(self.p.at[pl.ds(first, self.rows)], self.own.at[i], sem.at[i])
 
     def core_step(self, mask):
         self.core_copy(mask).wait_recv()
@@ -263,9 +297,11 @@
         )
 
     def ship(self, h, i, mask):
-        c = self.link_copy(h, i, mask, self.slots[h][(i, mask - self.grp.orders[h][i])])
-        c.start()
-        self.started.append(c)
+        self.out_copy(h, i, mask).start()
+        self.started.append((h, i, mask))
+
+    def out_copy(self, h, i, mask):
+        return self.link_copy(h, i, mask, self.slots[h][(i, mask - self.grp.orders[h][i])])
 
     def take(self, h, i, mask):
         k = self.slots[h][(i, mask)]
@@ -298,8 +334,10 @@
             self.take(h, len(self.grp.orders[h]) - 1, 0)
 
     def drain(self):
-        for c in self.started:
-            c.wait_send()
+        for m in self.grp.masks:
+            self.core_copy(m).wait_send()
+        for sent in self.started:
+            self.out_copy(*sent).wait_send()
 
 
 def plain_scatter(grp, p, rows, refs):
@@ -323,27 +361,35 @@
     def __init__(self, grp, send, recv):
         self.grp, self.send, self.recv = grp, send, recv
         self.used = 0
-        self.copies = []
-
-    def to(self, mask, src, dst):
-        if mask == 0:
-            c = pltpu.make_async_copy(src, dst, self.send.at[self.used])
-        else:
-            c = pltpu.make_async_remote_copy(
+        self.makers = []
+
+    def to(self, mask, views):
+        k = self.used
+        self.used += 1
+
+        def make():
+            src, dst = views()
+            if mask == 0:
+                return pltpu.make_async_copy(src, dst, self.send.at[k])
+            return pltpu.make_async_remote_copy(
                 src_ref=src,
                 dst_ref=dst,
-                send_sem=self.send.at[self.used],
-                recv_sem=self.recv.at[self.used],
+                send_sem=self.send.at[k],
+                recv_sem=self.recv.at[k],
                 device_id=self.grp.across(mask),
                 device_id_type=MESH,
             )
-        self.used += 1
-        c.start()
-        self.copies.append(c)
+
+        make().start()
+        self.makers.append(make)
 
     def wait(self):
-        for c in self.copies:
-            c.wait()
+        self.wait_first(len(self.makers))
+
+    def wait_first(self, count):
+        for make in self.makers[:count]:
+            make().wait()
+        self.makers = self.makers[count:]
 
 
 def spread_sems(grp, parts):
@@ -351,18 +397,19 @@
 
 
 def spread_weight(grp, spread, shard, whole, half_axis, at, masks=None):
-    z, _ = grp.place()
     axis = 1 - half_axis
     mine, other = shard
     for m in grp.far + (0, 1) if masks is None else masks:
-        src = other if m % 2 else mine
-        size, width = src.shape[axis], src.shape[half_axis]
-        place = pl.ds(pl.multiple_of(z * size, size), size)
-        if axis == 0:
-            dst = whole.at[place, at : at + width]
-        else:
-            dst = whole.at[at : at + width, place]
-        spread.to(m, src, dst)
+
+        def views(src=other if m % 2 else mine):
+            z, _ = grp.place()
+            size, width = src.shape[axis], src.shape[half_axis]
+            place = pl.ds(pl.multiple_of(z * size, size), size)
+            if axis == 0:
+                return src, whole.at[place, at : at + width]
+            return src, whole.at[at : at + width, place]
+
+        spread.to(m, views)
 
 
 def halves_of(grp, ref, axis):
@@ -375,12 +422,81 @@
     return out
 
 
+def weight_jobs(grp, spread, shard, whole, half_axis, pieces):
+    axis = 1 - half_axis
+    mine, other = shard
+    jobs = {m: [] for m in range(grp.z_size)}
+    for i in range(pieces):
+        for m in range(grp.z_size):
+
+            def views(i=i, src=other if m % 2 else mine):
+                z, _ = grp.place()
+                size, width = src.shape[0] // pieces, src.shape[1]
+                piece = src.at[pl.ds(i * size, size)]
+                if axis == 0:
+                    first = pl.multiple_of(z * (size * pieces) + i * size, size)
+                    return piece, whole.at[pl.ds(first, size)]
+                place = pl.ds(pl.multiple_of(z * width, width), width)
+                return piece, whole.at[pl.ds(i * size, size), place]
+
+            jobs[m].append(functools.partial(spread.to, m, views))
+    return by_distance(grp, jobs)
+
+
+def grad_jobs(grp, spread, grad, got, axis, pieces):
+    jobs = {m: [] for m in range(1, grp.z_size)}
+    for i in range(pieces):
+        for m in range(1, grp.z_size):
+
+            def views(i=i, m=m):
+                place = grp.across(m)[0]
+                size = got.shape[1] // pieces
+                land = got.at[m - 1, pl.ds(i * size, size)]
+                if axis == 0:
+                    first = pl.multiple_of(place * (size * pieces) + i * size, size)
+                    return grad.at[pl.ds(first, size)], land
+                width = got.shape[2]
+                part = pl.ds(pl.multiple_of(place * width, width), width)
+                return grad.at[pl.ds(i * size, size), part], land
+
+            jobs[m].append(functools.partial(spread.to, m, views))
+    return by_distance(grp, jobs)
+
+
+def by_distance(grp, jobs):
+    far = [job for jobs_i in zip(*(jobs[m] for m in grp.far)) for job in jobs_i]
+    near = [job for jobs_i in zip(*(jobs[m] for m in (1, 0) if m in jobs)) for job in jobs_i]
+    return far, near
+
+
+def mixed(steps, jobs, first=0):
+    out = list(steps[:first])
+    tail = steps[first:]
+    done = 0
+    for i, step in enumerate(tail):
+        upto = (i + 1) * len(jobs) // len(tail)
+        out.append(functools.partial(run, [step] + jobs[done:upto]))
+        done = upto
+    return out + (jobs if not tail else [])
+
+
+PIECES = 1
+
+
+def top_rows(views, which):
+    size = views[0].shape[0] // 2
+    return [v.at[pl.ds(which * size, size)] for v in views]
+
+
 def spread_grad(grp, spread, grad, got, axis, masks=None):
     for m in grp.far + (1,) if masks is None else masks:
-        place = grp.across(m)[0]
-        size = grad.shape[axis] // grp.z_size
-        part = pl.ds(pl.multiple_of(place * size, size), size)
-        spread.to(m, grad.at[part] if axis == 0 else grad.at[:, part], got.at[m - 1])
+
+        def views(m=m):
+            size = grad.shape[axis] // grp.z_size
+            part = pl.ds(pl.multiple_of(grp.across(m)[0] * size, size), size)
+            return (grad.at[part] if axis == 0 else grad.at[:, part]), got.at[m - 1]
+
+        spread.to(m, views)
 
 
 def staged_gather(gather, after_pair):
@@ -412,7 +528,7 @@
 
 def params(cid):
     return pltpu.CompilerParams(
-        collective_id=cid, has_side_effects=True, vmem_limit_bytes=60 << 20
+        collective_id=cid, has_side_effects=True, vmem_limit_bytes=61952 << 10
     )
 
 
@@ -445,9 +561,12 @@
     qkv_refs, rest = rest[:n_qkv], rest[n_qkv:]
     n_o = 2 if pre_o else 1
     o_refs, rest = rest[:n_o], rest[n_o:]
-    all_ref, wqkv_ref, wo_ref, local, send, recv, sem, zs, zr = rest
+    seg_ref, all_ref, wqkv_ref, wo_ref, start_ref, cos_ref, sin_ref, local, ids, send, recv, sem, zs, zr = rest
     grp.greet()
     spread = Spread(grp, zs, zr)
+    z, _ = grp.place()
+    spread.to(0, lambda: (seg_ref, ids.at[z % 2]))
+    spread.to(1, lambda: (seg_ref, ids.at[z % 2]))
 
     def weights(masks):
         at = 0
@@ -459,12 +578,14 @@
 
     def norm(rows):
         x = x_ref[rows].astype(F32)
-        local[rows] = (x * norm_scale(x) * gain_ref[...]).astype(BF16)
+        local[rows] = (x * norm_scale(x) * gain_ref[...].astype(F32)).astype(BF16)
 
     tiles(x_ref.shape[0], norm)
     gather = Gather(grp, local, all_ref, send, recv, sem)
     steps = gather.begin()
     weights(grp.far + (0,))
+    spread.wait_first(2)
+    places(ids, start_ref, cos_ref, sin_ref)
     run(steps[:6])
     weights((1,))
     run(steps[6:] or [lambda: None])
@@ -472,7 +593,34 @@
     spread.wait()
 
 
-def first(grp, low, x, gain, w_query, w_key, w_value, w_out, cid):
+def places(ids, start_ref, cos_ref, sin_ref):
+    planes, rows, length = ids.shape
+    wide = cos_ref.shape[1]
+    place = lax.broadcasted_iota(jnp.int32, (1, length), 1)
+    lane = lax.broadcasted_iota(jnp.int32, (LANES, LANES), 1)
+    pair = (lane % (HEAD // 2)).astype(F32)
+    inverse = jnp.exp(pair * (-2.0 / HEAD) * math.log(ROPE_BASE))
+    sign = jnp.where(lane % HEAD < HEAD // 2, -1.0, 1.0)
+    for a in range(planes):
+        for r in range(rows):
+            row = a * rows + r
+            own = ids[a, r : r + 1]
+            change = (place == 0) | (own != pltpu.roll(own, 1, 1))
+            start = jnp.where(change, place, 0)
+            step = 1
+            while step < length:
+                start = jnp.maximum(start, jnp.where(place >= step, pltpu.roll(start, step, 1), 0))
+                step *= 2
+            start_ref[row] = start
+            position = (place - start).astype(F32)
+            for c in range(0, length, LANES):
+                angle = jnp.broadcast_to(position[:, c : c + LANES], (LANES, LANES)).T * inverse
+                here = slice(row * length + c, row * length + c + LANES)
+                cos_ref[here] = jnp.cos(angle)[:, :wide]
+                sin_ref[here] = (sign * jnp.sin(angle))[:, :wide]
+
+
+def first(grp, low, x, gain, w_query, w_key, w_value, w_out, ids, cid):
     pre_qkv, qkv = shard_args(low, (w_query, w_key, w_value), 1)
     pre_o, out = shard_args(low, (w_out,), 0)
     rows, width = x.shape
@@ -480,21 +628,28 @@
         qkv = [jnp.concatenate(qkv[i::2], axis=1) for i in range(2)]
     deep = w_query.shape[0] * grp.z_size
     thin = 3 * w_query.shape[1] // 2
+    table = sds((2 * ids.shape[0] * ids.shape[1], thin // 3), F32)
     return pl.pallas_call(
         functools.partial(first_kernel, grp, (pre_qkv, pre_o), len(qkv)),
         out_shape=[
             sds((rows * grp.size, width), BF16),
             sds((deep, thin), BF16),
             sds((w_out.shape[0] // 2, w_out.shape[1] * grp.z_size), BF16),
+            sds((2 * ids.shape[0], 1, ids.shape[1]), jnp.int32),
+            table,
+            table,
         ],
-        in_specs=[VMEM, VMEM] + [ANY] * (len(qkv) + len(out)),
-        out_specs=[ANY] * 3,
-        scratch_shapes=[pltpu.VMEM((rows, width), BF16)]
+        in_specs=[VMEM, VMEM] + [ANY] * (len(qkv) + len(out)) + [VMEM],
+        out_specs=[ANY] * 3 + [VMEM] * 3,
+        scratch_shapes=[
+            pltpu.VMEM((rows, width), BF16),
+            pltpu.VMEM((2,) + ids.shape, jnp.int32),
+        ]
         + gather_scratch(grp)
-        + spread_sems(grp, 4),
+        + spread_sems(grp, 5),
         compiler_params=params(cid),
         name="first",
-    )(x, gain, *qkv, *out)
+    )(x, gain, *qkv, *out, ids)
 
 
 def attend_rows(length, heads, q_ref, k_ref, v_ref, start_ref, o_ref, lse_ref, row):
@@ -590,7 +745,7 @@
     views = [
         (halves_of(grp, gate_ref, 1), wg_ref, 1),
         (halves_of(grp, up_ref, 1), wu_ref, 1),
-        (halves_of(grp, down_ref, 0), wd_ref, 0),
+        (top_rows(halves_of(grp, down_ref, 0), 0), wd_ref, 0),
     ]
     outer = Gather(grp, dy_ref, dyall_ref, dsend, drecv, dsem)
     outer_steps = outer.begin()
@@ -654,7 +809,7 @@
     def norm(part):
         h = x_ref[part].astype(F32) + summed[part].astype(F32)
         h_ref[part] = h
-        local[part] = (h * norm_scale(h) * gain_ref[...]).astype(BF16)
+        local[part] = (h * norm_scale(h) * gain_ref[...].astype(F32)).astype(BF16)
 
     tiles(x_ref.shape[0], norm)
     gather = Gather(grp, local, nm_ref, send, recv, sem)
@@ -681,7 +836,7 @@
             sds((total, width), BF16),
             sds((w_gate.shape[0] * grp.z_size, w_gate.shape[1] // 2), BF16),
             sds((w_up.shape[0] * grp.z_size, w_up.shape[1] // 2), BF16),
-            sds((w_down.shape[0] // 2, w_down.shape[1] * grp.z_size), BF16),
+            sds((w_down.shape[0] // 4, w_down.shape[1] * grp.z_size), BF16),
         ],
         in_specs=[ANY, VMEM, VMEM, VMEM, VMEM, VMEM, ANY, VMEM, VMEM, ANY, ANY, ANY],
         out_specs=[VMEM] * 6 + [ANY] * 5,
@@ -694,7 +849,7 @@
         + scatter_scratch(grp, rows, width)
         + gather_scratch(grp)
         + gather_scratch(grp)
-        + spread_sems(grp, 3),
+        + spread_sems(grp, 3 * PIECES),
         compiler_params=params(cid),
         name="middle",
     )(normed, wqkv, wo, cosine, sine, start, dy, x, gain, w_gate, w_up, w_down)
@@ -708,63 +863,552 @@
     return back, jnp.sum(grad * value * scale, axis=0, keepdims=True)
 
 
+def weave(parts, steps, each=1):
+    for part in parts:
+        part()
+        for step in steps[:each]:
+            step()
+        steps = steps[each:]
+    return steps
+
+
+def last_kernel(
+    grp,
+    heads,
+    branch_ref,
+    na_ref,
+    part_ref,
+    gup_ref,
+    q_ref,
+    k_ref,
+    v_ref,
+    o_ref,
+    lse_ref,
+    cos_ref,
+    sin_ref,
+    start_ref,
+    wqkv_ref,
+    wo_ref,
+    h_ref,
+    x_ref,
+    dh_ref,
+    gain_ref,
+    gm_ref,
+    out_ref,
+    tok_ref,
+    gains_ref,
+    gout_ref,
+    gqkv_ref,
+    upgot_ref,
+    outgot_ref,
+    qkvgot_ref,
+    p,
+    own,
+    ownsem,
+    rowbuf,
+    rowsem,
+    cols,
+    csem,
+    do,
+    dqkv,
+    dq,
+    dk,
+    dv,
+    gacc,
+    buf,
+    gs,
+    gr,
+    *rest,
+):
+    na_scat, rest = rest[:N_SCATTER], rest[N_SCATTER:]
+    out_scat, rest = rest[:N_SCATTER], rest[N_SCATTER:]
+    zs, zr = rest
+    rows_all, _, length = start_ref.shape
+    rows, width = h_ref.shape
+    wide = heads * HEAD
+    z, _ = grp.place()
+    n = rows_all // 2
+    order = [(1 - z % 2) * n + j for j in range(n)] + [(z % 2) * n + j for j in range(n)]
+    blocks = length // QB
+    step = cols.shape[2]
+
+    def load(i, j):
+        part = pl.ds(pl.multiple_of(order[i] * length + j * QB, QB), QB)
+        return pltpu.make_async_copy(branch_ref.at[part], rowbuf.at[j % 2], rowsem.at[j % 2])
+
+    def load_cols(c):
+        part = pl.ds(pl.multiple_of(c * step, step), step)
+        return pltpu.make_async_copy(na_ref.at[:, part], cols.at[c % 2], csem.at[c % 2])
+
+    load(0, 0).start()
+    load_cols(0).start()
+    outer = Scatter(grp, part_ref, rows, *out_scat, own=own)
+    for m in outer.masks(True) + outer.masks(False):
+        outer.load(m, ownsem).start()
+    grp.greet()
+    outer.begin(outer.masks(True) + outer.masks(False))
+    spread = Spread(grp, zs, zr)
+    spread_grad(grp, spread, gup_ref, upgot_ref, 0)
+    scat = Scatter(grp, p, rows, *na_scat)
+    gacc[...] = jnp.zeros_like(gacc)
+
+    def outer_core(m):
+        outer.load(m, ownsem).wait()
+        outer.core_step(m)
+
+    outer_steps = [
+        functools.partial(outer_core, m) for m in outer.masks(True) + outer.masks(False)
+    ]
+    outer_steps += outer.link_steps(True) + outer.link_steps(False)
+
+    def prepare(i):
+        base = order[i] * length
+        if i:
+            load(i, 0).start()
+        dk[...] = jnp.zeros_like(dk)
+        dv[...] = jnp.zeros_like(dv)
+
+        @pl.loop(0, blocks)
+        def _(j):
+            @pl.when(j + 1 < blocks)
+            def _():
+                load(i, j + 1).start()
+
+            load(i, j).wait()
+            there = pl.ds(pl.multiple_of(base + j * QB, QB), QB)
+            here = pl.ds(pl.multiple_of(j * QB, QB), QB)
+            branch = rowbuf[j % 2]
+            do[here] = dot_nt(branch, wo_ref[...]).astype(BF16)
+            gacc[...] += dot_tn(o_ref[there], branch)
+
+    def banded_back(i):
+        row = order[i]
+        base = row * length
+
+        def band(h, at, first, width, size):
+            lanes = slice(h * HEAD, (h + 1) * HEAD)
+            cols_at = pl.ds(pl.multiple_of(at, QB), size)
+            keys_at = pl.ds(pl.multiple_of(first, QB), width)
+            mine = pl.ds(pl.multiple_of(base + at, QB), size)
+            keys = pl.ds(pl.multiple_of(base + first, QB), width)
+            query = q_ref[mine, lanes]
+            key = k_ref[keys, lanes]
+            grad = do[cols_at, lanes]
+            scores = dot_nt(key, query * BF16(HEAD**-0.5))
+            mask = kept(start_ref[row, :, cols_at], at, size, first, width)
+            scores = jnp.where(mask, scores, -1e9)
+            weights = jnp.exp(scores - lse_ref[row, h : h + 1, cols_at])
+            dv[keys_at, lanes] += jnp.dot(weights.astype(BF16), grad, preferred_element_type=F32)
+            grad_weights = dot_nt(v_ref[keys, lanes], grad)
+            inner = jnp.sum(weights * grad_weights, axis=0, keepdims=True)
+            grad_scores = (weights * (grad_weights - inner)).astype(BF16)
+            dq[cols_at, lanes] = dot_tn(grad_scores, key)
+            dk[keys_at, lanes] += jnp.dot(grad_scores, query, preferred_element_type=F32)
+
+        return banded(length, heads, band)
+
+    def turn_back(i):
+        base = order[i] * length
+
+        @pl.loop(0, blocks)
+        def _(j):
+            there = pl.ds(pl.multiple_of(base + j * QB, QB), QB)
+            here = pl.ds(pl.multiple_of(j * QB, QB), QB)
+            cosine, sine = cos_ref[there], sin_ref[there]
+            query, key = dq[here] * HEAD**-0.5, dk[here] * HEAD**-0.5
+            dqkv[there, :wide] = (query * cosine - swap_halves(query) * sine).astype(BF16)
+            dqkv[there, wide : 2 * wide] = (key * cosine - swap_halves(key) * sine).astype(BF16)
+            dqkv[there, 2 * wide :] = dv[here].astype(BF16)
+            p[there] = dot_nt(dqkv[there], wqkv_ref[...]).astype(BF16)
+
+    def parts(i):
+        return (
+            [functools.partial(prepare, i)] + banded_back(i) + [functools.partial(turn_back, i)]
+        )
+
+    for i in range(n):
+        outer_steps = weave(parts(i), outer_steps)
+    scat.begin(scat.masks(True))
+    pair_core = scat.core_steps(True)
+    for i in range(n, 2 * n):
+        todo = parts(i)
+        merged = []
+        for a in range(len(todo)):
+            merged += [x[a] for x in (outer_steps, pair_core) if a < len(x)]
+        outer_steps, pair_core = outer_steps[len(todo) :], pair_core[len(todo) :]
+        merged = weave(todo, merged, 2)
+        outer_steps = merged + outer_steps
+    scat.begin(scat.masks(False))
+    gout_ref[...] = gacc[...].astype(BF16)
+    spread_grad(grp, spread, gout_ref, outgot_ref, 1)
+
+    def qkv_cols(c):
+        @pl.when(c + 1 < width // step)
+        def _():
+            load_cols(c + 1).start()
+
+        load_cols(c).wait()
+        part = pl.ds(pl.multiple_of(c * step, step), step)
+        gqkv_ref[part] = dot_tn(cols[c % 2], dqkv[...]).astype(BF16)
+
+    paced(width // step, qkv_cols, outer_steps + pair_core + scat.core_steps(False))
+    spread_grad(grp, spread, gqkv_ref, qkvgot_ref, 0)
+    run(scat.link_steps(True) + scat.link_steps(False))
+    outer.finish()
+    whole = outer.block(0)
+
+    def output(part):
+        out_ref[part] = (h_ref[part] + whole[part].astype(F32)).astype(BF16)
+
+    tiles(rows, output)
+    scat.finish()
+    summed = scat.block(0)
+    buf[0, 0:1] = jnp.zeros_like(gm_ref)
+    buf[0, 1:2] = gm_ref[...]
+
+    def back(part):
+        dn, gain_part = norm_back_tile(
+            x_ref[part].astype(F32), gain_ref[...].astype(F32), summed[part].astype(F32)
+        )
+        buf[0, 0:1] += gain_part
+        tok_ref[part] = (dh_ref[part] + dn).astype(BF16)
+
+    tiles(rows, back)
+    sum_gains(grp, buf, gs, gr)
+    gains_ref[...] = buf[buf.shape[0] - 1]
+    outer.drain()
+    scat.drain()
+    spread.wait()
+
+
+def sum_gains(grp, buf, send, recv):
+    hops = [grp.partner(b) for b in grp.bits if b != grp.pair]
+    bit = 1
+    while bit < grp.z_size:
+        hops.append(grp.across(bit))
+        bit *= 2
+    for i, hop in enumerate(hops):
+        c = pltpu.make_async_remote_copy(
+            src_ref=buf.at[2 * i],
+            dst_ref=buf.at[2 * i + 1],
+            send_sem=send.at[i],
+            recv_sem=recv.at[i],
+            device_id=hop,
+            device_id_type=MESH,
+        )
+        c.start()
+        c.wait()
+        buf[2 * i + 2] = buf[2 * i] + buf[2 * i + 1]
+
+
+def last(
+    grp, heads, branch, normed, part, grad_up, query, key, value, attended, lse, cosine, sine, start,
+    wqkv, wo, hidden, x, dh, gain, gain_m, cid,
+):
+    rows, width = x.shape
+    total = rows * grp.size
+    wide = heads * HEAD
+    length = start.shape[2]
+    hops = len(grp.bits) - 1 + (grp.z_size - 1).bit_length()
+    n = len(grp.masks)
+    gout, gqkv = sds((wide, width), BF16), sds((width, 3 * wide), BF16)
+    return pl.pallas_call(
+        functools.partial(last_kernel, grp, heads),
+        out_shape=[
+            sds((rows, width), BF16),
+            sds((rows, width), BF16),
+            sds((2, width), F32),
+            gout,
+            gqkv,
+            got_shape(grp, grad_up, 0),
+            got_shape(grp, gout, 1),
+            got_shape(grp, gqkv, 0),
+        ],
+        in_specs=[ANY] * 4 + [VMEM] * 15,
+        out_specs=[VMEM] * 5 + [ANY] * 3,
+        scratch_shapes=[
+            pltpu.VMEM((total, width), BF16),
+            pltpu.VMEM((n, rows, width), BF16),
+            pltpu.SemaphoreType.DMA((n,)),
+            pltpu.VMEM((2, QB, width), BF16),
+            pltpu.SemaphoreType.DMA((2,)),
+            pltpu.VMEM((2, total, cols_of(total)), BF16),
+            pltpu.SemaphoreType.DMA((2,)),
+            pltpu.VMEM((length, wide), BF16),
+            pltpu.VMEM((total, 3 * wide), BF16),
+            pltpu.VMEM((length, wide), F32),
+            pltpu.VMEM((length, wide), F32),
+            pltpu.VMEM((length, wide), F32),
+            pltpu.VMEM((wide, width), F32),
+            pltpu.VMEM((2 * hops + 1, 2, width), F32),
+            pltpu.SemaphoreType.DMA((hops,)),
+            pltpu.SemaphoreType.DMA((hops,)),
+        ]
+        + scatter_scratch(grp, rows, width)
+        + scatter_scratch(grp, rows, width)
+        + spread_sems(grp, 3 * PIECES),
+        compiler_params=params(cid),
+        name="last",
+    )(
+        branch, normed, part, grad_up, query, key, value, attended, lse, cosine, sine, start,
+        wqkv, wo, hidden, x, dh, gain, gain_m,
+    )
+
+
 def got_shape(grp, grad, axis):
     shape = list(grad.shape)
     shape[axis] //= grp.z_size
     return sds((grp.z_size - 1, *shape), BF16)
 
 
-def fourth_kernel(
-    grp, p_ref, h_ref, dy_ref, gain_ref, gdown_ref, ggate_ref, dh_ref, gm_ref, all_ref, down_ref, gate_ref, *rest
+def paced(count, body, steps, first=0):
+    turns = count - first
+    each = -(-len(steps) // turns) if steps else 0
+
+    @pl.loop(0, count)
+    def _(i):
+        body(i)
+        for k in range(turns):
+            mine = steps[k * each : (k + 1) * each]
+            if mine:
+
+                @pl.when(i == first + k)
+                def _(mine=mine):
+                    for step in mine:
+                        step()
+
+
+def cols_of(total):
+    return max(128, 655360 // total // 128 * 128)
+
+
+def mlp_kernel(
+    grp,
+    nm_ref,
+    dyall_ref,
+    wg_ref,
+    wu_ref,
+    top_ref,
+    h_ref,
+    dy_ref,
+    gain_ref,
+    down_ref,
+    dh_ref,
+    gm_ref,
+    gdown_ref,
+    ggate_ref,
+    gup_ref,
+    branch_ref,
+    out_ref,
+    downgot_ref,
+    gategot_ref,
+    p,
+    wd,
+    tile_n,
+    tsem,
+    act,
+    dgu,
+    cols,
+    csem,
+    dsem,
+    *rest,
 ):
-    p, psem, rest = rest[0], rest[1], rest[2:]
-    scat, rest = rest[:N_SCATTER], rest[N_SCATTER:]
-    local, send, recv, sem, zs, zr = rest
-    pltpu.make_async_copy(p_ref, p, psem).start()
+    scat_refs, rest = rest[:N_SCATTER], rest[N_SCATTER:]
+    send, recv, sem, zs, zr = rest
+    rows, width = h_ref.shape
+    size = 2 * rows
+    n = len(grp.masks)
+    units = wd.shape[0]
+    step = cols.shape[2]
+
+    def at(j):
+        return pl.ds(pl.multiple_of(grp.chip_at(j) * size, size), size)
+
+    def load(src, buf, k, j):
+        return pltpu.make_async_copy(src.at[at(j)], buf.at[j % 2], tsem.at[k, j % 2])
+
+    def load_cols(src, c):
+        part = pl.ds(pl.multiple_of(c * step, step), step)
+        return pltpu.make_async_copy(src.at[:, part], cols.at[c % 2], csem.at[c % 2])
+
+    load(nm_ref, tile_n, 0, 0).start()
     grp.greet()
     spread = Spread(grp, zs, zr)
-    spread_grad(grp, spread, gdown_ref, down_ref, 1)
-    spread_grad(grp, spread, ggate_ref, gate_ref, 0, grp.far)
-    pltpu.make_async_copy(p_ref, p, psem).wait()
-    acc = plain_scatter(grp, p, h_ref.shape[0], scat)
+    spread.to(0, lambda: (top_ref, wd.at[pl.ds(0, units // 2)]))
+    spread_weight(
+        grp,
+        spread,
+        top_rows(halves_of(grp, down_ref, 0), 1),
+        wd.at[pl.ds(units // 2, units // 2)],
+        0,
+        0,
+    )
+
+    def forward(j):
+        @pl.when(j + 1 < n)
+        def _():
+            load(nm_ref, tile_n, 0, j + 1).start()
+
+        load(nm_ref, tile_n, 0, j).wait()
+        normed = tile_n[j % 2]
+        gate = jnp.dot(normed, wg_ref[...], preferred_element_type=F32)
+        up = jnp.dot(normed, wu_ref[...], preferred_element_type=F32)
+        here = at(j)
+        act[here] = (gate * jax.nn.sigmoid(gate) * up).astype(BF16)
+        dgu[here, :units] = gate.astype(BF16)
+        dgu[here, units:] = up.astype(BF16)
+
+    load_cols(dyall_ref, 0).start()
+    paced(n, forward, [])
+    blocks = width // step
+
+    def down_cols(c):
+        @pl.when(c + 1 < blocks)
+        def _():
+            load_cols(dyall_ref, c + 1).start()
+
+        load_cols(dyall_ref, c).wait()
+        part = pl.ds(pl.multiple_of(c * step, step), step)
+        gdown_ref[:, part] = dot_tn(cols[c % 2], act[...]).T.astype(BF16)
+
+    load(dyall_ref, tile_n, 1, 0).start()
+    paced(blocks, down_cols, [])
+    spread.wait()
+    spread_grad(grp, spread, gdown_ref, downgot_ref, 1)
+
+    scat = Scatter(grp, p, rows, *scat_refs)
+    chunk = min(512, width)
+
+    def backward(j):
+        @pl.when(j + 1 < n)
+        def _():
+            load(dyall_ref, tile_n, 1, j + 1).start()
+
+        load(dyall_ref, tile_n, 1, j).wait()
+        here = at(j)
+        grad_act = dot_nt(tile_n[j % 2], wd[...])
+        gate, up = dgu[here, :units].astype(F32), dgu[here, units:].astype(F32)
+        sigma = jax.nn.sigmoid(gate)
+        grad_gate = (grad_act * up * (sigma * (1.0 + gate * (1.0 - sigma)))).astype(BF16)
+        grad_up = (grad_act * (gate * sigma)).astype(BF16)
+        dgu[here, :units] = grad_gate
+        dgu[here, units:] = grad_up
+        for c in range(0, width, chunk):
+            p[here, c : c + chunk] = (
+                dot_nt(grad_gate, wg_ref[c : c + chunk]) + dot_nt(grad_up, wu_ref[c : c + chunk])
+            ).astype(BF16)
+        scat.begin_tile(j)
+
+    core = scat.core_steps(True) + scat.core_steps(False)
+    pair_links = scat.link_steps(True)
+    todo = []
+    late = n // 2
+    share = -(-len(pair_links) // max(1, late - 1))
+    for j in range(1, n):
+        todo.append([core[j - 1]])
+        if j > late:
+            k = (j - late - 1) * share
+            todo[-1] += pair_links[k : k + share]
+    done = share * max(0, late - 1)
+    paced(n, backward, [functools.partial(run, x) for x in todo], 1)
+    rest_steps = [core[n - 1]] + pair_links[done:] + scat.link_steps(False)
+
+    def gate_up_cols(c):
+        @pl.when(c + 1 < blocks)
+        def _():
+            load_cols(nm_ref, c + 1).start()
+
+        load_cols(nm_ref, c).wait()
+        part = pl.ds(pl.multiple_of(c * step, step), step)
+        grads = dot_tn(cols[c % 2], dgu[...]).astype(BF16)
+        ggate_ref[part] = grads[:, :units]
+        gup_ref[part] = grads[:, units:]
+
+    load_cols(nm_ref, 0).start()
+    paced(blocks, gate_up_cols, rest_steps)
+    spread_grad(grp, spread, ggate_ref, gategot_ref, 0, grp.far)
+    dy = scat_refs[0].at[n - 1]
+    fetches = [
+        pltpu.make_async_copy(dy_ref, dy, dsem.at[0]),
+        pltpu.make_async_copy(h_ref, dh_ref, dsem.at[1]),
+    ]
+    for fetch in fetches:
+        fetch.start()
+    scat.finish()
+    summed = scat.block(0)
+    for fetch in fetches:
+        fetch.wait()
     gm_ref[...] = jnp.zeros_like(gm_ref)
 
-    def back(rows):
-        dn, gain_part = norm_back_tile(h_ref[rows], gain_ref[...], acc[rows].astype(F32))
+    def back(part):
+        dn, gain_part = norm_back_tile(dh_ref[part], gain_ref[...].astype(F32), summed[part].astype(F32))
         gm_ref[...] += gain_part
-        dh = dy_ref[rows].astype(F32) + dn
-        dh_ref[rows] = dh
-        local[rows] = dh.astype(BF16)
-
-    tiles(h_ref.shape[0], back)
-    staged_gather(
-        Gather(grp, local, all_ref, send, recv, sem),
-        lambda: spread_grad(grp, spread, ggate_ref, gate_ref, 0, (1,)),
-    )
+        dh = dy[part].astype(F32) + dn
+        dh_ref[part] = dh
+        summed[part] = dh.astype(BF16)
+
+    tiles(rows, back)
+    gather = Gather(grp, summed, branch_ref, send, recv, sem)
+    steps = gather.begin()
+    scat.drain()
+
+    def save(j):
+        return pltpu.make_async_copy(tile_n.at[j % 2], out_ref.at[at(j)], tsem.at[0, j % 2])
+
+    def branch(j):
+        @pl.when(j > 1)
+        def _():
+            save(j - 2).wait()
+
+        tile_n[j % 2] = jnp.dot(act[at(j)], wd[...], preferred_element_type=F32).astype(BF16)
+        save(j).start()
+
+    near = functools.partial(spread_grad, grp, spread, ggate_ref, gategot_ref, 0, (1,))
+    paced(n, branch, steps[:6] + [near] + steps[6:], 1)
+    save(n - 2).wait()
+    save(n - 1).wait()
+    gather.finish()
     spread.wait()
 
 
-def fourth(grp, part, hidden, out_grad, gain, grad_down, grad_gate, cid):
+def mlp(grp, normed, dy_all, wg, wu, wd_top, hidden, dy, gain, w_down, cid):
     rows, width = hidden.shape
+    total = rows * grp.size
+    n = len(grp.masks)
+    units = wg.shape[1]
+    gdown, ggate = sds((units, width), BF16), sds((width, units), BF16)
     return pl.pallas_call(
-        functools.partial(fourth_kernel, grp),
+        functools.partial(mlp_kernel, grp),
         out_shape=[
             sds((rows, width), F32),
             sds((1, width), F32),
-            sds((rows * grp.size, width), BF16),
-            got_shape(grp, grad_down, 1),
-            got_shape(grp, grad_gate, 0),
+            gdown,
+            ggate,
+            ggate,
+            sds((total, width), BF16),
+            sds((total, width), BF16),
+            got_shape(grp, gdown, 1),
+            got_shape(grp, ggate, 0),
         ],
-        in_specs=[ANY, VMEM, VMEM, VMEM, ANY, ANY],
-        out_specs=[VMEM, VMEM, ANY, ANY, ANY],
-        scratch_shapes=[pltpu.VMEM((rows * grp.size, width), BF16), pltpu.SemaphoreType.DMA]
+        in_specs=[ANY, ANY, VMEM, VMEM, ANY, ANY, ANY, VMEM, ANY],
+        out_specs=[VMEM] * 5 + [ANY] * 4,
+        scratch_shapes=[
+            pltpu.VMEM((total, width), BF16),
+            pltpu.VMEM((units, width), BF16),
+            pltpu.VMEM((2, 2 * rows, width), BF16),
+            pltpu.SemaphoreType.DMA((2, 2)),
+            pltpu.VMEM((total, units), BF16),
+            pltpu.VMEM((total, 2 * units), BF16),
+            pltpu.VMEM((2, total, cols_of(total)), BF16),
+            pltpu.SemaphoreType.DMA((2,)),
+            pltpu.SemaphoreType.DMA((2,)),
+        ]
         + scatter_scratch(grp, rows, width)
-        + [pltpu.VMEM((rows, width), BF16)]
         + gather_scratch(grp)
-        + spread_sems(grp, 2),
+        + spread_sems(grp, 4),
         compiler_params=params(cid),
-        name="fourth",
-    )(part, hidden, out_grad, gain, grad_down, grad_gate)
+        name="mlp",
+    )(normed, dy_all, wg, wu, wd_top, hidden, dy, gain, w_down)
 
 
 def fifth_kernel(grp, p_ref, h_ref, gup_ref, out_ref, up_ref, *rest):
@@ -818,30 +1462,14 @@
 
     def back(rows):
         dn, gain_part = norm_back_tile(
-            x_ref[rows].astype(F32), gain_ref[...], acc[rows].astype(F32)
+            x_ref[rows].astype(F32), gain_ref[...].astype(F32), acc[rows].astype(F32)
         )
         buf[0, 0:1] += gain_part
         tok_ref[rows] = (dh_ref[rows] + dn).astype(BF16)
 
     tiles(x_ref.shape[0], back)
-    hops = [grp.partner(b) for b in grp.bits if b != grp.pair]
-    bit = 1
-    while bit < grp.z_size:
-        hops.append(grp.across(bit))
-        bit *= 2
-    for i, hop in enumerate(hops):
-        c = pltpu.make_async_remote_copy(
-            src_ref=buf.at[2 * i],
-            dst_ref=buf.at[2 * i + 1],
-            send_sem=gs.at[i],
-            recv_sem=gr.at[i],
-            device_id=hop,
-            device_id_type=MESH,
-        )
-        c.start()
-        c.wait()
-        buf[2 * i + 2] = buf[2 * i] + buf[2 * i + 1]
-    gains_ref[...] = buf[2 * len(hops)]
+    sum_gains(grp, buf, gs, gr)
+    gains_ref[...] = buf[buf.shape[0] - 1]
     spread.wait()
 
 
@@ -962,6 +1590,54 @@
     )(query, key, value, grad, lse, cosine, sine, start)
 
 
+def finish_kernel(z_size, parts, z_ref, *refs):
+    low = z_ref[0] % 2
+    n = len(parts)
+    owns, gots, outs = refs[:n], refs[n : 2 * n], list(refs[2 * n :])
+    for own, got, (axis, count) in zip(owns, gots, parts):
+        sums = [own[...].astype(F32), None]
+        for m in range(1, z_size):
+            term = got[m - 1].astype(F32)
+            sums[m % 2] = term if sums[m % 2] is None else sums[m % 2] + term
+        if axis == 0:
+            out = outs.pop(0)
+            out[low] = sums[0]
+            out[1 - low] = sums[1]
+            continue
+        width = sums[0].shape[1] // count
+        for i in range(count):
+            out = outs.pop(0)
+            for which, total in ((low, sums[0]), (1 - low, sums[1])):
+                place = pl.ds(pl.multiple_of(which * width, width), width)
+                out[:, place] = total[:, i * width : (i + 1) * width]
+
+
+def finish(z_size, z, grads, gots, axes):
+    steps = 4
+    owns, blocks, outs, shapes = [], [], [], []
+    for grad, got, (axis, count) in zip(grads, gots, axes):
+        rows, cols = got.shape[1] // steps, got.shape[2]
+        if axis == 0:
+            owns.append(pl.BlockSpec((rows, cols), lambda i, z_ref: (i, z_ref[0])))
+            outs.append(pl.BlockSpec((2, rows, cols), lambda i, z_ref: (0, i, 0)))
+            shapes.append(sds((2, rows * steps, cols), F32))
+        else:
+            owns.append(pl.BlockSpec((rows, cols), lambda i, z_ref: (z_ref[0] * steps + i, 0)))
+            wide = 2 * cols // count
+            outs += [pl.BlockSpec((rows, wide), lambda i, z_ref: (i, 0))] * count
+            shapes += [sds((rows * steps, wide), F32)] * count
+        blocks.append(pl.BlockSpec((z_size - 1, rows, cols), lambda i, z_ref: (0, i, 0)))
+    return pl.pallas_call(
+        functools.partial(finish_kernel, z_size, axes),
+        out_shape=shapes,
+        grid_spec=pltpu.PrefetchScalarGridSpec(
+            num_scalar_prefetch=1, grid=(steps,), in_specs=owns + blocks, out_specs=outs
+        ),
+        compiler_params=pltpu.CompilerParams(vmem_limit_bytes=56 << 20),
+        name="finish",
+    )(jnp.reshape(z, (1,)), *grads, *gots)
+
+
 def shards(
     z_size,
     t_size,
@@ -982,9 +1658,6 @@
     z = lax.axis_index("fsdp")
     low = z % 2
 
-    def hop(value, mask):
-        return lax.ppermute(value, "fsdp", [(i, i ^ mask) for i in range(z_size)])
-
     def deliver(grad, got, half_axis, axis, parts=1):
         size = grad.shape[axis] // z_size
         sums = [lax.dynamic_slice_in_dim(grad, z * size, size, axis).astype(F32), None]
@@ -1007,27 +1680,12 @@
     wide = w_query.shape[1] // 2
     heads = wide // HEAD
 
-    other_ids = hop(segment_ids, 1)
-    segments = jnp.where(
-        low == 0,
-        jnp.concatenate([segment_ids, other_ids], axis=0),
-        jnp.concatenate([other_ids, segment_ids], axis=0),
+    gain_a = gain_attn[None, :]
+    gain_m = gain_mlp[None, :]
+    normed_a, wqkv, wo, start, cosine, sine = first(
+        grp, low, tokens, gain_a, w_query, w_key, w_value, w_out, segment_ids, 0
     )
-    rows, length = segments.shape
-    start = jnp.sum(segments[:, :, None] > segments[:, None, :], axis=2, dtype=jnp.int32)
-    position = (jnp.arange(length, dtype=jnp.int32)[None, :] - start).astype(F32)
-    lane = jnp.arange(wide, dtype=jnp.int32)
-    half = (lane % (HEAD // 2)).astype(F32)
-    inverse = jnp.exp(half * (-2.0 / HEAD) * math.log(ROPE_BASE))
-    angle = position.reshape(rows * length, 1) * inverse[None, :]
-    cosine = jnp.cos(angle)
-    sine = jnp.where(lane[None, :] % HEAD < HEAD // 2, -1.0, 1.0) * jnp.sin(angle)
-    start = start.reshape(rows, 1, length)
-
-    gain_a = gain_attn.astype(F32)[None, :]
-    gain_m = gain_mlp.astype(F32)[None, :]
-    normed_a, wqkv, wo = first(grp, low, tokens, gain_a, w_query, w_key, w_value, w_out, 0)
-    query, key, value, attended, lse, hidden, normed_m, grad_all, wg, wu, wd = middle(
+    query, key, value, attended, lse, hidden, normed_m, grad_all, wg, wu, wd_top = middle(
         grp,
         heads,
         normed_a,
@@ -1044,36 +1702,38 @@
         w_down,
         1,
     )
-    gate = jnp.dot(normed_m, wg, preferred_element_type=F32)
-    up = jnp.dot(normed_m, wu, preferred_element_type=F32)
-    sigma = jax.nn.sigmoid(gate)
-    silu_gate = gate * sigma
-    act = (silu_gate * up).astype(BF16)
-    grad_down = dot_tn(act, grad_all).astype(BF16)
-    grad_act = dot_nt(grad_all, wd)
-    grad_gate = (grad_act * up * (sigma * (1.0 + gate * (1.0 - sigma)))).astype(BF16)
-    grad_up = (grad_act * silu_gate).astype(BF16)
-    grad_wg = dot_tn(normed_m, grad_gate).astype(BF16)
-    grad_wu = dot_tn(normed_m, grad_up).astype(BF16)
-    grad_nm = (dot_nt(grad_gate, wg) + dot_nt(grad_up, wu)).astype(BF16)
-    grad_hidden, gain_m_part, branch_all, got_down, got_gate = fourth(
-        grp, grad_nm, hidden, out_grad, gain_m, grad_down, grad_wg, 3
+    grad_hidden, gain_m_part, grad_down, grad_wg, grad_wu, branch_all, out_part, got_down, got_gate = mlp(
+        grp, normed_m, grad_all, wg, wu, wd_top, hidden, out_grad, gain_m, w_down, 3
     )
-    out_part = jnp.dot(act, wd, preferred_element_type=F32).astype(BF16)
-    output, got_up = fifth(grp, out_part, hidden, grad_wu, 4)
-    grad_wout = dot_tn(attended, branch_all).astype(BF16)
-    grad_attended = dot_nt(branch_all, wo).astype(BF16)
-    grad_qkv = attend_back(query, key, value, grad_attended, lse, cosine, sine, start, heads)
-    grad_wqkv = dot_tn(normed_a, grad_qkv).astype(BF16)
-    grad_na = dot_nt(grad_qkv, wqkv).astype(BF16)
-    tokens_grad, gains, got_out, got_qkv = sixth(
-        grp, grad_na, tokens, grad_hidden, gain_a, gain_m_part, grad_wout, grad_wqkv, 5
-    )
-    (down_out,) = deliver(grad_down, got_down, 0, 1)
-    (gate_out,) = deliver(grad_wg, got_gate, 1, 0)
-    (up_out,) = deliver(grad_wu, got_up, 1, 0)
-    (out_out,) = deliver(grad_wout, got_out, 0, 1)
-    query_out, key_out, value_out = deliver(grad_wqkv, got_qkv, 1, 0, 3)
+    if grp.size <= 16:
+        output, tokens_grad, gains, grad_wout, grad_wqkv, got_up, got_out, got_qkv = last(
+            grp, heads, branch_all, normed_a, out_part, grad_wu, query, key, value, attended, lse,
+            cosine, sine, start, wqkv, wo, hidden, tokens, grad_hidden, gain_a, gain_m_part, 4,
+        )
+    else:
+        output, got_up = fifth(grp, out_part, hidden, grad_wu, 4)
+        grad_wout = dot_tn(attended, branch_all).astype(BF16)
+        grad_attended = dot_nt(branch_all, wo).astype(BF16)
+        grad_qkv = attend_back(query, key, value, grad_attended, lse, cosine, sine, start, heads)
+        grad_wqkv = dot_tn(normed_a, grad_qkv).astype(BF16)
+        grad_na = dot_nt(grad_qkv, wqkv).astype(BF16)
+        tokens_grad, gains, got_out, got_qkv = sixth(
+            grp, grad_na, tokens, grad_hidden, gain_a, gain_m_part, grad_wout, grad_wqkv, 5
+        )
+    grads = (grad_down, grad_wg, grad_wu, grad_wout, grad_wqkv)
+    gots = (got_down, got_gate, got_up, got_out, got_qkv)
+    axes = ((0, 1), (1, 1), (1, 1), (0, 1), (1, 3))
+    if wide % LANES == 0:
+        outs = finish(z_size, z, grads, gots, axes)
+        down_out, out_out = (x.reshape(-1, x.shape[2]) for x in (outs[0], outs[3]))
+        gate_out, up_out = outs[1:3]
+        query_out, key_out, value_out = outs[4:]
+    else:
+        (down_out,) = deliver(grad_down, got_down, 0, 1)
+        (gate_out,) = deliver(grad_wg, got_gate, 1, 0)
+        (up_out,) = deliver(grad_wu, got_up, 1, 0)
+        (out_out,) = deliver(grad_wout, got_out, 0, 1)
+        query_out, key_out, value_out = deliver(grad_wqkv, got_qkv, 1, 0, 3)
     return (
         output,
         tokens_grad,

time: 689 us -> 530 us (0.77)
  matrix products: 112 us -> 0 us
  other arithmetic: 36.3 us -> 0 us
  Pallas kernels: 523 us -> 516 us
    dot_general x13 -> x0, matrix products: 112 us -> none  [the longest x5 46 us: dot_nt(): lax.dot_general(left, right, (((1,), (1,)), ((), ())), preferred_element_...]
    pallas_call x1, Pallas kernels: 187 us -> 169 us  [middle(): pl.pallas_call(functools.partial(middle_kernel, grp, heads), out_shape=[t...]
    add x10 -> x0, other arithmetic: 16.6 us -> none  [deliver(): sums[m % 2] = term if sums[m % 2] is None else sums[m % 2] + term]
    select_n x9 -> x0, other arithmetic: 9.14 us -> none  [the longest x7 8.35 us: deliver(): jnp.where(low == 0, jnp.concatenate([a, b], axis=half_axis), jnp.concaten...]
    pallas_call x4 -> x3, Pallas kernels: 280 us -> 289 us  [the longest x1 141 us: last(): pl.pallas_call(functools.partial(last_kernel, grp, heads), out_shape=[sds...]
  transfers between devices with their start and end apart: 1 -> 0, of which waited for: 0 -> 0; matrix products, arithmetic and copies ran while one was open for 0% -> 0% of each run, Pallas kernels for 8% -> 0%
where the time goes in v3:
time: 530 us; the launch traced here: 521 us
  Pallas kernels  516 us (97%)
    pallas_call x1, Pallas kernels, middle(): pl.pallas_call(functools.partial(middle_kernel, grp, heads), out_shape=[t...  169 us
    pallas_call x1, Pallas kernels, last(): pl.pallas_call(functools.partial(last_kernel, grp, heads), out_shape=[sds...  141 us
    pallas_call x1, Pallas kernels, mlp(): pl.pallas_call(functools.partial(mlp_kernel, grp), out_shape=[sds((rows,...  141 us
    pallas_call x1, Pallas kernels, first(): pl.pallas_call(functools.partial(first_kernel, grp, (pre_qkv, pre_o), len...  57.1 us

profile of v3, /device:TPU:8, one launch (start us, length us, event | category | flops | bytes accessed | tf_op | source)
XLA Modules:
  0.0 521.3 jit_solution(7919449973746225914)
XLA Ops:
  0.6 1.3 broadcast_in_dim.6.gain_ref
  1.9 57.1 %first.1 = (bf16[2560,2048]{1,0:T(8,128)(2,1)}, bf16[2048,384]{1,0:T(8,128)(2,1)}, bf16[128,2048]{1,0:T(8,128)(2,1)}, s32[2,1,1280]{2,1,0:T(1,128)}, f32[2560,128]{1,0:T(8,128)}, /*index=5*/f32[2560,128]{1,0:T(8,128)}) custom-call(bf16[160,2048]{1,0:T(8,128)(2,1)} %x_ref.5, bf16[1,2048]{1,0:T(2,128)(2,1)} %broadcast_in_dim.6.gain_ref, ...), custom_call_target="tpu_custom_call" | custom-call | tf_op jit(solution)/shard_map/first/pallas_call | solution.py:632
  59.1 1.3 broadcast_in_dim.7.gain_ref
  60.3 169.2 %middle.1 = (bf16[2560,128]{1,0:T(8,128)(2,1)}, bf16[2560,128]{1,0:T(8,128)(2,1)}, bf16[2560,128]{1,0:T(8,128)(2,1)}, bf16[2560,128]{1,0:T(8,128)(2,1)}, f32[2,2...) custom-call(bf16[2560,2048]{1,0:T(8,128)(2,1)} %get-tuple-element.52, ...), custom_call_target="tpu_custom_call" | custom-call | tf_op jit(solution)/shard_map/middle/pallas_call | solution.py:829
  229.5 140.8 %mlp.1 = (f32[160,2048]{1,0:T(8,128)}, f32[1,2048]{1,0:T(1,128)}, bf16[512,2048]{1,0:T(8,128)(2,1)}, bf16[2048,512]{1,0:T(8,128)(2,1)}, bf16[2048,512]{1,0:T(8,1...) custom-call(bf16[2560,2048]{1,0:T(8,128)(2,1)} %get-tuple-element.58, ...), custom_call_target="tpu_custom_call" | custom-call | tf_op jit(solution)/shard_map/mlp/pallas_call | solution.py:1380
  370.3 141.2 %last.1 = (bf16[160,2048]{1,0:T(8,128)(2,1)}, bf16[160,2048]{1,0:T(8,128)(2,1)}, f32[2,2048]{1,0:T(2,128)}, bf16[128,2048]{1,0:T(8,128)(2,1)}, bf16[2048,384]{1,...) custom-call(bf16[2560,2048]{1,0:T(8,128)(2,1)} %get-tuple-element.64.branc, ...), custom_call_target="tpu_custom_call" | custom-call | tf_op jit(solution)/shard_map/last/pallas_call | solution.py:1115
  511.5 0.0 copy-start.2
  511.5 0.0 copy-start.1
  511.6 0.0 copy-start
  511.6 7.3 %finish.1 = (f32[2,512,512]{2,1,0:T(8,128)}, f32[512,1024]{1,0:T(8,128)}, f32[512,1024]{1,0:T(8,128)}, f32[2,128,512]{2,1,0:T(8,128)}, f32[512,256]{1,0:T(8,128)...) custom-call(s32[1]{0:T(128)} %bitcast.2.z_ref, bf16[512,2048]{1,0:T(8,128)(2,1)} %get-tuple-element.77.refs_0_, ...), custom_call_target="tpu_custom_call" | custom-call | tf_op jit(solution)/shard_map/finish/pallas_call | solution.py:1630
  518.8 0.0 copy-done.2
  518.8 0.6 fusion
  519.5 0.0 copy-done.1
  519.5 0.8 copy.25
  520.3 0.0 copy-done
  520.3 0.8 copy.26
Async XLA Ops:
  511.5 7.3 %copy-start.2 = (f32[2,2048]{1,0:T(2,128)S(1)}, f32[2,2048]{1,0:T(2,128)}, u32[]{:S(2)}) copy-start(f32[2,2048]{1,0:T(2,128)} %get-tuple-element.76) | copy-start | bytes 49156
  511.5 7.9 %copy-start.1 = (bf16[160,2048]{1,0:T(8,128)(2,1)S(1)}, bf16[160,2048]{1,0:T(8,128)(2,1)}, u32[]{:S(2)}) copy-start(bf16[160,2048]{1,0:T(8,128)(2,1)} %get-tuple-element.106) | copy-start | bytes 1966084
  511.6 8.8 %copy-start = (bf16[160,2048]{1,0:T(8,128)(2,1)S(1)}, bf16[160,2048]{1,0:T(8,128)(2,1)}, u32[]{:S(2)}) copy-start(bf16[160,2048]{1,0:T(8,128)(2,1)} %get-tuple-element.107) | copy-start | bytes 1966084

commit v4 on v3

--- a/solution.py
+++ b/solution.py
@@ -90,9 +90,21 @@
             bit *= 2
         return (z, t)
 
-    def greet(self):
+    def beside(self, mask):
+        z, t = self.place()
+        bit = 1
+        while bit < self.t_size:
+            if mask & bit:
+                t = flip(t, bit)
+            bit *= 2
+        return (z, t)
+
+    def greet(self, everyone=False):
         barrier = pltpu.get_barrier_semaphore()
-        peers = [self.partner(b) for b in self.bits if b != self.pair]
+        if everyone:
+            peers = [self.beside(m) for m in range(1, self.t_size)]
+        else:
+            peers = [self.partner(b) for b in self.bits if b != self.pair]
         peers += [self.across(m) for m in range(1, self.z_size)]
         for peer in peers:
             pl.semaphore_signal(barrier, inc=1, device_id=peer, device_id_type=MESH)
@@ -612,12 +624,18 @@
                 start = jnp.maximum(start, jnp.where(place >= step, pltpu.roll(start, step, 1), 0))
                 step *= 2
             start_ref[row] = start
-            position = (place - start).astype(F32)
-            for c in range(0, length, LANES):
-                angle = jnp.broadcast_to(position[:, c : c + LANES], (LANES, LANES)).T * inverse
-                here = slice(row * length + c, row * length + c + LANES)
-                cos_ref[here] = jnp.cos(angle)[:, :wide]
-                sin_ref[here] = (sign * jnp.sin(angle))[:, :wide]
+
+    @pl.loop(0, planes * rows)
+    def _(row):
+        @pl.loop(0, length // LANES)
+        def _(c):
+            here = pl.ds(pl.multiple_of(c * LANES, LANES), LANES)
+            token = c * LANES + lax.broadcasted_iota(jnp.int32, (1, LANES), 1)
+            position = (token - start_ref[row, :, here]).astype(F32)
+            angle = jnp.broadcast_to(position, (LANES, LANES)).T * inverse
+            there = pl.ds(pl.multiple_of(row * length + c * LANES, LANES), LANES)
+            cos_ref[there] = jnp.cos(angle)[:, :wide]
+            sin_ref[there] = (sign * jnp.sin(angle))[:, :wide]
 
 
 def first(grp, low, x, gain, w_query, w_key, w_value, w_out, ids, cid):
@@ -945,7 +963,7 @@
     outer = Scatter(grp, part_ref, rows, *out_scat, own=own)
     for m in outer.masks(True) + outer.masks(False):
         outer.load(m, ownsem).start()
-    grp.greet()
+    grp.greet(everyone=True)
     outer.begin(outer.masks(True) + outer.masks(False))
     spread = Spread(grp, zs, zr)
     spread_grad(grp, spread, gup_ref, upgot_ref, 0)
@@ -1081,24 +1099,40 @@
     spread.wait()
 
 
+def gain_scratch(grp, width):
+    n = grp.t_size + grp.z_size - 2
+    return [
+        pltpu.VMEM((grp.t_size + grp.z_size + 3, 2, width), F32),
+        pltpu.SemaphoreType.DMA((n,)),
+        pltpu.SemaphoreType.DMA((n,)),
+    ]
+
+
 def sum_gains(grp, buf, send, recv):
-    hops = [grp.partner(b) for b in grp.bits if b != grp.pair]
-    bit = 1
-    while bit < grp.z_size:
-        hops.append(grp.across(bit))
-        bit *= 2
-    for i, hop in enumerate(hops):
-        c = pltpu.make_async_remote_copy(
-            src_ref=buf.at[2 * i],
-            dst_ref=buf.at[2 * i + 1],
-            send_sem=send.at[i],
-            recv_sem=recv.at[i],
-            device_id=hop,
-            device_id_type=MESH,
-        )
-        c.start()
-        c.wait()
-        buf[2 * i + 2] = buf[2 * i] + buf[2 * i + 1]
+    z, t = grp.place()
+    at, sem = 0, 0
+    for index, size, peer in ((t, grp.t_size, grp.beside), (z, grp.z_size, grp.across)):
+        copies = []
+        for m in range(1, size):
+            c = pltpu.make_async_remote_copy(
+                src_ref=buf.at[at],
+                dst_ref=buf.at[at + 1 + index],
+                send_sem=send.at[sem],
+                recv_sem=recv.at[sem],
+                device_id=peer(m),
+                device_id_type=MESH,
+            )
+            c.start()
+            copies.append(c)
+            sem += 1
+        buf[at + 1 + index] = buf[at]
+        for c in copies:
+            c.wait()
+        total = buf[at + 1]
+        for i in range(1, size):
+            total = total + buf[at + 1 + i]
+        at += size + 1
+        buf[at] = total
 
 
 def last(
@@ -1109,7 +1143,6 @@
     total = rows * grp.size
     wide = heads * HEAD
     length = start.shape[2]
-    hops = len(grp.bits) - 1 + (grp.z_size - 1).bit_length()
     n = len(grp.masks)
     gout, gqkv = sds((wide, width), BF16), sds((width, 3 * wide), BF16)
     return pl.pallas_call(
@@ -1140,10 +1173,8 @@
             pltpu.VMEM((length, wide), F32),
             pltpu.VMEM((length, wide), F32),
             pltpu.VMEM((wide, width), F32),
-            pltpu.VMEM((2 * hops + 1, 2, width), F32),
-            pltpu.SemaphoreType.DMA((hops,)),
-            pltpu.SemaphoreType.DMA((hops,)),
         ]
+        + gain_scratch(grp, width)
         + scatter_scratch(grp, rows, width)
         + scatter_scratch(grp, rows, width)
         + spread_sems(grp, 3 * PIECES),
@@ -1326,7 +1357,6 @@
 
     load_cols(nm_ref, 0).start()
     paced(blocks, gate_up_cols, rest_steps)
-    spread_grad(grp, spread, ggate_ref, gategot_ref, 0, grp.far)
     dy = scat_refs[0].at[n - 1]
     fetches = [
         pltpu.make_async_copy(dy_ref, dy, dsem.at[0]),
@@ -1350,6 +1380,7 @@
     tiles(rows, back)
     gather = Gather(grp, summed, branch_ref, send, recv, sem)
     steps = gather.begin()
+    spread_grad(grp, spread, ggate_ref, gategot_ref, 0, grp.far)
     scat.drain()
 
     def save(j):
@@ -1451,7 +1482,7 @@
     scat, rest = rest[:N_SCATTER], rest[N_SCATTER:]
     buf, gs, gr, zs, zr = rest
     pltpu.make_async_copy(p_ref, p, psem).start()
-    grp.greet()
+    grp.greet(everyone=True)
     spread = Spread(grp, zs, zr)
     spread_grad(grp, spread, gout_ref, o_ref, 1)
     spread_grad(grp, spread, gqkv_ref, qkv_ref, 0)
@@ -1475,7 +1506,6 @@
 
 def sixth(grp, part, x, dh, gain, gain_m, grad_out, grad_qkv, cid):
     rows, width = x.shape
-    n = len(grp.bits) - 1 + (grp.z_size - 1).bit_length()
     return pl.pallas_call(
         functools.partial(sixth_kernel, grp),
         out_shape=[
@@ -1488,11 +1518,7 @@
         out_specs=[VMEM, VMEM, ANY, ANY],
         scratch_shapes=[pltpu.VMEM((rows * grp.size, width), BF16), pltpu.SemaphoreType.DMA]
         + scatter_scratch(grp, rows, width)
-        + [
-            pltpu.VMEM((2 * n + 1, 2, width), F32),
-            pltpu.SemaphoreType.DMA((n,)),
-            pltpu.SemaphoreType.DMA((n,)),
-        ]
+        + gain_scratch(grp, width)
         + spread_sems(grp, 2),
         compiler_params=params(cid),
         name="sixth",

time: 530 us -> 511 us (0.964); the launches traced: 521 us -> 508 us
  Pallas kernels: 516 us -> 502 us
    pallas_call x1, Pallas kernels: 141 us -> 133 us  [last(): pl.pallas_call(functools.partial(last_kernel, grp, heads), out_shape=[sds...]
where the time goes in v4:
time: 511 us; the launch traced here: 508 us
  Pallas kernels  502 us (98%)
    pallas_call x1, Pallas kernels, middle(): pl.pallas_call(functools.partial(middle_kernel, grp, heads), out_shape=[t...  169 us
    pallas_call x1, Pallas kernels, mlp(): pl.pallas_call(functools.partial(mlp_kernel, grp), out_shape=[sds((rows,...  136 us
    pallas_call x1, Pallas kernels, last(): pl.pallas_call(functools.partial(last_kernel, grp, heads), out_shape=[sds...  133 us
    pallas_call x1, Pallas kernels, first(): pl.pallas_call(functools.partial(first_kernel, grp, (pre_qkv, pre_o), len...  57.1 us

profile of v4, /device:TPU:8, one launch (start us, length us, event | category | flops | bytes accessed | tf_op | source)
XLA Modules:
  0.0 507.7 jit_solution(10250642703723185014)
XLA Ops:
  0.6 1.3 broadcast_in_dim.6.gain_ref
  1.9 57.1 %first.1 = (bf16[2560,2048]{1,0:T(8,128)(2,1)}, bf16[2048,384]{1,0:T(8,128)(2,1)}, bf16[128,2048]{1,0:T(8,128)(2,1)}, s32[2,1,1280]{2,1,0:T(1,128)}, f32[2560,128]{1,0:T(8,128)}, /*index=5*/f32[2560,128]{1,0:T(8,128)}) custom-call(bf16[160,2048]{1,0:T(8,128)(2,1)} %x_ref.5, bf16[1,2048]{1,0:T(2,128)(2,1)} %broadcast_in_dim.6.gain_ref, ...), custom_call_target="tpu_custom_call" | custom-call | tf_op jit(solution)/shard_map/first/pallas_call | solution.py:650
  59.1 1.3 broadcast_in_dim.7.gain_ref
  60.3 169.2 %middle.1 = (bf16[2560,128]{1,0:T(8,128)(2,1)}, bf16[2560,128]{1,0:T(8,128)(2,1)}, bf16[2560,128]{1,0:T(8,128)(2,1)}, bf16[2560,128]{1,0:T(8,128)(2,1)}, f32[2,2...) custom-call(bf16[2560,2048]{1,0:T(8,128)(2,1)} %get-tuple-element.52, ...), custom_call_target="tpu_custom_call" | custom-call | tf_op jit(solution)/shard_map/middle/pallas_call | solution.py:847
  229.5 135.7 %mlp.1 = (f32[160,2048]{1,0:T(8,128)}, f32[1,2048]{1,0:T(1,128)}, bf16[512,2048]{1,0:T(8,128)(2,1)}, bf16[2048,512]{1,0:T(8,128)(2,1)}, bf16[2048,512]{1,0:T(8,1...) custom-call(bf16[2560,2048]{1,0:T(8,128)(2,1)} %get-tuple-element.58, ...), custom_call_target="tpu_custom_call" | custom-call | tf_op jit(solution)/shard_map/mlp/pallas_call | solution.py:1411
  365.2 132.9 %last.1 = (bf16[160,2048]{1,0:T(8,128)(2,1)}, bf16[160,2048]{1,0:T(8,128)(2,1)}, f32[2,2048]{1,0:T(2,128)}, bf16[128,2048]{1,0:T(8,128)(2,1)}, bf16[2048,384]{1,...) custom-call(bf16[2560,2048]{1,0:T(8,128)(2,1)} %get-tuple-element.64.branc, ...), custom_call_target="tpu_custom_call" | custom-call | tf_op jit(solution)/shard_map/last/pallas_call | solution.py:1148
  498.1 0.0 copy-start.2
  498.1 0.0 copy-start.1
  498.1 0.0 copy-start
  498.1 7.3 %finish.1 = (f32[2,512,512]{2,1,0:T(8,128)}, f32[512,1024]{1,0:T(8,128)}, f32[512,1024]{1,0:T(8,128)}, f32[2,128,512]{2,1,0:T(8,128)}, f32[512,256]{1,0:T(8,128)...) custom-call(s32[1]{0:T(128)} %bitcast.2.z_ref, bf16[512,2048]{1,0:T(8,128)(2,1)} %get-tuple-element.77.refs_0_, ...), custom_call_target="tpu_custom_call" | custom-call | tf_op jit(solution)/shard_map/finish/pallas_call | solution.py:1656
  505.4 0.0 copy-done.2
  505.4 0.6 fusion
  506.0 0.0 copy-done.1
  506.0 0.8 copy.25
  506.9 0.0 copy-done
  506.9 0.8 copy.26
Async XLA Ops:
  498.1 7.3 %copy-start.2 = (f32[2,2048]{1,0:T(2,128)S(1)}, f32[2,2048]{1,0:T(2,128)}, u32[]{:S(2)}) copy-start(f32[2,2048]{1,0:T(2,128)} %get-tuple-element.76) | copy-start | bytes 49156
  498.1 7.9 %copy-start.1 = (bf16[160,2048]{1,0:T(8,128)(2,1)S(1)}, bf16[160,2048]{1,0:T(8,128)(2,1)}, u32[]{:S(2)}) copy-start(bf16[160,2048]{1,0:T(8,128)(2,1)} %get-tuple-element.106) | copy-start | bytes 1966084
  498.1 8.8 %copy-start = (bf16[160,2048]{1,0:T(8,128)(2,1)S(1)}, bf16[160,2048]{1,0:T(8,128)(2,1)}, u32[]{:S(2)}) copy-start(bf16[160,2048]{1,0:T(8,128)(2,1)} %get-tuple-element.107) | copy-start | bytes 1966084

commit v5 on v4

--- a/solution.py
+++ b/solution.py
@@ -64,9 +64,9 @@
                 r = flip(r, b)
         return r
 
-    def chip_at(self, j):
+    def chip_at(self, j, near=False):
         chip = self.rank() // 2
-        mask = len(self.masks) - 1 - j
+        mask = j if near else len(self.masks) - 1 - j
         out = 0
         bit = 1
         while bit < len(self.masks):
@@ -173,6 +173,7 @@
         if len(plain) > 3:
             plain.remove(grp.pair)
             plain.insert(2, grp.pair)
+        self.plain = plain
 
         def step(h, m):
             self.arrived(h, m)
@@ -184,11 +185,31 @@
             for h in range(2)
         ]
 
+    def chip_arrived(self, mask):
+        for h in range(2):
+            self.arrived(h, mask | self.grp.core)
+        if mask == 0:
+            self.own.wait()
+
+    def needs(self, steps):
+        plain = self.plain
+        done = 0
+        out = []
+        for m in sorted(self.grp.masks):
+            upto = done
+            if m:
+                other = next(k for k in plain if mirror(self.grp, k) == m)
+                upto = 2 * (max(plain.index(m), plain.index(other)) + 1)
+            out.append(steps[done : max(done, upto)] + [functools.partial(self.chip_arrived, m)])
+            done = max(done, upto)
+        return out
+
     def finish(self):
         for m in self.grp.masks:
-            for h in range(2):
-                self.arrived(h, m | self.grp.core)
-        self.own.wait()
+            self.chip_arrived(m)
+        self.drain()
+
+    def drain(self):
         for sent in self.sent:
             self.own_copy(*sent).wait_send()
 
@@ -375,7 +396,7 @@
         self.used = 0
         self.makers = []
 
-    def to(self, mask, views):
+    def to(self, mask, views, start=True):
         k = self.used
         self.used += 1
 
@@ -392,8 +413,10 @@
                 device_id_type=MESH,
             )
 
-        make().start()
+        if start:
+            make().start()
         self.makers.append(make)
+        return make
 
     def wait(self):
         self.wait_first(len(self.makers))
@@ -408,9 +431,10 @@
     return [pltpu.SemaphoreType.DMA((grp.z_size * parts,))] * 2
 
 
-def spread_weight(grp, spread, shard, whole, half_axis, at, masks=None):
+def spread_weight(grp, spread, shard, whole, half_axis, at, masks=None, start=True):
     axis = 1 - half_axis
     mine, other = shard
+    makers = []
     for m in grp.far + (0, 1) if masks is None else masks:
 
         def views(src=other if m % 2 else mine):
@@ -421,7 +445,8 @@
                 return src, whole.at[place, at : at + width]
             return src, whole.at[at : at + width, place]
 
-        spread.to(m, views)
+        makers.append(spread.to(m, views, start))
+    return makers
 
 
 def halves_of(grp, ref, axis):
@@ -495,12 +520,8 @@
 PIECES = 1
 
 
-def top_rows(views, which):
-    size = views[0].shape[0] // 2
-    return [v.at[pl.ds(which * size, size)] for v in views]
-
-
-def spread_grad(grp, spread, grad, got, axis, masks=None):
+def spread_grad(grp, spread, grad, got, axis, masks=None, start=True):
+    makers = []
     for m in grp.far + (1,) if masks is None else masks:
 
         def views(m=m):
@@ -508,7 +529,25 @@
             part = pl.ds(pl.multiple_of(grp.across(m)[0] * size, size), size)
             return (grad.at[part] if axis == 0 else grad.at[:, part]), got.at[m - 1]
 
-        spread.to(m, views)
+        makers.append(spread.to(m, views, start))
+    return makers
+
+
+def launch(makers, where=None):
+    if where is None:
+        for make in makers:
+            make().start()
+    else:
+
+        @pl.when(where)
+        def _():
+            for make in makers:
+                make().start()
+
+
+def inner_plane(grp):
+    z, _ = grp.place()
+    return (z * 4 >= grp.z_size) & (z * 4 < 3 * grp.z_size)
 
 
 def staged_gather(gather, after_pair):
@@ -714,6 +753,7 @@
 def middle_kernel(
     grp,
     heads,
+    fused,
     na_ref,
     wqkv_ref,
     wo_ref,
@@ -737,12 +777,14 @@
     wg_ref,
     wu_ref,
     wd_ref,
-    p,
-    rowbuf,
-    rowsem,
-    local,
     *rest,
 ):
+    early, rest = (rest[:2], rest[2:]) if fused else (None, rest)
+    p, rowbuf, rowsem, local = rest[:4]
+    rest = rest[4:]
+    if fused:
+        wg, wu, tile, tilesem, stage_a, stage_g, stagesem = rest[:7]
+        rest = rest[7:]
     scat_refs, rest = rest[:N_SCATTER], rest[N_SCATTER:]
     dsend, drecv, dsem, send, recv, sem, zs, zr = rest
     rows_all, _, length = start_ref.shape
@@ -763,13 +805,20 @@
     views = [
         (halves_of(grp, gate_ref, 1), wg_ref, 1),
         (halves_of(grp, up_ref, 1), wu_ref, 1),
-        (top_rows(halves_of(grp, down_ref, 0), 0), wd_ref, 0),
+        (halves_of(grp, down_ref, 0), wd_ref, 0),
     ]
     outer = Gather(grp, dy_ref, dyall_ref, dsend, drecv, dsem)
     outer_steps = outer.begin()
-    for masks in (grp.far, (0, 1)):
-        for pair, whole, axis in views:
-            spread_weight(grp, spread, pair, whole, axis, 0, masks)
+    for pair, whole, axis in views[:2]:
+        spread_weight(grp, spread, pair, whole, axis, 0, (1, 0))
+    far = []
+    for pair, whole, axis in views[:2]:
+        far += spread_weight(grp, spread, pair, whole, axis, 0, grp.far, start=False)
+    inner = inner_plane(grp)
+    outer_plane = jnp.logical_not(inner)
+    cut = len(far) // 2
+    launch(far[:cut])
+    launch(far[cut:], inner)
     scat = Scatter(grp, p, x_ref.shape[0], *scat_refs)
 
     def project(i):
@@ -807,20 +856,20 @@
             + [functools.partial(branch, i)]
         )
 
-    for i in range(n):
-        run(parts(i))
+    todo = [part for i in range(n) for part in parts(i)]
+    wait = max(0, len(todo) - 4)
+    run(todo[:wait])
+    outer_steps = weave(todo[wait:], outer_steps)
     scat.begin(scat.masks(True))
-    run(outer_steps[:4])
-    pair_steps = scat.core_steps(True)
-    for i in range(n, 2 * n):
-        todo = parts(i)
-        run(todo, pair_steps)
-        pair_steps = pair_steps[len(todo) :]
+    todo = [part for i in range(n, 2 * n) for part in parts(i)]
+    links = scat.link_steps(True)
+    beside = scat.core_steps(True) + links[:-2]
+    beside = weave(todo, beside, -(-len(beside) // len(todo)))
     scat.begin(scat.masks(False))
-    run(pair_steps or [lambda: None])
-    run(scat.core_steps(False), outer_steps[4:8])
-    run(scat.link_steps(True), outer_steps[8:])
-    run(scat.link_steps(False))
+    run(beside + scat.core_steps(False)[:1] + links[-2:])
+    launch(far[cut:], outer_plane)
+    run(scat.core_steps(False)[1:])
+    run(scat.link_steps(False), outer_steps)
     scat.finish()
     summed = scat.block(0)
 
@@ -831,10 +880,61 @@
 
     tiles(x_ref.shape[0], norm)
     gather = Gather(grp, local, nm_ref, send, recv, sem)
-    run(gather.begin())
+    steps = gather.begin()
+    pair, whole, axis = views[2]
+    spread_weight(grp, spread, pair, whole, axis, 0)
+    if not fused:
+        run(steps)
+        scat.drain()
+        outer.finish()
+        gather.finish()
+        spread.wait()
+        return
+    spread.wait_first(2 * grp.z_size)
+    loads = [
+        pltpu.make_async_copy(src, dst, tilesem.at[i])
+        for i, (src, dst) in enumerate(((wg_ref, wg), (wu_ref, wu)))
+    ]
+    for c in loads:
+        c.start()
     scat.drain()
+    for c in loads:
+        c.wait()
+    size = tile.shape[0]
+    units = wg.shape[1]
+
+    def saves(j):
+        here = pl.ds(pl.multiple_of(grp.chip_at(j, near=True) * size, size), size)
+        return (
+            pltpu.make_async_copy(stage_a.at[j % 2], early[0].at[here], stagesem.at[0, j % 2]),
+            pltpu.make_async_copy(stage_g.at[j % 2], early[1].at[here], stagesem.at[1, j % 2]),
+        )
+
+    def forward(j):
+        here = pl.ds(pl.multiple_of(grp.chip_at(j, near=True) * size, size), size)
+        load = pltpu.make_async_copy(nm_ref.at[here], tile, tilesem.at[0])
+        load.start()
+
+        @pl.when(j > 1)
+        def _():
+            for c in saves(j - 2):
+                c.wait()
+
+        load.wait()
+        act, gate, up = gate_up(tile[...], wg[...], wu[...])
+        stage_a[j % 2] = act
+        stage_g[j % 2, :, :units] = gate
+        stage_g[j % 2, :, units:] = up
+        for c in saves(j):
+            c.start()
+
+    count = len(grp.masks)
+    led(count, forward, gather.needs(steps))
+    for j in (count - 2, count - 1):
+        for c in saves(j):
+            c.wait()
     outer.finish()
-    gather.finish()
+    gather.drain()
     spread.wait()
 
 
@@ -844,8 +944,22 @@
     wide = heads * HEAD
     rows_all, _, length = start.shape
     thin = sds((total, wide), BF16)
+    fused = grp.size <= 16
+    units = w_gate.shape[1] // 2
+    early, beside = [], []
+    if fused:
+        early = [sds((total, units), BF16), sds((total, 2 * units), BF16)]
+        beside = [
+            pltpu.VMEM((width, units), BF16),
+            pltpu.VMEM((width, units), BF16),
+            pltpu.VMEM((2 * rows, width), BF16),
+            pltpu.SemaphoreType.DMA((2,)),
+            pltpu.VMEM((2, 2 * rows, units), BF16),
+            pltpu.VMEM((2, 2 * rows, 2 * units), BF16),
+            pltpu.SemaphoreType.DMA((2, 2)),
+        ]
     return pl.pallas_call(
-        functools.partial(middle_kernel, grp, heads),
+        functools.partial(middle_kernel, grp, heads, fused),
         out_shape=[thin] * 4
         + [
             sds((rows_all, heads, length), F32),
@@ -854,16 +968,18 @@
             sds((total, width), BF16),
             sds((w_gate.shape[0] * grp.z_size, w_gate.shape[1] // 2), BF16),
             sds((w_up.shape[0] * grp.z_size, w_up.shape[1] // 2), BF16),
-            sds((w_down.shape[0] // 4, w_down.shape[1] * grp.z_size), BF16),
-        ],
+            sds((w_down.shape[0] // 2, w_down.shape[1] * grp.z_size), BF16),
+        ]
+        + early,
         in_specs=[ANY, VMEM, VMEM, VMEM, VMEM, VMEM, ANY, VMEM, VMEM, ANY, ANY, ANY],
-        out_specs=[VMEM] * 6 + [ANY] * 5,
+        out_specs=[VMEM] * 6 + [ANY] * (5 + len(early)),
         scratch_shapes=[
             pltpu.VMEM((total, width), BF16),
             pltpu.VMEM((2, QB, width), BF16),
             pltpu.SemaphoreType.DMA((2,)),
             pltpu.VMEM((rows, width), BF16),
         ]
+        + beside
         + scatter_scratch(grp, rows, width)
         + gather_scratch(grp)
         + gather_scratch(grp)
@@ -1209,41 +1325,60 @@
                         step()
 
 
+def led(count, body, lists):
+    @pl.loop(0, count)
+    def _(i):
+        for k, steps in enumerate(lists):
+
+            @pl.when(i == k)
+            def _(steps=steps):
+                run(steps)
+
+        body(i)
+
+
+def gate_up(normed, wg, wu):
+    gate = jnp.dot(normed, wg, preferred_element_type=F32)
+    up = jnp.dot(normed, wu, preferred_element_type=F32)
+    return (gate * jax.nn.sigmoid(gate) * up).astype(BF16), gate.astype(BF16), up.astype(BF16)
+
+
 def cols_of(total):
     return max(128, 655360 // total // 128 * 128)
 
 
-def mlp_kernel(
-    grp,
-    nm_ref,
-    dyall_ref,
-    wg_ref,
-    wu_ref,
-    top_ref,
-    h_ref,
-    dy_ref,
-    gain_ref,
-    down_ref,
-    dh_ref,
-    gm_ref,
-    gdown_ref,
-    ggate_ref,
-    gup_ref,
-    branch_ref,
-    out_ref,
-    downgot_ref,
-    gategot_ref,
-    p,
-    wd,
-    tile_n,
-    tsem,
-    act,
-    dgu,
-    cols,
-    csem,
-    dsem,
-    *rest,
-):
+def mlp_kernel(grp, n_early, *refs):
+    early, refs = refs[:n_early], refs[n_early:]
+    (
+        nm_ref,
+        dyall_ref,
+        wg_ref,
+        wu_ref,
+        down_all_ref,
+        h_ref,
+        dy_ref,
+        gain_ref,
+        down_ref,
+        dh_ref,
+        gm_ref,
+        gdown_ref,
+        ggate_ref,
+        gup_ref,
+        branch_ref,
+        out_ref,
+        downgot_ref,
+        gategot_ref,
+        p,
+        wd,
+        tile_n,
+        tsem,
+        act,
+        dgu,
+        cols,
+        csem,
+        dsem,
+        *rest,
+    ) = refs
     scat_refs, rest = rest[:N_SCATTER], rest[N_SCATTER:]
     send, recv, sem, zs, zr = rest
     rows, width = h_ref.shape
@@ -1262,18 +1397,19 @@
         part = pl.ds(pl.multiple_of(c * step, step), step)
         return pltpu.make_async_copy(src.at[:, part], cols.at[c % 2], csem.at[c % 2])
 
-    load(nm_ref, tile_n, 0, 0).start()
+    takes = []
+    if n_early:
+        takes = [
+            pltpu.make_async_copy(src, dst, tsem.at[0, i])
+            for i, (src, dst) in enumerate(zip(early, (act, dgu)))
+        ]
+        for c in takes:
+            c.start()
+    else:
+        load(nm_ref, tile_n, 0, 0).start()
     grp.greet()
     spread = Spread(grp, zs, zr)
-    spread.to(0, lambda: (top_ref, wd.at[pl.ds(0, units // 2)]))
-    spread_weight(
-        grp,
-        spread,
-        top_rows(halves_of(grp, down_ref, 0), 1),
-        wd.at[pl.ds(units // 2, units // 2)],
-        0,
-        0,
-    )
+    spread.to(0, lambda: (down_all_ref, wd))
 
     def forward(j):
         @pl.when(j + 1 < n)
@@ -1281,16 +1417,17 @@
             load(nm_ref, tile_n, 0, j + 1).start()
 
         load(nm_ref, tile_n, 0, j).wait()
-        normed = tile_n[j % 2]
-        gate = jnp.dot(normed, wg_ref[...], preferred_element_type=F32)
-        up = jnp.dot(normed, wu_ref[...], preferred_element_type=F32)
         here = at(j)
-        act[here] = (gate * jax.nn.sigmoid(gate) * up).astype(BF16)
-        dgu[here, :units] = gate.astype(BF16)
-        dgu[here, units:] = up.astype(BF16)
+        act[here], dgu[here, :units], dgu[here, units:] = gate_up(
+            tile_n[j % 2], wg_ref[...], wu_ref[...]
+        )
 
     load_cols(dyall_ref, 0).start()
-    paced(n, forward, [])
+    if n_early:
+        for c in takes:
+            c.wait()
+    else:
+        paced(n, forward, [])
     blocks = width // step
 
     def down_cols(c):
@@ -1402,14 +1539,14 @@
     spread.wait()
 
 
-def mlp(grp, normed, dy_all, wg, wu, wd_top, hidden, dy, gain, w_down, cid):
+def mlp(grp, early, normed, dy_all, wg, wu, wd, hidden, dy, gain, w_down, cid):
     rows, width = hidden.shape
     total = rows * grp.size
     n = len(grp.masks)
     units = wg.shape[1]
     gdown, ggate = sds((units, width), BF16), sds((width, units), BF16)
     return pl.pallas_call(
-        functools.partial(mlp_kernel, grp),
+        functools.partial(mlp_kernel, grp, len(early)),
         out_shape=[
             sds((rows, width), F32),
             sds((1, width), F32),
@@ -1421,7 +1558,7 @@
             got_shape(grp, gdown, 1),
             got_shape(grp, ggate, 0),
         ],
-        in_specs=[ANY, ANY, VMEM, VMEM, ANY, ANY, ANY, VMEM, ANY],
+        in_specs=[ANY] * len(early) + [ANY, ANY, VMEM, VMEM, ANY, ANY, ANY, VMEM, ANY],
         out_specs=[VMEM] * 5 + [ANY] * 4,
         scratch_shapes=[
             pltpu.VMEM((total, width), BF16),
@@ -1439,7 +1576,7 @@
         + spread_sems(grp, 4),
         compiler_params=params(cid),
         name="mlp",
-    )(normed, dy_all, wg, wu, wd_top, hidden, dy, gain, w_down)
+    )(*early, normed, dy_all, wg, wu, wd, hidden, dy, gain, w_down)
 
 
 def fifth_kernel(grp, p_ref, h_ref, gup_ref, out_ref, up_ref, *rest):
@@ -1711,7 +1848,7 @@
     normed_a, wqkv, wo, start, cosine, sine = first(
         grp, low, tokens, gain_a, w_query, w_key, w_value, w_out, segment_ids, 0
     )
-    query, key, value, attended, lse, hidden, normed_m, grad_all, wg, wu, wd_top = middle(
+    query, key, value, attended, lse, hidden, normed_m, grad_all, wg, wu, wd, *early = middle(
         grp,
         heads,
         normed_a,
@@ -1729,7 +1866,7 @@
         1,
     )
     grad_hidden, gain_m_part, grad_down, grad_wg, grad_wu, branch_all, out_part, got_down, got_gate = mlp(
-        grp, normed_m, grad_all, wg, wu, wd_top, hidden, out_grad, gain_m, w_down, 3
+        grp, early, normed_m, grad_all, wg, wu, wd, hidden, out_grad, gain_m, w_down, 3
     )
     if grp.size <= 16:
         output, tokens_grad, gains, grad_wout, grad_wqkv, got_up, got_out, got_qkv = last(

time: 511 us -> 483 us (0.945)
  Pallas kernels: 502 us -> 474 us
    pallas_call x2, Pallas kernels: 305 us -> 283 us  [the longest x1 156 us: middle(): pl.pallas_call(functools.partial(middle_kernel, grp, heads, fused), out_s...]
    pallas_call x1, Pallas kernels: 133 us -> 127 us  [last(): pl.pallas_call(functools.partial(last_kernel, grp, heads), out_shape=[sds...]
where the time goes in v5:
time: 483 us; the launch traced here: 479 us
  Pallas kernels  474 us (98%)
  local copies, waits for them, and re-layouts  4.89 us (1%)
    pallas_call x1, Pallas kernels, middle(): pl.pallas_call(functools.partial(middle_kernel, grp, heads, fused), out_s...  156 us
    pallas_call x1, Pallas kernels, mlp(): pl.pallas_call(functools.partial(mlp_kernel, grp, len(early)), out_shape=...  127 us
    pallas_call x1, Pallas kernels, last(): pl.pallas_call(functools.partial(last_kernel, grp, heads), out_shape=[sds...  127 us
    pallas_call x1, Pallas kernels, first(): pl.pallas_call(functools.partial(first_kernel, grp, (pre_qkv, pre_o), len...  57.2 us

profile of v5, /device:TPU:8, one launch (start us, length us, event | category | flops | bytes accessed | tf_op | source)
XLA Modules:
  0.0 479.4 jit_solution(8450609166911854107)
XLA Ops:
  0.6 1.3 broadcast_in_dim.6.gain_ref
  1.9 57.2 %first.1 = (bf16[2560,2048]{1,0:T(8,128)(2,1)}, bf16[2048,384]{1,0:T(8,128)(2,1)}, bf16[128,2048]{1,0:T(8,128)(2,1)}, s32[2,1,1280]{2,1,0:T(1,128)}, f32[2560,128]{1,0:T(8,128)}, /*index=5*/f32[2560,128]{1,0:T(8,128)}) custom-call(bf16[160,2048]{1,0:T(8,128)(2,1)} %x_ref.5, bf16[1,2048]{1,0:T(2,128)(2,1)} %broadcast_in_dim.6.gain_ref, ...), custom_call_target="tpu_custom_call" | custom-call | tf_op jit(solution)/shard_map/first/pallas_call | solution.py:689
  59.1 1.3 broadcast_in_dim.7.gain_ref.refs_9_
  60.4 155.8 %middle.1 = (bf16[2560,128]{1,0:T(8,128)(2,1)}, bf16[2560,128]{1,0:T(8,128)(2,1)}, bf16[2560,128]{1,0:T(8,128)(2,1)}, bf16[2560,128]{1,0:T(8,128)(2,1)}, f32[2,2...) custom-call(bf16[2560,2048]{1,0:T(8,128)(2,1)} %get-tuple-element.54, ...), custom_call_target="tpu_custom_call" | custom-call | tf_op jit(solution)/shard_map/middle/pallas_call | solution.py:961
  216.2 126.8 %mlp.1 = (f32[160,2048]{1,0:T(8,128)}, f32[1,2048]{1,0:T(1,128)}, bf16[512,2048]{1,0:T(8,128)(2,1)}, bf16[2048,512]{1,0:T(8,128)(2,1)}, bf16[2048,512]{1,0:T(8,1...) custom-call(bf16[2560,512]{1,0:T(8,128)(2,1)} %get-tuple-element.60., ...), custom_call_target="tpu_custom_call" | custom-call | tf_op jit(solution)/shard_map/mlp/pallas_call | solution.py:1548
  343.0 126.7 %last.1 = (bf16[160,2048]{1,0:T(8,128)(2,1)}, bf16[160,2048]{1,0:T(8,128)(2,1)}, f32[2,2048]{1,0:T(2,128)}, bf16[128,2048]{1,0:T(8,128)(2,1)}, bf16[2048,384]{1,...) custom-call(bf16[2560,2048]{1,0:T(8,128)(2,1)} %get-tuple-element.68.branc, ...), custom_call_target="tpu_custom_call" | custom-call | tf_op jit(solution)/shard_map/last/pallas_call | solution.py:1264
  469.8 0.0 copy-start.2
  469.8 0.0 copy-start.1
  469.8 0.0 copy-start
  469.8 7.3 %finish.1 = (f32[2,512,512]{2,1,0:T(8,128)}, f32[512,1024]{1,0:T(8,128)}, f32[512,1024]{1,0:T(8,128)}, f32[2,128,512]{2,1,0:T(8,128)}, f32[512,256]{1,0:T(8,128)...) custom-call(s32[1]{0:T(128)} %bitcast.2.z_ref, bf16[512,2048]{1,0:T(8,128)(2,1)} %get-tuple-element.81.refs_0_, ...), custom_call_target="tpu_custom_call" | custom-call | tf_op jit(solution)/shard_map/finish/pallas_call | solution.py:1793
  477.1 0.0 copy-done.2
  477.1 0.6 fusion
  477.7 0.0 copy-done.1
  477.7 0.8 copy.25
  478.5 0.0 copy-done
  478.5 0.8 copy.26
Async XLA Ops:
  469.8 7.3 %copy-start.2 = (f32[2,2048]{1,0:T(2,128)S(1)}, f32[2,2048]{1,0:T(2,128)}, u32[]{:S(2)}) copy-start(f32[2,2048]{1,0:T(2,128)} %get-tuple-element.80) | copy-start | bytes 49156
  469.8 7.9 %copy-start.1 = (bf16[160,2048]{1,0:T(8,128)(2,1)S(1)}, bf16[160,2048]{1,0:T(8,128)(2,1)}, u32[]{:S(2)}) copy-start(bf16[160,2048]{1,0:T(8,128)(2,1)} %get-tuple-element.110) | copy-start | bytes 1966084
  469.8 8.8 %copy-start = (bf16[160,2048]{1,0:T(8,128)(2,1)S(1)}, bf16[160,2048]{1,0:T(8,128)(2,1)}, u32[]{:S(2)}) copy-start(bf16[160,2048]{1,0:T(8,128)(2,1)} %get-tuple-element.111) | copy-start | bytes 1966084

commit v6 on v5

--- a/solution.py
+++ b/solution.py
@@ -629,16 +629,15 @@
 
     def norm(rows):
         x = x_ref[rows].astype(F32)
-        local[rows] = (x * norm_scale(x) * gain_ref[...].astype(F32)).astype(BF16)
+        local[rows] = (x * norm_scale(x) * gain_ref[0:1].astype(F32)).astype(BF16)
 
     tiles(x_ref.shape[0], norm)
     gather = Gather(grp, local, all_ref, send, recv, sem)
     steps = gather.begin()
-    weights(grp.far + (0,))
+    weights((1,) + grp.far + (0,))
     spread.wait_first(2)
     places(ids, start_ref, cos_ref, sin_ref)
     run(steps[:6])
-    weights((1,))
     run(steps[6:] or [lambda: None])
     gather.finish()
     spread.wait()
@@ -876,7 +875,7 @@
     def norm(part):
         h = x_ref[part].astype(F32) + summed[part].astype(F32)
         h_ref[part] = h
-        local[part] = (h * norm_scale(h) * gain_ref[...].astype(F32)).astype(BF16)
+        local[part] = (h * norm_scale(h) * gain_ref[1:2].astype(F32)).astype(BF16)
 
     tiles(x_ref.shape[0], norm)
     gather = Gather(grp, local, nm_ref, send, recv, sem)
@@ -997,6 +996,19 @@
     return back, jnp.sum(grad * value * scale, axis=0, keepdims=True)
 
 
+class Fetch:
+    def __init__(self, sems, *pairs):
+        self.copies = [
+            pltpu.make_async_copy(src, dst, sems.at[i]) for i, (src, dst) in enumerate(pairs)
+        ]
+        for c in self.copies:
+            c.start()
+
+    def wait(self):
+        for c in self.copies:
+            c.wait()
+
+
 def weave(parts, steps, each=1):
     for part in parts:
         part()
@@ -1018,14 +1030,14 @@
     v_ref,
     o_ref,
     lse_ref,
-    cos_ref,
-    sin_ref,
+    cos_in,
+    sin_in,
     start_ref,
-    wqkv_ref,
+    wqkv_in,
     wo_ref,
-    h_ref,
-    x_ref,
-    dh_ref,
+    h_in,
+    x_in,
+    dh_in,
     gain_ref,
     gm_ref,
     out_ref,
@@ -1049,6 +1061,13 @@
     dk,
     dv,
     gacc,
+    cos_ref,
+    sin_ref,
+    wqkv_ref,
+    h_ref,
+    x_ref,
+    dh_ref,
+    fsem,
     buf,
     gs,
     gr,
@@ -1058,7 +1077,7 @@
     out_scat, rest = rest[:N_SCATTER], rest[N_SCATTER:]
     zs, zr = rest
     rows_all, _, length = start_ref.shape
-    rows, width = h_ref.shape
+    rows, width = h_in.shape
     wide = heads * HEAD
     z, _ = grp.place()
     n = rows_all // 2
@@ -1075,6 +1094,15 @@
         return pltpu.make_async_copy(na_ref.at[:, part], cols.at[c % 2], csem.at[c % 2])
 
     load(0, 0).start()
+    fetch = Fetch(
+        fsem,
+        (cos_in, cos_ref),
+        (sin_in, sin_ref),
+        (wqkv_in, wqkv_ref),
+        (h_in, h_ref),
+        (x_in, x_ref),
+        (dh_in, dh_ref),
+    )
     load_cols(0).start()
     outer = Scatter(grp, part_ref, rows, *out_scat, own=own)
     for m in outer.masks(True) + outer.masks(False):
@@ -1082,7 +1110,7 @@
     grp.greet(everyone=True)
     outer.begin(outer.masks(True) + outer.masks(False))
     spread = Spread(grp, zs, zr)
-    spread_grad(grp, spread, gup_ref, upgot_ref, 0)
+    spread_grad(grp, spread, gup_ref, upgot_ref, 0, (1,) + grp.far)
     scat = Scatter(grp, p, rows, *na_scat)
     gacc[...] = jnp.zeros_like(gacc)
 
@@ -1143,6 +1171,8 @@
 
     def turn_back(i):
         base = order[i] * length
+        if i == 0:
+            fetch.wait()
 
         @pl.loop(0, blocks)
         def _(j):
@@ -1166,15 +1196,16 @@
     pair_core = scat.core_steps(True)
     for i in range(n, 2 * n):
         todo = parts(i)
-        merged = []
-        for a in range(len(todo)):
-            merged += [x[a] for x in (outer_steps, pair_core) if a < len(x)]
+        beside = [
+            functools.partial(run, pair_core[a : a + 1] + outer_steps[a : a + 1])
+            for a in range(len(todo))
+        ]
         outer_steps, pair_core = outer_steps[len(todo) :], pair_core[len(todo) :]
-        merged = weave(todo, merged, 2)
-        outer_steps = merged + outer_steps
+        weave(todo, beside)
     scat.begin(scat.masks(False))
     gout_ref[...] = gacc[...].astype(BF16)
-    spread_grad(grp, spread, gout_ref, outgot_ref, 1)
+    inner = inner_plane(grp)
+    spread_grad(grp, spread, gout_ref, outgot_ref, 1, (1,) + grp.far)
 
     def qkv_cols(c):
         @pl.when(c + 1 < width // step)
@@ -1185,9 +1216,13 @@
         part = pl.ds(pl.multiple_of(c * step, step), step)
         gqkv_ref[part] = dot_tn(cols[c % 2], dqkv[...]).astype(BF16)
 
-    paced(width // step, qkv_cols, outer_steps + pair_core + scat.core_steps(False))
-    spread_grad(grp, spread, gqkv_ref, qkvgot_ref, 0)
-    run(scat.link_steps(True) + scat.link_steps(False))
+    paced(width // step, qkv_cols, pair_core + scat.core_steps(False))
+    spread_grad(grp, spread, gqkv_ref, qkvgot_ref, 0, (1,))
+    far = spread_grad(grp, spread, gqkv_ref, qkvgot_ref, 0, grp.far, start=False)
+    launch(far, inner)
+    run(scat.link_steps(True))
+    launch(far, jnp.logical_not(inner))
+    run(scat.link_steps(False), outer_steps)
     outer.finish()
     whole = outer.block(0)
 
@@ -1202,7 +1237,7 @@
 
     def back(part):
         dn, gain_part = norm_back_tile(
-            x_ref[part].astype(F32), gain_ref[...].astype(F32), summed[part].astype(F32)
+            x_ref[part].astype(F32), gain_ref[0:1].astype(F32), summed[part].astype(F32)
         )
         buf[0, 0:1] += gain_part
         tok_ref[part] = (dh_ref[part] + dn).astype(BF16)
@@ -1273,7 +1308,7 @@
             got_shape(grp, gout, 1),
             got_shape(grp, gqkv, 0),
         ],
-        in_specs=[ANY] * 4 + [VMEM] * 15,
+        in_specs=[ANY] * 4 + [VMEM] * 5 + [ANY] * 2 + [VMEM, ANY, VMEM] + [ANY] * 3 + [VMEM] * 2,
         out_specs=[VMEM] * 5 + [ANY] * 3,
         scratch_shapes=[
             pltpu.VMEM((total, width), BF16),
@@ -1289,6 +1324,13 @@
             pltpu.VMEM((length, wide), F32),
             pltpu.VMEM((length, wide), F32),
             pltpu.VMEM((wide, width), F32),
+            pltpu.VMEM((total, wide), F32),
+            pltpu.VMEM((total, wide), F32),
+            pltpu.VMEM((width, 3 * wide), BF16),
+            pltpu.VMEM((rows, width), F32),
+            pltpu.VMEM((rows, width), BF16),
+            pltpu.VMEM((rows, width), F32),
+            pltpu.SemaphoreType.DMA((6,)),
         ]
         + gain_scratch(grp, width)
         + scatter_scratch(grp, rows, width)
@@ -1352,8 +1394,8 @@
     (
         nm_ref,
         dyall_ref,
-        wg_ref,
-        wu_ref,
+        wg_in,
+        wu_in,
         down_all_ref,
         h_ref,
         dy_ref,
@@ -1361,9 +1403,9 @@
         down_ref,
         dh_ref,
         gm_ref,
-        gdown_ref,
-        ggate_ref,
-        gup_ref,
+        gdown_out,
+        ggate_out,
+        gup_out,
         branch_ref,
         out_ref,
         downgot_ref,
@@ -1377,6 +1419,12 @@
         cols,
         csem,
         dsem,
+        wg_ref,
+        wu_ref,
+        gdown_ref,
+        ggate_ref,
+        gup_ref,
+        fsem,
         *rest,
     ) = refs
     scat_refs, rest = rest[:N_SCATTER], rest[N_SCATTER:]
@@ -1397,6 +1445,7 @@
         part = pl.ds(pl.multiple_of(c * step, step), step)
         return pltpu.make_async_copy(src.at[:, part], cols.at[c % 2], csem.at[c % 2])
 
+    fetch = Fetch(fsem, (wg_in, wg_ref), (wu_in, wu_ref))
     takes = []
     if n_early:
         takes = [
@@ -1427,6 +1476,7 @@
         for c in takes:
             c.wait()
     else:
+        fetch.wait()
         paced(n, forward, [])
     blocks = width // step
 
@@ -1441,6 +1491,10 @@
 
     load(dyall_ref, tile_n, 1, 0).start()
     paced(blocks, down_cols, [])
+    outs = [pltpu.make_async_copy(gdown_ref, gdown_out, fsem.at[2])]
+    outs[0].start()
+    if n_early:
+        fetch.wait()
     spread.wait()
     spread_grad(grp, spread, gdown_ref, downgot_ref, 1)
 
@@ -1494,6 +1548,9 @@
 
     load_cols(nm_ref, 0).start()
     paced(blocks, gate_up_cols, rest_steps)
+    for i, pair in enumerate(((ggate_ref, ggate_out), (gup_ref, gup_out))):
+        outs.append(pltpu.make_async_copy(*pair, fsem.at[3 + i]))
+        outs[-1].start()
     dy = scat_refs[0].at[n - 1]
     fetches = [
         pltpu.make_async_copy(dy_ref, dy, dsem.at[0]),
@@ -1508,7 +1565,7 @@
     gm_ref[...] = jnp.zeros_like(gm_ref)
 
     def back(part):
-        dn, gain_part = norm_back_tile(dh_ref[part], gain_ref[...].astype(F32), summed[part].astype(F32))
+        dn, gain_part = norm_back_tile(dh_ref[part], gain_ref[1:2].astype(F32), summed[part].astype(F32))
         gm_ref[...] += gain_part
         dh = dy[part].astype(F32) + dn
         dh_ref[part] = dh
@@ -1533,6 +1590,8 @@
 
     near = functools.partial(spread_grad, grp, spread, ggate_ref, gategot_ref, 0, (1,))
     paced(n, branch, steps[:6] + [near] + steps[6:], 1)
+    for c in outs:
+        c.wait()
     save(n - 2).wait()
     save(n - 1).wait()
     gather.finish()
@@ -1558,8 +1617,8 @@
             got_shape(grp, gdown, 1),
             got_shape(grp, ggate, 0),
         ],
-        in_specs=[ANY] * len(early) + [ANY, ANY, VMEM, VMEM, ANY, ANY, ANY, VMEM, ANY],
-        out_specs=[VMEM] * 5 + [ANY] * 4,
+        in_specs=[ANY] * (len(early) + 7) + [VMEM, ANY],
+        out_specs=[VMEM] * 2 + [ANY] * 7,
         scratch_shapes=[
             pltpu.VMEM((total, width), BF16),
             pltpu.VMEM((units, width), BF16),
@@ -1570,6 +1629,12 @@
             pltpu.VMEM((2, total, cols_of(total)), BF16),
             pltpu.SemaphoreType.DMA((2,)),
             pltpu.SemaphoreType.DMA((2,)),
+            pltpu.VMEM((width, units), BF16),
+            pltpu.VMEM((width, units), BF16),
+            pltpu.VMEM((units, width), BF16),
+            pltpu.VMEM((width, units), BF16),
+            pltpu.VMEM((width, units), BF16),
+            pltpu.SemaphoreType.DMA((5,)),
         ]
         + scatter_scratch(grp, rows, width)
         + gather_scratch(grp)
@@ -1630,7 +1695,7 @@
 
     def back(rows):
         dn, gain_part = norm_back_tile(
-            x_ref[rows].astype(F32), gain_ref[...].astype(F32), acc[rows].astype(F32)
+            x_ref[rows].astype(F32), gain_ref[0:1].astype(F32), acc[rows].astype(F32)
         )
         buf[0, 0:1] += gain_part
         tok_ref[rows] = (dh_ref[rows] + dn).astype(BF16)
@@ -1776,7 +1841,7 @@
 
 
 def finish(z_size, z, grads, gots, axes):
-    steps = 4
+    steps = 2
     owns, blocks, outs, shapes = [], [], [], []
     for grad, got, (axis, count) in zip(grads, gots, axes):
         rows, cols = got.shape[1] // steps, got.shape[2]
@@ -1843,10 +1908,9 @@
     wide = w_query.shape[1] // 2
     heads = wide // HEAD
 
-    gain_a = gain_attn[None, :]
-    gain_m = gain_mlp[None, :]
+    gains_in = jnp.stack([gain_attn, gain_mlp])
     normed_a, wqkv, wo, start, cosine, sine = first(
-        grp, low, tokens, gain_a, w_query, w_key, w_value, w_out, segment_ids, 0
+        grp, low, tokens, gains_in, w_query, w_key, w_value, w_out, segment_ids, 0
     )
     query, key, value, attended, lse, hidden, normed_m, grad_all, wg, wu, wd, *early = middle(
         grp,
@@ -1859,19 +1923,19 @@
         start,
         out_grad,
         tokens,
-        gain_m,
+        gains_in,
         w_gate,
         w_up,
         w_down,
         1,
     )
     grad_hidden, gain_m_part, grad_down, grad_wg, grad_wu, branch_all, out_part, got_down, got_gate = mlp(
-        grp, early, normed_m, grad_all, wg, wu, wd, hidden, out_grad, gain_m, w_down, 3
+        grp, early, normed_m, grad_all, wg, wu, wd, hidden, out_grad, gains_in, w_down, 3
     )
     if grp.size <= 16:
         output, tokens_grad, gains, grad_wout, grad_wqkv, got_up, got_out, got_qkv = last(
             grp, heads, branch_all, normed_a, out_part, grad_wu, query, key, value, attended, lse,
-            cosine, sine, start, wqkv, wo, hidden, tokens, grad_hidden, gain_a, gain_m_part, 4,
+            cosine, sine, start, wqkv, wo, hidden, tokens, grad_hidden, gains_in, gain_m_part, 4,
         )
     else:
         output, got_up = fifth(grp, out_part, hidden, grad_wu, 4)
@@ -1881,7 +1945,7 @@
         grad_wqkv = dot_tn(normed_a, grad_qkv).astype(BF16)
         grad_na = dot_nt(grad_qkv, wqkv).astype(BF16)
         tokens_grad, gains, got_out, got_qkv = sixth(
-            grp, grad_na, tokens, grad_hidden, gain_a, gain_m_part, grad_wout, grad_wqkv, 5
+            grp, grad_na, tokens, grad_hidden, gains_in, gain_m_part, grad_wout, grad_wqkv, 5
         )
     grads = (grad_down, grad_wg, grad_wu, grad_wout, grad_wqkv)
     gots = (got_down, got_gate, got_up, got_out, got_qkv)

time: 483 us -> 481 us (level)
  no operation moved by 1% of the time
where the time goes in v6:
time: 481 us; the launch traced here: 477 us
  Pallas kernels  472 us (98%)
    pallas_call x1, Pallas kernels, middle(): pl.pallas_call(functools.partial(middle_kernel, grp, heads, fused), out_s...  158 us
    pallas_call x1, Pallas kernels, last(): pl.pallas_call(functools.partial(last_kernel, grp, heads), out_shape=[sds...  127 us
    pallas_call x1, Pallas kernels, mlp(): pl.pallas_call(functools.partial(mlp_kernel, grp, len(early)), out_shape=...  125 us
    pallas_call x1, Pallas kernels, first(): pl.pallas_call(functools.partial(first_kernel, grp, (pre_qkv, pre_o), len...  55.6 us

profile of v6, /device:TPU:8, one launch (start us, length us, event | category | flops | bytes accessed | tf_op | source)
XLA Modules:
  0.0 477.2 jit_solution(7169826995562407891)
XLA Ops:
  0.6 0.7 stack.10
  1.3 0.7 stack.9
  2.0 0.6 pad_maximum_fusion.gain_ref.refs_9_
  2.7 55.6 %first.1 = (bf16[2560,2048]{1,0:T(8,128)(2,1)}, bf16[2048,384]{1,0:T(8,128)(2,1)}, bf16[128,2048]{1,0:T(8,128)(2,1)}, s32[2,1,1280]{2,1,0:T(1,128)}, f32[2560,128]{1,0:T(8,128)}, /*index=5*/f32[2560,128]{1,0:T(8,128)}) custom-call(bf16[160,2048]{1,0:T(8,128)(2,1)} %x_in.1, bf16[2,2048]{1,0:T(2,128)(2,1)} %pad_maximum_fusion.gain_ref.refs_9_, ...), custom_call_target="tpu_custom_call" | custom-call | tf_op jit(solution)/shard_map/first/pallas_call | solution.py:688
  58.2 158.4 %middle.1 = (bf16[2560,128]{1,0:T(8,128)(2,1)}, bf16[2560,128]{1,0:T(8,128)(2,1)}, bf16[2560,128]{1,0:T(8,128)(2,1)}, bf16[2560,128]{1,0:T(8,128)(2,1)}, f32[2,2...) custom-call(bf16[2560,2048]{1,0:T(8,128)(2,1)} %get-tuple-element.54, ...), custom_call_target="tpu_custom_call" | custom-call | tf_op jit(solution)/shard_map/middle/pallas_call | solution.py:960
  216.6 125.4 %mlp.1 = (f32[160,2048]{1,0:T(8,128)}, f32[1,2048]{1,0:T(1,128)}, bf16[512,2048]{1,0:T(8,128)(2,1)}, bf16[2048,512]{1,0:T(8,128)(2,1)}, bf16[2048,512]{1,0:T(8,1...) custom-call(bf16[2560,512]{1,0:T(8,128)(2,1)} %get-tuple-element.60., ...), custom_call_target="tpu_custom_call" | custom-call | tf_op jit(solution)/shard_map/mlp/pallas_call | solution.py:1607
  342.0 126.9 %last.1 = (bf16[160,2048]{1,0:T(8,128)(2,1)}, bf16[160,2048]{1,0:T(8,128)(2,1)}, f32[2,2048]{1,0:T(2,128)}, bf16[128,2048]{1,0:T(8,128)(2,1)}, bf16[2048,384]{1,...) custom-call(bf16[2560,2048]{1,0:T(8,128)(2,1)} %get-tuple-element.68.branc, ...), custom_call_target="tpu_custom_call" | custom-call | tf_op jit(solution)/shard_map/last/pallas_call | solution.py:1299
  468.8 0.0 copy-start.2
  468.8 0.0 copy-start.1
  468.9 0.0 copy-start
  468.9 6.0 %finish.1 = (f32[2,512,512]{2,1,0:T(8,128)}, f32[512,1024]{1,0:T(8,128)}, f32[512,1024]{1,0:T(8,128)}, f32[2,128,512]{2,1,0:T(8,128)}, f32[512,256]{1,0:T(8,128)...) custom-call(s32[1]{0:T(128)} %bitcast.2.z_ref, bf16[512,2048]{1,0:T(8,128)(2,1)} %get-tuple-element.81.refs_0_, ...), custom_call_target="tpu_custom_call" | custom-call | tf_op jit(solution)/shard_map/finish/pallas_call | solution.py:1858
  474.9 0.0 copy-done.2
  474.9 0.6 fusion
  475.5 0.0 copy-done.1
  475.5 0.8 copy.25
  476.3 0.0 copy-done
  476.3 0.8 copy.26
Async XLA Ops:
  468.8 6.0 %copy-start.2 = (f32[2,2048]{1,0:T(2,128)S(1)}, f32[2,2048]{1,0:T(2,128)}, u32[]{:S(2)}) copy-start(f32[2,2048]{1,0:T(2,128)} %get-tuple-element.80) | copy-start | bytes 49156
  468.8 6.6 %copy-start.1 = (bf16[160,2048]{1,0:T(8,128)(2,1)S(1)}, bf16[160,2048]{1,0:T(8,128)(2,1)}, u32[]{:S(2)}) copy-start(bf16[160,2048]{1,0:T(8,128)(2,1)} %get-tuple-element.110) | copy-start | bytes 1966084
  468.9 7.5 %copy-start = (bf16[160,2048]{1,0:T(8,128)(2,1)S(1)}, bf16[160,2048]{1,0:T(8,128)(2,1)}, u32[]{:S(2)}) copy-start(bf16[160,2048]{1,0:T(8,128)(2,1)} %get-tuple-element.111) | copy-start | bytes 1966084

commit v7 on v6

--- a/solution.py
+++ b/solution.py
@@ -227,7 +227,9 @@
 
 
 def add_rows(dst, src, rows):
-    @pl.loop(0, rows // TILE)
+    count = rows // TILE
+
+    @pl.loop(0, count, unroll=1 + (count + 1) % 2)
     def _(i):
         part = pl.ds(pl.multiple_of(i * TILE, TILE), TILE)
         dst[part] = (dst[part].astype(F32) + src[part].astype(F32)).astype(dst.dtype)
@@ -560,7 +562,9 @@
 
 
 def tiles(rows, body):
-    @pl.loop(0, rows // TILE)
+    count = rows // TILE
+
+    @pl.loop(0, count, unroll=1 + (count + 1) % 2)
     def _(i):
         body(pl.ds(pl.multiple_of(i * TILE, TILE), TILE))
 
@@ -1487,7 +1491,7 @@
 
         load_cols(dyall_ref, c).wait()
         part = pl.ds(pl.multiple_of(c * step, step), step)
-        gdown_ref[:, part] = dot_tn(cols[c % 2], act[...]).T.astype(BF16)
+        gdown_ref[:, part] = dot_tn(act[...], cols[c % 2]).astype(BF16)
 
     load(dyall_ref, tile_n, 1, 0).start()
     paced(blocks, down_cols, [])

time: 481 us -> 480 us (level)
  no operation moved by 1% of the time
where the time goes in v7:
time: 480 us; the launch traced here: 476 us
  Pallas kernels  471 us (98%)
    pallas_call x1, Pallas kernels, middle(): pl.pallas_call(functools.partial(middle_kernel, grp, heads, fused), out_s...  158 us
    pallas_call x1, Pallas kernels, last(): pl.pallas_call(functools.partial(last_kernel, grp, heads), out_shape=[sds...  127 us
    pallas_call x1, Pallas kernels, mlp(): pl.pallas_call(functools.partial(mlp_kernel, grp, len(early)), out_shape=...  126 us
    pallas_call x1, Pallas kernels, first(): pl.pallas_call(functools.partial(first_kernel, grp, (pre_qkv, pre_o), len...  55.1 us

profile of v7, /device:TPU:8, one launch (start us, length us, event | category | flops | bytes accessed | tf_op | source)
XLA Modules:
  0.0 476.4 jit_solution(16165542551601011809)
XLA Ops:
  0.6 0.7 stack.10
  1.3 0.7 stack.9
  2.0 0.6 pad_maximum_fusion.gain_ref.refs_9_
  2.7 55.1 %first.1 = (bf16[2560,2048]{1,0:T(8,128)(2,1)}, bf16[2048,384]{1,0:T(8,128)(2,1)}, bf16[128,2048]{1,0:T(8,128)(2,1)}, s32[2,1,1280]{2,1,0:T(1,128)}, f32[2560,128]{1,0:T(8,128)}, /*index=5*/f32[2560,128]{1,0:T(8,128)}) custom-call(bf16[160,2048]{1,0:T(8,128)(2,1)} %x_in.1, bf16[2,2048]{1,0:T(2,128)(2,1)} %pad_maximum_fusion.gain_ref.refs_9_, ...), custom_call_target="tpu_custom_call" | custom-call | tf_op jit(solution)/shard_map/first/pallas_call | solution.py:692
  57.7 157.9 %middle.1 = (bf16[2560,128]{1,0:T(8,128)(2,1)}, bf16[2560,128]{1,0:T(8,128)(2,1)}, bf16[2560,128]{1,0:T(8,128)(2,1)}, bf16[2560,128]{1,0:T(8,128)(2,1)}, f32[2,2...) custom-call(bf16[2560,2048]{1,0:T(8,128)(2,1)} %get-tuple-element.54, ...), custom_call_target="tpu_custom_call" | custom-call | tf_op jit(solution)/shard_map/middle/pallas_call | solution.py:964
  215.6 125.6 %mlp.1 = (f32[160,2048]{1,0:T(8,128)}, f32[1,2048]{1,0:T(1,128)}, bf16[512,2048]{1,0:T(8,128)(2,1)}, bf16[2048,512]{1,0:T(8,128)(2,1)}, bf16[2048,512]{1,0:T(8,1...) custom-call(bf16[2560,512]{1,0:T(8,128)(2,1)} %get-tuple-element.60., ...), custom_call_target="tpu_custom_call" | custom-call | tf_op jit(solution)/shard_map/mlp/pallas_call | solution.py:1611
  341.2 126.8 %last.1 = (bf16[160,2048]{1,0:T(8,128)(2,1)}, bf16[160,2048]{1,0:T(8,128)(2,1)}, f32[2,2048]{1,0:T(2,128)}, bf16[128,2048]{1,0:T(8,128)(2,1)}, bf16[2048,384]{1,...) custom-call(bf16[2560,2048]{1,0:T(8,128)(2,1)} %get-tuple-element.68.branc, ...), custom_call_target="tpu_custom_call" | custom-call | tf_op jit(solution)/shard_map/last/pallas_call | solution.py:1303
  468.0 0.0 copy-start.2
  468.0 0.0 copy-start.1
  468.1 0.0 copy-start
  468.1 6.0 %finish.1 = (f32[2,512,512]{2,1,0:T(8,128)}, f32[512,1024]{1,0:T(8,128)}, f32[512,1024]{1,0:T(8,128)}, f32[2,128,512]{2,1,0:T(8,128)}, f32[512,256]{1,0:T(8,128)...) custom-call(s32[1]{0:T(128)} %bitcast.2.z_ref, bf16[512,2048]{1,0:T(8,128)(2,1)} %get-tuple-element.81.refs_0_, ...), custom_call_target="tpu_custom_call" | custom-call | tf_op jit(solution)/shard_map/finish/pallas_call | solution.py:1862
  474.1 0.0 copy-done.2
  474.1 0.6 fusion
  474.7 0.0 copy-done.1
  474.7 0.8 copy.25
  475.5 0.0 copy-done
  475.5 0.8 copy.26
Async XLA Ops:
  468.0 6.0 %copy-start.2 = (f32[2,2048]{1,0:T(2,128)S(1)}, f32[2,2048]{1,0:T(2,128)}, u32[]{:S(2)}) copy-start(f32[2,2048]{1,0:T(2,128)} %get-tuple-element.80) | copy-start | bytes 49156
  468.0 6.6 %copy-start.1 = (bf16[160,2048]{1,0:T(8,128)(2,1)S(1)}, bf16[160,2048]{1,0:T(8,128)(2,1)}, u32[]{:S(2)}) copy-start(bf16[160,2048]{1,0:T(8,128)(2,1)} %get-tuple-element.110) | copy-start | bytes 1966084
  468.1 7.5 %copy-start = (bf16[160,2048]{1,0:T(8,128)(2,1)S(1)}, bf16[160,2048]{1,0:T(8,128)(2,1)}, u32[]{:S(2)}) copy-start(bf16[160,2048]{1,0:T(8,128)(2,1)} %get-tuple-element.111) | copy-start | bytes 1966084
